TPU v7x, 32 devices: a whole 2x2x4 slice. The times are simulated.
32 devices in a mesh: expert: 4 (over y, x), seq: 2 (over core), mp: 4 (over z).
Axes of the slice: x: 2, y: 2, z: 4, core: 2. Of those that a mesh axis runs over, the one named last changes fastest.
Arguments:
- queries: bfloat16 [4, 1536, 2560], P('expert', 'seq', 'mp'), may hold values from -4000 to 4000
- key_input: bfloat16 [4, 1536, 2560], P('expert', 'seq', 'mp'), may hold values from -4000 to 4000
- value_input: bfloat16 [4, 1536, 2560], P('expert', 'seq', 'mp'), may hold values from -6 to 6
- timestep: int32 [4], P('expert'), may hold values from 0 to 999
- neighbours: int32 [4, 12, 5], P('expert', 'seq'), may hold values from 0 to 11, as said below
- q_gain: float32 [2, 2560], P(None, 'mp'), may hold values from 0.1 to 1.9
- k_gain: float32 [2, 2560], P(None, 'mp'), may hold values from 0.1 to 1.9
Outputs:
- mixed: bfloat16 [4, 1536, 2560], P('expert', 'seq', 'mp')
Inputs may be any that keep to these rules, and one draw needn't show every extreme that they name: For a query tile i, let d = i // 6. The 5 entries of neighbours[s, i] are distinct tile numbers from d * 6 - 1 to d * 6 + 6, and the first entry is i itself.
All inputs are finite; a program needn't handle non-finite values.
Results may differ from a plain program's by a relative error of at most 0.0099.
Values may be sent and summed in bfloat16 or wider, within the bound.
No kernel may reach another device: no remote copies, remote signals or barrier semaphores. Data moves between devices by JAX's collectives and lax.ppermute only.
A program may use at most 64 MiB of HBM per device.

v0:
```python
import jax
import jax.numpy as jnp
from jax import lax
from jax.sharding import PartitionSpec as P

DH = 128
TILE = 128


epsilon = 1e-06
switch_step = 875


def padded(x, sides, width):
    for axis, dim in sides:
        devices, length = (lax.axis_size(axis), x.shape[dim])
        up = [(i, (i + 1) % devices) for i in range(devices - 1)]
        down = [(j, i) for i, j in up]
        last = lax.slice_in_dim(x, length - width, length, axis=dim)
        initial = lax.slice_in_dim(x, 0, width, axis=dim)
        before = lax.ppermute(last, axis, up)
        after = lax.ppermute(initial, axis, down)
        x = jnp.concatenate([before, x, after], axis=dim)
    return x


def scaled_rows(rows, mean_sq, gain):
    return (
        rows.astype(jnp.float32) * lax.rsqrt(mean_sq + epsilon)[:, None] * gain[None, :]
    ).astype(jnp.bfloat16)


def square_sums(rows):
    values = rows.astype(jnp.float32)
    return jnp.sum(values * values, axis=-1)


def shards(queries, key_input, value_input, timestep, neighbours, q_gain, k_gain):
    rows = queries.shape[1]
    width = queries.shape[2]
    tiles_dev = rows // TILE
    heads_dev = width // DH
    full_width = width * lax.axis_size("mp")
    expert_id = jnp.where(timestep[0] >= switch_step, 0, 1)
    gain_q = q_gain[expert_id]
    gain_k = k_gain[expert_id]
    q_rows = queries[0]
    k_rows = key_input[0]
    v_rows = value_input[0]
    q_part = square_sums(q_rows)
    k_part = square_sums(k_rows)
    q_total, k_total = lax.psum((q_part, k_part), "mp")
    q_normed = scaled_rows(q_rows, q_total / full_width, gain_q)
    k_normed = scaled_rows(k_rows, k_total / full_width, gain_k)
    widened = padded(jnp.stack([k_normed, v_rows]), (("seq", 1),), TILE)
    keys_wide = widened[0]
    values_wide = widened[1]
    first_tile = lax.axis_index("seq") * tiles_dev - 1
    local_ids = neighbours[0] - first_tile
    key_tiles = keys_wide.reshape(tiles_dev + 2, TILE, heads_dev, DH)
    value_tiles = values_wide.reshape(tiles_dev + 2, TILE, heads_dev, DH)
    picked_keys = jnp.take(key_tiles, local_ids, axis=0).reshape(tiles_dev, -1, heads_dev, DH)
    picked_values = jnp.take(value_tiles, local_ids, axis=0).reshape(tiles_dev, -1, heads_dev, DH)
    query_tiles = q_normed.reshape(tiles_dev, TILE, heads_dev, DH)
    scores = jnp.einsum(
        "tqhd,tkhd->thqk", query_tiles, picked_keys, preferred_element_type=jnp.float32
    ) * DH ** (-0.5)
    top = jnp.max(scores, axis=-1, keepdims=True)
    expo = jnp.exp(scores - top)
    weights = (expo / jnp.sum(expo, axis=-1, keepdims=True)).astype(jnp.bfloat16)
    mixed = jnp.einsum(
        "thqk,tkhd->tqhd", weights, picked_values, preferred_element_type=jnp.float32
    )
    return mixed.astype(jnp.bfloat16).reshape(1, rows, width)


def solution(mesh):
    return jax.shard_map(
        shards,
        mesh=mesh,
        in_specs=(
            P("expert", "seq", "mp"),
            P("expert", "seq", "mp"),
            P("expert", "seq", "mp"),
            P("expert"),
            P("expert", "seq", None),
            P(None, "mp"),
            P(None, "mp"),
        ),
        out_specs=P("expert", "seq", "mp"),
        check_vma=False,
    )
```

profile of v0, /device:TPU:0, one launch (start us, length us, event | category | flops | bytes accessed | tf_op | source)
XLA Modules:
  0.0 89.6 jit_solution(18276754440406230383)
XLA Ops:
  0.8 2.0 %fusion.6 = (f32[768]{0:T(1024)S(1)}, f32[768]{0:T(1024)S(1)}) fusion(bf16[1,768,640]{2,1,0:T(8,128)(2,1)} %param.10, bf16[1,768,640]{2,1,0:T(8,128)(2,1)} %param.9), kind=kLoop, calls=%fused_computation.15 | loop fusion | flops 2947584 | bytes 1972224 | tf_op jit(solution)/shard_map/reduce_sum | solution.py:35
  2.7 13.7 %all-reduce = (f32[768]{0:T(1024)S(1)}, f32[768]{0:T(1024)S(1)}) all-reduce(f32[768]{0:T(1024)S(1)} %get-tuple-element.18, f32[768]{0:T(1024)S(1)} %get-tuple-element.19), channel_id=1, replica_groups=mesh['expert'=4,'seq'=2,'mp'=4] {'mp'}, use_global_device_ids=true, to_apply=%region_1.2 | all-reduce | flops 1536 | bytes 12288 | tf_op jit(solution)/shard_map/psum | solution.py:52
  17.2 1.5 %fusion.8 = bf16[1,768,640]{2,1,0:T(8,128)(2,1)S(1)} fusion(bf16[1,768,640]{2,1,0:T(8,128)(2,1)} %param.10, f32[640]{0:T(1024)S(1)} %get-tuple-element.17, f32[768]{0:T(1024)S(1)} %add_rsqrt_fusion), kind=kLoop, calls=%fused_computation.17 | loop fusion | flops 1966080 | bytes 1971712 | tf_op jit(solution)/shard_map/convert_element_type | solution.py:30
  19.6 1.9 %pad_maximum_fusion.2 = (bf16[2,128,640]{2,1,0:T(8,128)(2,1)}, bf16[2,128,640]{2,1,0:T(8,128)(2,1)}) fusion(bf16[1,768,640]{2,1,0:T(8,128)(2,1)} %param.11, bf16[1,768,640]{2,1,0:T(8,128)(2,1)S(1)} %fusion.8), kind=kLoop, calls=%fused_computation.24 | loop fusion | flops 1310720 | bytes 2621440 | tf_op jit(solution)/shard_map/slice | solution.py:19
  21.5 1.3 %collective-permute-start.1 = (bf16[2,128,640]{2,1,0:T(8,128)(2,1)}, bf16[2,128,640]{2,1,0:T(8,128)(2,1)S(1)}, u32[]{:S(2)}, u32[]{:S(2)}) collective-permute-start(bf16[2,128,640]{2,1,0:T(8,128)(2,1)} %get-tuple-element.13), channel_id=1, source_target_pairs={{4,0},{5,1},{6,2},{7,3},{12,8},{13,9},{14,10},{15,11},{20,16},{21,... | collective-permute-start | bytes 983048 | tf_op jit(solution)/shard_map/ppermute | solution.py:22
  22.8 3.1 %collective-permute-start = (bf16[2,128,640]{2,1,0:T(8,128)(2,1)}, bf16[2,128,640]{2,1,0:T(8,128)(2,1)S(1)}, u32[]{:S(2)}, u32[]{:S(2)}) collective-permute-start(bf16[2,128,640]{2,1,0:T(8,128)(2,1)} %get-tuple-element.12), channel_id=1, source_target_pairs={{0,4},{1,5},{2,6},{3,7},{8,12},{9,13},{10,14},{11,15},{16,20},{17,... | collective-permute-start | bytes 983048 | tf_op jit(solution)/shard_map/ppermute | solution.py:21
  26.1 1.6 %copy.37 = f32[1,768,640]{1,2,0:T(8,128)} copy(bf16[1,768,640]{2,1,0:T(8,128)(2,1)S(1)} %copy-done.3) | data formatting | bytes 2949120 | tf_op jit(solution)/shard_map/convert_element_type | solution.py:29
  27.7 2.3 %reshape.57 = f32[6,128,5,128]{1,0,3,2:T(8,128)S(1)} reshape(f32[1,768,640]{1,2,0:T(8,128)} %copy.37) | data formatting | bytes 3932160 | tf_op jit(solution)/shard_map/convert_element_type | solution.py:29
  30.0 1.7 %multiply_convert_fusion = bf16[6,128,5,128]{1,0,3,2:T(8,128)(2,1)} fusion(f32[6,128,5,128]{1,0,3,2:T(8,128)S(1)} %reshape.57, f32[5,128]{1,0:T(8,128)S(1)} %bitcast.21, f32[6,128]{1,0:T(8,128)S(1)} %rsqrt_bitcast_fusion), kind=kLoop, calls=%fused_computation.12 | loop fusion | flops 1474560 | bytes 2954752 | tf_op jit(solution)/shard_map/convert_element_type | solution.py:30
  31.7 1.7 %pad_maximum_fusion = bf16[2,1024,640]{2,1,0:T(8,128)(2,1)S(1)} fusion(bf16[2,128,640]{2,1,0:T(8,128)(2,1)S(1)} %collective-permute-done.1, bf16[1,768,640]{2,1,0:T(8,128)(2,1)} %param.11, bf16[1,768,640]{2,1,0:T(8,128)(2,1)} %copy-done.1, bf16[2,128,640]{2,1,0:T(8,128)(2,1)S(1)} %collective-permute-done), kind=kLoop, calls=%fused_computation.11 | loop fusion | flops 10485760 | bytes 5242880 | tf_op jit(solution)/shard_map/concatenate | solution.py:23
  33.5 1.3 %fusion.21 = (bf16[1,1024,640]{2,1,0:T(8,128)(2,1)S(1)}, bf16[1,1024,640]{2,1,0:T(8,128)(2,1)}) fusion(bf16[2,1024,640]{2,1,0:T(8,128)(2,1)S(1)} %pad_maximum_fusion), kind=kLoop, calls=%fused_computation.35 | loop fusion | bytes 5242880 | tf_op jit(solution)/shard_map/slice | solution.py:56
  34.7 1.5 %reshape.87 = bf16[8,128,5,128]{3,2,1,0:T(8,128)(2,1)S(1)} reshape(bf16[1,1024,640]{2,1,0:T(8,128)(2,1)S(1)} %get-tuple-element.10) | data formatting | bytes 2621440 | tf_op jit(solution)/shard_map/reshape;squeeze | solution.py:60
  36.6 4.1 %reshape.86 = bf16[8,128,5,128]{3,2,1,0:T(8,128)(2,1)} reshape(bf16[1,1024,640]{2,1,0:T(8,128)(2,1)} %get-tuple-element.11) | data formatting | bytes 2621440 | tf_op jit(solution)/shard_map/reshape;squeeze | solution.py:61
  40.7 1.9 %copy.35 = bf16[8,128,5,128]{3,1,2,0:T(8,128)(2,1)S(1)} copy(bf16[8,128,5,128]{3,2,1,0:T(8,128)(2,1)} %reshape.86) | data formatting | bytes 2621440 | tf_op jit(solution)/shard_map/reshape;squeeze | solution.py:61
  42.7 3.5 %gather_fusion.1 = bf16[30,128,5,128]{3,1,2,0:T(8,128)(2,1)} fusion(bf16[8,128,5,128]{3,1,2,0:T(8,128)(2,1)S(1)} %copy.39, s32[1024]{0:T(1024)S(1)} %pad_clamp_fusion), kind=kCustom, calls=%fused_computation.1.clone | custom fusion | bytes 9830520 | tf_op jit(solution)/shard_map/jit(_take)/gather | solution.py:62
  46.1 3.5 %gather_fusion = bf16[30,128,5,128]{3,1,2,0:T(8,128)(2,1)} fusion(bf16[8,128,5,128]{3,1,2,0:T(8,128)(2,1)S(1)} %copy.35, s32[1024]{0:T(1024)S(1)} %pad_clamp_fusion), kind=kCustom, calls=%fused_computation.clone | custom fusion | bytes 9830520 | tf_op jit(solution)/shard_map/jit(_take)/gather | solution.py:63
  49.6 7.0 %broadcast_select_fusion = (bf16[6,5,128,5,128]{4,2,3,1,0:T(8,128)(2,1)S(1)}, bf16[6,5,128,5,128]{4,2,3,1,0:T(8,128)(2,1)}) fusion(bf16[6,5,128,5,128]{4,2,3,1,0:T(8,128)(2,1)} %bitcast.18, pred[6,5]{1,0:T(8,128)(4,1)S(1)} %get-tuple-element.8, bf16[6,5,128,5,128]{4,2,3,1,0:T(8,128)(2,1)} %bitcast.19), kind=kLoop, calls=%fused_computation.9 | loop fusion | flops 4915200 | bytes 19660830 | tf_op jit(solution)/shard_map/jit(_take)/select_n | solution.py:62
  56.6 6.6 %copy.36 = bf16[6,5,128,5,128]{4,2,1,3,0:T(8,128)(2,1)} copy(bf16[6,5,128,5,128]{4,2,3,1,0:T(8,128)(2,1)} %get-tuple-element.15) | data formatting | bytes 9830400 | tf_op jit(solution)/shard_map/jit(_take)/select_n | solution.py:63
  63.2 1.0 %copy.40 = bf16[6,5,128,5,128]{4,2,1,3,0:T(8,128)(2,1)S(1)} copy(bf16[6,5,128,5,128]{4,2,3,1,0:T(8,128)(2,1)S(1)} %get-tuple-element.14) | data formatting | bytes 9830400 | tf_op jit(solution)/shard_map/jit(_take)/select_n | solution.py:62
  64.5 1.7 %fusion.11 = f32[6,5,128,640]{3,2,1,0:T(8,128)S(1)} fusion(bf16[6,640,5,128]{3,1,2,0:T(8,128)(2,1)S(1)} %bitcast.17, bf16[6,128,5,128]{1,0,3,2:T(8,128)(2,1)S(1)} %copy-done.2), kind=kOutput, calls=%fused_computation.21 | convolution fusion | flops 629145600 | bytes 15728640 | tf_op jit(solution)/shard_map/tqhd,tkhd->thqk/dot_general | solution.py:65
  66.3 2.7 %fusion.22 = f32[6,5,128]{2,1,0:T(8,128)S(1)} fusion(f32[6,5,128,640]{3,2,1,0:T(8,128)S(1)} %fusion.11), kind=kOutput, calls=%fused_computation.36 | output fusion | flops 9831039 | bytes 9845760 | tf_op jit(solution)/shard_map/sub | solution.py:69
  69.0 1.1 %copy-done = f32[6,5,128,640]{3,2,1,0:T(8,128)} copy-done((f32[6,5,128,640]{3,2,1,0:T(8,128)}, f32[6,5,128,640]{3,2,1,0:T(8,128)S(1)}, u32[]{:S(2)}) %copy-start) | copy-done | bytes 9830424
  70.1 16.6 %fusion.10 = bf16[6,128,5,128]{1,3,2,0:T(8,128)(2,1)S(1)} fusion(bf16[6,640,5,128]{3,1,2,0:T(8,128)(2,1)} %bitcast.20, f32[6,5,128]{2,1,0:T(8,128)S(1)} %fusion.22, f32[6,5,128,640]{3,2,1,0:T(8,128)} %copy-done), kind=kOutput, calls=%fused_computation.20 | convolution fusion | flops 641929600 | bytes 15744000 | tf_op jit(solution)/shard_map/thqk,tkhd->tqhd/dot_general | solution.py:71
  87.7 2.0 %reshape.88 = bf16[1,768,640]{2,1,0:T(8,128)(2,1)} reshape(bf16[6,128,5,128]{3,2,1,0:T(8,128)(2,1)S(1)} %copy.50) | data formatting | bytes 1966080 | tf_op jit(solution)/shard_map/reshape | solution.py:74
  (20 shorter events, 3.5 us)
Async XLA Ops:
  0.0 26.1 %copy-start.3 = (bf16[1,768,640]{2,1,0:T(8,128)(2,1)S(1)}, bf16[1,768,640]{2,1,0:T(8,128)(2,1)}, u32[]{:S(2)}) copy-start(bf16[1,768,640]{2,1,0:T(8,128)(2,1)} %param.9) | copy-start | bytes 2949124
  0.0 25.9 %copy-start.4 = (s32[1,6,5]{1,0,2:T(1,128)S(1)}, s32[1,6,5]{1,0,2:T(1,128)}, u32[]{:S(2)}) copy-start(s32[1,6,5]{1,0,2:T(1,128)} %param.13) | copy-start | bytes 364
  18.7 0.9 %copy-start.1 = (bf16[1,768,640]{2,1,0:T(8,128)(2,1)}, bf16[1,768,640]{2,1,0:T(8,128)(2,1)S(1)}, u32[]{:S(2)}) copy-start(bf16[1,768,640]{2,1,0:T(8,128)(2,1)S(1)} %fusion.8) | copy-start | bytes 2949124
  21.5 10.2 %collective-permute-start.1 = (bf16[2,128,640]{2,1,0:T(8,128)(2,1)}, bf16[2,128,640]{2,1,0:T(8,128)(2,1)S(1)}, u32[]{:S(2)}, u32[]{:S(2)}) collective-permute-start(bf16[2,128,640]{2,1,0:T(8,128)(2,1)} %get-tuple-element.13), channel_id=1, source_target_pairs={{4,0},{5,1},{6,2},{7,3},{12,8},{13,9},{14,10},{15,11},{20,16},{21,... | collective-permute-start | bytes 983048 | tf_op jit(solution)/shard_map/ppermute | solution.py:22
  22.8 8.9 %collective-permute-start = (bf16[2,128,640]{2,1,0:T(8,128)(2,1)}, bf16[2,128,640]{2,1,0:T(8,128)(2,1)S(1)}, u32[]{:S(2)}, u32[]{:S(2)}) collective-permute-start(bf16[2,128,640]{2,1,0:T(8,128)(2,1)} %get-tuple-element.12), channel_id=1, source_target_pairs={{0,4},{1,5},{2,6},{3,7},{8,12},{9,13},{10,14},{11,15},{16,20},{17,... | collective-permute-start | bytes 983048 | tf_op jit(solution)/shard_map/ppermute | solution.py:21
  63.2 1.3 %copy-start.2 = (bf16[6,128,5,128]{1,0,3,2:T(8,128)(2,1)S(1)}, bf16[6,128,5,128]{1,0,3,2:T(8,128)(2,1)}, u32[]{:S(2)}) copy-start(bf16[6,128,5,128]{1,0,3,2:T(8,128)(2,1)} %multiply_convert_fusion) | copy-start | bytes 2949124
  66.3 3.8 %copy-start = (f32[6,5,128,640]{3,2,1,0:T(8,128)}, f32[6,5,128,640]{3,2,1,0:T(8,128)S(1)}, u32[]{:S(2)}) copy-start(f32[6,5,128,640]{3,2,1,0:T(8,128)S(1)} %fusion.11) | copy-start | bytes 29491204
where the time goes:
time: 90.2 us; the launch traced here: 89.6 us
  local copies, waits for them, and re-layouts  33.8 us (37%)
  other arithmetic  18.5 us (21%)
  matrix products  18.4 us (20%)
  blocking collectives  13.7 us (15%)
  starting transfers between devices  4.35 us (5%)
  between operations  0.91 us (1%)
    dot_general x1, matrix products, shards(): jnp.einsum('thqk,tkhd->tqhd', weights, picked_values, preferred_element_t...  16.6 us
    psum x1, blocking collectives, shards(): q_total, k_total = lax.psum((q_part, k_part), 'mp')  13.7 us
    select_n x1, other arithmetic, shards(): jnp.take(key_tiles, local_ids, axis=0).reshape(tiles_dev, -1, heads_dev, DH)  7.01 us
    select_n x1, local copies, waits for them, and re-layouts, shards(): jnp.take(value_tiles, local_ids, axis=0)  6.61 us
    another operation x2, local copies, waits for them, and re-layouts, shards(): value_tiles = values_wide.reshape(tiles_dev + 2, TILE, heads_dev, DH)  6.08 us
    convert_element_type x2, local copies, waits for them, and re-layouts, scaled_rows(): rows.astype(jnp.float32) * lax.rsqrt(mean_sq + epsilon)[:, None]  3.91 us
    gather x1, local copies, waits for them, and re-layouts, shards(): jnp.take(value_tiles, local_ids, axis=0)  3.49 us
    gather x1, local copies, waits for them, and re-layouts, shards(): jnp.take(key_tiles, local_ids, axis=0).reshape(tiles_dev, -1, heads_dev, DH)  3.45 us
  transfers between devices with their start and end apart: 2, of which 0 were waited for; matrix products, arithmetic and copies ran while one was open for 6% of the time, Pallas kernels for 0%

commit v1 on v0

v1 whole, which is shorter than its diff:
```python
import functools

import jax
import jax.numpy as jnp
from jax import lax
from jax.experimental import pallas as pl
from jax.experimental.pallas import tpu as pltpu
from jax.sharding import PartitionSpec as P

DH = 128
TILE = 128
EPSILON = 1e-06
SWITCH_STEP = 875
LOG2E = 1.4426950408889634
MIB = 1 << 20

HBM = pl.BlockSpec(memory_space=pltpu.HBM)
VMEM = pl.BlockSpec(memory_space=pltpu.VMEM)
SMEM = pl.BlockSpec(memory_space=pltpu.SMEM)


def tile_rows(index):
    if isinstance(index, int):
        return pl.ds(index * TILE, TILE)
    return pl.ds(pl.multiple_of(index * TILE, TILE), TILE)


def sums_kernel(chunk, edge_ref, q_hbm, k_hbm, v_hbm, sums_ref, *rest):
    edges = rest[: edge_ref.shape[0]]
    q_buf, k_buf, sems, edge_sems = rest[edge_ref.shape[0] :]
    rows, width = q_hbm.shape
    copies = []
    for a, (src, dst) in enumerate(((q_hbm, q_buf), (k_hbm, k_buf))):
        for j in range(rows // chunk):
            part = pl.ds(j * chunk, chunk)
            copies.append(pltpu.make_async_copy(src.at[part], dst.at[part], sems.at[a, j]))
            copies[-1].start()
    edge_copies = []
    for e, edge in enumerate(edges):
        part = tile_rows(edge_ref[e])
        for a, src in enumerate((k_hbm, v_hbm)):
            edge_copies.append(pltpu.make_async_copy(src.at[part], edge.at[a], edge_sems.at[e, a]))
            edge_copies[-1].start()
    diagonal = lax.broadcasted_iota(jnp.int32, (TILE, TILE), 0) == lax.broadcasted_iota(
        jnp.int32, (TILE, TILE), 1
    )
    tiles = rows // TILE
    for a, buf in enumerate((q_buf, k_buf)):
        for t in range(tiles):
            if t * TILE % chunk == 0:
                copies[a * (rows // chunk) + t * TILE // chunk].wait()
            total = 0.0
            for j in range(width // DH):
                x = buf[t * TILE : (t + 1) * TILE, j * DH : (j + 1) * DH].astype(jnp.float32)
                total = total + x * x
            total = jnp.sum(total, axis=1, keepdims=True)
            total = jnp.sum(jnp.where(diagonal, total, 0.0), axis=0, keepdims=True)
            sums_ref[a * tiles + t : a * tiles + t + 1, :] = total
    for copy in edge_copies:
        copy.wait()


def gather_kernel(q_hbm, k_hbm, v_hbm, *rest):
    edges = rest[:-4]
    q_ref, k_ref, v_ref, sems = rest[-4:]
    rows = q_hbm.shape[0]
    own = pl.ds(0, rows)
    copies = [
        pltpu.make_async_copy(q_hbm, q_ref, sems.at[0]),
        pltpu.make_async_copy(k_hbm, k_ref.at[own], sems.at[1]),
        pltpu.make_async_copy(v_hbm, v_ref.at[own], sems.at[2]),
    ]
    for e, edge in enumerate(edges):
        part = pl.ds(rows + e * TILE, TILE)
        copies.append(pltpu.make_async_copy(edge.at[0], k_ref.at[part], sems.at[3 + 2 * e]))
        copies.append(pltpu.make_async_copy(edge.at[1], v_ref.at[part], sems.at[4 + 2 * e]))
    for copy in copies:
        copy.start()
    for copy in copies:
        copy.wait()


def attention_kernel(
    full_width, depth, slot_ref, step_ref, sums_ref, edge_sums_ref, gq_ref, gk_ref, q_ref, k_ref, v_ref,
    out_hbm, out_buf, scale_buf, sems,
):
    tiles, slots = slot_ref.shape
    heads = q_ref.shape[1] // DH
    expert = jnp.where(step_ref[0] >= SWITCH_STEP, 0, 1)
    gain = gq_ref[pl.ds(expert, 1), :] * gk_ref[pl.ds(expert, 1), :] * (DH ** -0.5 * LOG2E)

    def scale(sums):
        return lax.rsqrt(sums * (1.0 / full_width) + EPSILON)

    q_scale = scale(sums_ref[0:tiles, :])
    q_scale = jnp.concatenate([q_scale, jnp.zeros((8 - tiles % 8, TILE), jnp.float32)], axis=0).T
    scale_buf[0:tiles, :] = scale(sums_ref[tiles : 2 * tiles, :])
    scale_buf[tiles : tiles + edge_sums_ref.shape[0], :] = scale(edge_sums_ref[...])
    ones = jnp.ones((TILE, DH), jnp.bfloat16)

    def scores(i, h):
        cols = slice(h * DH, (h + 1) * DH)
        query = q_ref[i * TILE : (i + 1) * TILE, cols].astype(jnp.float32)
        query = (query * q_scale[:, i : i + 1] * gain[:, cols]).astype(jnp.bfloat16)
        return [
            lax.dot_general(
                query, k_ref[tile_rows(slot_ref[i, n]), cols], (((1,), (1,)), ((), ())),
                preferred_element_type=jnp.float32,
            )
            for n in range(slots)
        ]

    def mix(i, h, score):
        cols = slice(h * DH, (h + 1) * DH)
        score = [x * scale_buf[pl.ds(slot_ref[i, n], 1), :] for n, x in enumerate(score)]
        top = jnp.max(functools.reduce(jnp.maximum, score), axis=1, keepdims=True)
        weight = jnp.concatenate([jnp.exp2(x - top).astype(jnp.bfloat16) for x in score], axis=1)
        value = jnp.concatenate(
            [
                jnp.concatenate([v_ref[tile_rows(slot_ref[i, n]), cols], ones], axis=1)
                for n in range(slots)
            ],
            axis=0,
        )
        return jnp.dot(weight, value, preferred_element_type=jnp.float32)

    def finish(i, h, mixed):
        rows = pl.ds(i * TILE, TILE)
        out_buf[rows, h * DH : (h + 1) * DH] = (mixed[:, :DH] / mixed[:, DH:]).astype(jnp.bfloat16)
        if h == heads - 1:
            pltpu.make_async_copy(out_buf.at[rows], out_hbm.at[rows], sems.at[i]).start()

    pairs = [(i, h) for i in range(tiles) for h in range(heads)]
    score, mixed = {}, {}
    for s in range(len(pairs) + depth + 1):
        if s < len(pairs):
            score[s] = scores(*pairs[s])
        if depth <= s < len(pairs) + depth:
            mixed[s - depth] = mix(*pairs[s - depth], score.pop(s - depth))
        if s > depth:
            finish(*pairs[s - depth - 1], mixed.pop(s - depth - 1))
    for i in range(tiles):
        rows = pl.ds(i * TILE, TILE)
        pltpu.make_async_copy(out_buf.at[rows], out_hbm.at[rows], sems.at[i]).wait()


def shards(queries, key_input, value_input, timestep, neighbours, q_gain, k_gain):
    q_rows, k_rows, v_rows = queries[0], key_input[0], value_input[0]
    rows, width = q_rows.shape
    tiles = rows // TILE
    slots = neighbours.shape[2]
    groups, devices = lax.axis_size("mp"), lax.axis_size("seq")
    place = lax.axis_index("seq")

    up = [(i, (i + 1) % devices) for i in range(devices)]
    down = [(i, (i - 1) % devices) for i in range(devices)]
    if devices == 2:
        hops = [up]
        edge_tiles = jnp.where(place == 0, tiles - 1, 0).reshape(1)
    else:
        hops = [down, up]
        edge_tiles = jnp.array([0, tiles - 1], jnp.int32)
    count = len(hops)
    edge_tiles = edge_tiles.astype(jnp.int32)

    chunk = 2 * TILE if tiles % 2 == 0 else TILE
    sums, *edges = pl.pallas_call(
        functools.partial(sums_kernel, chunk),
        out_shape=[pltpu.VMEM((2 * tiles, TILE), jnp.float32)]
        + [pltpu.VMEM((2, TILE, width), jnp.bfloat16)] * count,
        in_specs=[SMEM, HBM, HBM, HBM],
        out_specs=[VMEM] * (1 + count),
        scratch_shapes=[
            pltpu.VMEM((rows, width), jnp.bfloat16),
            pltpu.VMEM((rows, width), jnp.bfloat16),
            pltpu.SemaphoreType.DMA((2, rows // chunk)),
            pltpu.SemaphoreType.DMA((count, 2)),
        ],
        compiler_params=pltpu.CompilerParams(vmem_limit_bytes=58 * MIB),
        cost_estimate=pl.CostEstimate(flops=4 * rows * width, bytes_accessed=4 * rows * width, transcendentals=0),
        name="sums",
    )(edge_tiles, q_rows, k_rows, v_rows)

    total = sums
    for s in list(range(groups - 1, groups - 2, -1)) + list(range(1, groups - 1)):
        total = total + lax.ppermute(sums, "mp", [(i, (i + s) % groups) for i in range(groups)])
    edges = [lax.ppermute(edge, "seq", hop) for edge, hop in zip(edges, hops)]
    edge_sums = jnp.concatenate(
        [
            lax.ppermute(lax.dynamic_slice_in_dim(total, tiles + edge_tiles[e], 1), "seq", hop)
            for e, hop in enumerate(hops)
        ],
        axis=0,
    )

    q_all, k_all, v_all = pl.pallas_call(
        gather_kernel,
        out_shape=[
            pltpu.VMEM((rows, width), jnp.bfloat16),
            pltpu.VMEM((rows + count * TILE, width), jnp.bfloat16),
            pltpu.VMEM((rows + count * TILE, width), jnp.bfloat16),
        ],
        in_specs=[HBM] * 3 + [VMEM] * count,
        out_specs=[VMEM] * 3,
        scratch_shapes=[pltpu.SemaphoreType.DMA((3 + 2 * count,))],
        compiler_params=pltpu.CompilerParams(vmem_limit_bytes=58 * MIB),
        cost_estimate=pl.CostEstimate(flops=0, bytes_accessed=6 * rows * width, transcendentals=0),
        name="gather",
    )(q_rows, k_rows, v_rows, *edges)

    local = neighbours[0] - place * tiles
    where_at = jnp.where(local == tiles, tiles, jnp.where(local < 0, tiles + count - 1, local)).astype(jnp.int32)

    pairs = tiles * slots * TILE * TILE * (width // DH)
    mixed = pl.pallas_call(
        functools.partial(attention_kernel, width * groups, 2),
        out_shape=jax.ShapeDtypeStruct((rows, width), jnp.bfloat16),
        in_specs=[SMEM, SMEM] + [VMEM] * 7,
        out_specs=HBM,
        scratch_shapes=[
            pltpu.VMEM((rows, width), jnp.bfloat16),
            pltpu.VMEM((tiles + 2, TILE), jnp.float32),
            pltpu.SemaphoreType.DMA((tiles,)),
        ],
        compiler_params=pltpu.CompilerParams(vmem_limit_bytes=32 * MIB),
        cost_estimate=pl.CostEstimate(flops=4 * pairs * DH, bytes_accessed=2 * rows * width, transcendentals=pairs),
        name="attention",
    )(where_at, timestep, total, edge_sums, q_gain, k_gain, q_all, k_all, v_all)
    return mixed.reshape(1, rows, width)


def solution(mesh):
    return jax.shard_map(
        shards,
        mesh=mesh,
        in_specs=(
            P("expert", "seq", "mp"),
            P("expert", "seq", "mp"),
            P("expert", "seq", "mp"),
            P("expert"),
            P("expert", "seq", None),
            P(None, "mp"),
            P(None, "mp"),
        ),
        out_specs=P("expert", "seq", "mp"),
        check_vma=False,
    )
```

time: 90.2 us -> 22.9 us (0.25)
  local copies, waits for them, and re-layouts: 33.8 us -> 0.84 us
  other arithmetic: 18.5 us -> 0.01 us
  matrix products: 18.4 us -> 0 us
  blocking collectives: 13.7 us -> 0 us
  Pallas kernels: 0 us -> 11.5 us
  starting transfers between devices: 4.35 us -> 8 us
  waiting for transfers between devices: 0.01 us -> 1.53 us
    dot_general x2 -> x0, matrix products: 18.4 us -> none  [the longest x1 16.6 us: shards(): jnp.einsum('thqk,tkhd->tqhd', weights, picked_values, preferred_element_t...]
    psum x1 -> x0, blocking collectives: 13.7 us -> none  [shards(): q_total, k_total = lax.psum((q_part, k_part), 'mp')]
    pallas_call x0 -> x3, Pallas kernels: none -> 11.5 us  [the longest x1 6.76 us: shards(): pl.pallas_call(functools.partial(attention_kernel, width * groups, 2), ou...]
    another operation x4 -> x0, local copies, waits for them, and re-layouts: 7.91 us -> none  [the longest x2 6.08 us: shards(): value_tiles = values_wide.reshape(tiles_dev + 2, TILE, heads_dev, DH)]
    select_n x2 -> x0, local copies, waits for them, and re-layouts: 7.61 us -> none  [the longest x1 6.61 us: shards(): jnp.take(value_tiles, local_ids, axis=0)]
    select_n x1, other arithmetic: 7.01 us -> 0.01 us  [shards(): jnp.where(local == tiles, tiles, jnp.where(local < 0, tiles + count - 1,...]
    gather x2 -> x0, local copies, waits for them, and re-layouts: 6.94 us -> none  [the longest x1 3.49 us: shards(): jnp.take(value_tiles, local_ids, axis=0)]
    convert_element_type x2 -> x0, local copies, waits for them, and re-layouts: 3.91 us -> none  [scaled_rows(): rows.astype(jnp.float32) * lax.rsqrt(mean_sq + epsilon)[:, None]]
  transfers between devices with their start and end apart: 2 -> 5, of which waited for: 0 -> 1; matrix products, arithmetic and copies ran while one was open for 6% -> 1% of each run, Pallas kernels for 0% -> 12%
where the time goes in v1:
time: 22.9 us; the launch traced here: 22.6 us
  Pallas kernels  11.5 us (50%)
  starting transfers between devices  8 us (35%)
  waiting for transfers between devices  1.53 us (7%)
  local copies, waits for them, and re-layouts  0.84 us (4%)
  between operations  0.75 us (3%)
    ppermute x3, starting transfers between devices, shards(): lax.ppermute(sums, 'mp', [(i, (i + s) % groups) for i in range(groups)])  7.93 us
    pallas_call x1, Pallas kernels, shards(): pl.pallas_call(functools.partial(attention_kernel, width * groups, 2), ou...  6.76 us
    pallas_call x1, Pallas kernels, shards(): pl.pallas_call(gather_kernel, out_shape=[pltpu.VMEM((rows, width), jnp.bf...  2.81 us
    pallas_call x1, Pallas kernels, shards(): pl.pallas_call(functools.partial(sums_kernel, chunk), out_shape=[pltpu.VM...  1.94 us
    ppermute x3, waiting for transfers between devices, shards(): lax.ppermute(sums, 'mp', [(i, (i + s) % groups) for i in range(groups)])  1.53 us
    unnamed x9, local copies, waits for them, and re-layouts  0.83 us
  transfers between devices with their start and end apart: 5, of which 1 were waited for; matrix products, arithmetic and copies ran while one was open for 1% of the time, Pallas kernels for 12%

profile of v1, /device:TPU:0, one launch (start us, length us, event | category | flops | bytes accessed | tf_op | source)
XLA Modules:
  0.0 22.6 jit_solution(416168054292766701)
XLA Ops:
  0.0 0.0 copy-start.3
  0.0 1.9 %sums.1 = (f32[12,128]{1,0:T(8,128)S(1)}, bf16[2,128,640]{2,1,0:T(8,128)(2,1)S(1)}) custom-call(s32[1]{0:T(128)} %bitcast.1.edge_ref, bf16[768,640]{1,0:T(8,128)(2,1)} %bitcast.10, bf16[768,640]{1,0:T(8,128)(2,1)} %bitcast.12, bf16[768,640]{1,0:T(8,128)(2,1)} %bitcast.14), custom_call_target="tpu_custom_call" | custom-call | flops 1966080 | bytes 1966080 | tf_op jit(solution)/shard_map/sums/pallas_call | solution.py:167
  1.9 4.1 %collective-permute-start.2 = (f32[12,128]{1,0:T(8,128)S(1)}, f32[12,128]{1,0:T(8,128)S(1)}, u32[]{:S(2)}, u32[]{:S(2)}) collective-permute-start(f32[12,128]{1,0:T(8,128)S(1)} %get-tuple-element.10), channel_id=1, source_target_pairs={{0,2},{1,3},{2,0},{3,1},{4,6},{5,7},{6,4},{7,5},{8,10},{9,11},{10,... | collective-permute-start | bytes 18440 | tf_op jit(solution)/shard_map/ppermute | solution.py:186
  6.1 1.6 %collective-permute-start.1 = (f32[12,128]{1,0:T(8,128)S(1)}, f32[12,128]{1,0:T(8,128)S(1)}, u32[]{:S(2)}, u32[]{:S(2)}) collective-permute-start(f32[12,128]{1,0:T(8,128)S(1)} %get-tuple-element.10), channel_id=1, source_target_pairs={{0,1},{1,2},{2,3},{3,0},{4,5},{5,6},{6,7},{7,4},{8,9},{9,10},{10,1... | collective-permute-start | bytes 18440 | tf_op jit(solution)/shard_map/ppermute | solution.py:186
  7.6 2.2 %collective-permute-start = (f32[12,128]{1,0:T(8,128)S(1)}, f32[12,128]{1,0:T(8,128)S(1)}, u32[]{:S(2)}, u32[]{:S(2)}) collective-permute-start(f32[12,128]{1,0:T(8,128)S(1)} %get-tuple-element.10), channel_id=1, source_target_pairs={{0,3},{1,0},{2,1},{3,2},{4,7},{5,4},{6,5},{7,6},{8,11},{9,8},{10,9... | collective-permute-start | bytes 18440 | tf_op jit(solution)/shard_map/ppermute | solution.py:186
  9.9 0.0 collective-permute-start.4
  9.9 0.0 copy-done.3
  9.9 0.1 copy.8
  10.0 0.0 collective-permute-done.2
  10.0 1.5 %collective-permute-done.1 = f32[12,128]{1,0:T(8,128)S(1)} collective-permute-done((f32[12,128]{1,0:T(8,128)S(1)}, f32[12,128]{1,0:T(8,128)S(1)}, u32[]{:S(2)}, u32[]{:S(2)}) %collective-permute-start.1) | collective-permute-done | bytes 6176 | tf_op jit(solution)/shard_map/ppermute | solution.py:186
  11.5 0.0 collective-permute-done
  11.5 0.1 collective-permute-start.3
  12.3 0.0 copy-start
  12.3 0.0 copy-start.1
  12.3 0.0 collective-permute-done.4.rest_0_
  12.3 0.0 copy-start.2
  12.3 0.7 %copy-done.2 = bf16[2,128,640]{2,1,0:T(8,128)(2,1)} copy-done((bf16[2,128,640]{2,1,0:T(8,128)(2,1)}, bf16[2,128,640]{2,1,0:T(8,128)(2,1)S(1)}, u32[]{:S(2)}) %copy-start.2) | copy-done | bytes 327704
  13.0 2.8 %gather.1 = (bf16[768,640]{1,0:T(8,128)(2,1)S(1)}, bf16[896,640]{1,0:T(8,128)(2,1)S(1)}, bf16[896,640]{1,0:T(8,128)(2,1)S(1)}) custom-call(bf16[768,640]{1,0:T(8,128)(2,1)} %bitcast.11, bf16[768,640]{1,0:T(8,128)(2,1)} %bitcast.13, bf16[768,640]{1,0:T(8,128)(2,1)} %bitcast.15, bf16[2,128,640]{2,1,0:T(8,128)(2,1)} %copy-done.2), custom_call_target="tpu_custom_call" | custom-call | bytes 2949120 | tf_op jit(solution)/shard_map/gather/pallas_call | solution.py:196
  15.9 0.0 collective-permute-done.3.edge_sums_ref
  15.9 0.0 copy-done
  15.9 0.0 copy-done.1
  15.9 6.8 %attention.1 = bf16[768,640]{1,0:T(8,128)(2,1)} custom-call(s32[6,5]{1,0:T(8,128)S(1)} %fusion.slot_ref, s32[1]{0:T(128)S(6)} %copy.9.step_ref, f32[12,128]{1,0:T(8,128)S(1)} %add_add_fusion.sums_ref, f32[1,128]{1,0:T(1,128)S(1)} %collective-permute-done.3.edge_sums_ref, f32[2,640]{1,0:T(2,128)S(1)} %copy-done, f32[2,640]{1,0:T(2,128)S(1)} %copy-done.1, ...), custom_call_target="tpu_custom_call" | custom-call | flops 1258291200 | bytes 983040 | tf_op jit(solution)/shard_map/attention/pallas_call | solution.py:215
  (3 shorter events, 0.0 us)
Async XLA Ops:
  0.0 9.9 %copy-start.3 = (s32[1,6,5]{1,0,2:T(1,128)S(1)}, s32[1,6,5]{1,0,2:T(1,128)}, u32[]{:S(2)}) copy-start(s32[1,6,5]{1,0,2:T(1,128)} %param.11) | copy-start | bytes 364
  1.9 8.0 %collective-permute-start.2 = (f32[12,128]{1,0:T(8,128)S(1)}, f32[12,128]{1,0:T(8,128)S(1)}, u32[]{:S(2)}, u32[]{:S(2)}) collective-permute-start(f32[12,128]{1,0:T(8,128)S(1)} %get-tuple-element.10), channel_id=1, source_target_pairs={{0,2},{1,3},{2,0},{3,1},{4,6},{5,7},{6,4},{7,5},{8,10},{9,11},{10,... | collective-permute-start | bytes 18440 | tf_op jit(solution)/shard_map/ppermute | solution.py:186
  6.1 5.4 %collective-permute-start.1 = (f32[12,128]{1,0:T(8,128)S(1)}, f32[12,128]{1,0:T(8,128)S(1)}, u32[]{:S(2)}, u32[]{:S(2)}) collective-permute-start(f32[12,128]{1,0:T(8,128)S(1)} %get-tuple-element.10), channel_id=1, source_target_pairs={{0,1},{1,2},{2,3},{3,0},{4,5},{5,6},{6,7},{7,4},{8,9},{9,10},{10,1... | collective-permute-start | bytes 18440 | tf_op jit(solution)/shard_map/ppermute | solution.py:186
  7.6 3.9 %collective-permute-start = (f32[12,128]{1,0:T(8,128)S(1)}, f32[12,128]{1,0:T(8,128)S(1)}, u32[]{:S(2)}, u32[]{:S(2)}) collective-permute-start(f32[12,128]{1,0:T(8,128)S(1)} %get-tuple-element.10), channel_id=1, source_target_pairs={{0,3},{1,0},{2,1},{3,2},{4,7},{5,4},{6,5},{7,6},{8,11},{9,8},{10,9... | collective-permute-start | bytes 18440 | tf_op jit(solution)/shard_map/ppermute | solution.py:186
  9.9 2.4 %collective-permute-start.4 = (bf16[2,128,640]{2,1,0:T(8,128)(2,1)S(1)}, bf16[2,128,640]{2,1,0:T(8,128)(2,1)S(1)}, u32[]{:S(2)}, u32[]{:S(2)}) collective-permute-start(bf16[2,128,640]{2,1,0:T(8,128)(2,1)S(1)} %get-tuple-element.11), channel_id=1, source_target_pairs={{0,4},{4,0},{1,5},{5,1},{2,6},{6,2},{3,7},{7,3},{8,12},{12,8},{9,1... | collective-permute-start | bytes 983048 | tf_op jit(solution)/shard_map/ppermute | solution.py:187
  11.5 4.3 %collective-permute-start.3 = (f32[1,128]{1,0:T(1,128)S(1)}, f32[1,128]{1,0:T(1,128)S(1)}, u32[]{:S(2)}, u32[]{:S(2)}) collective-permute-start(f32[1,128]{1,0:T(1,128)S(1)} %constant_dynamic-slice_fusion), channel_id=1, source_target_pairs={{0,4},{4,0},{1,5},{5,1},{2,6},{6,2},{3,7},{7,3},{8,12},{12,8},{9,1... | collective-permute-start | bytes 1544 | tf_op jit(solution)/shard_map/ppermute | solution.py:190
  12.3 3.6 %copy-start = (f32[2,640]{1,0:T(2,128)S(1)}, f32[2,640]{1,0:T(2,128)}, u32[]{:S(2)}) copy-start(f32[2,640]{1,0:T(2,128)} %gq_ref.1) | copy-start | bytes 15364
  12.3 3.6 %copy-start.1 = (f32[2,640]{1,0:T(2,128)S(1)}, f32[2,640]{1,0:T(2,128)}, u32[]{:S(2)}) copy-start(f32[2,640]{1,0:T(2,128)} %gk_ref.1) | copy-start | bytes 15364
  12.3 0.7 %copy-start.2 = (bf16[2,128,640]{2,1,0:T(8,128)(2,1)}, bf16[2,128,640]{2,1,0:T(8,128)(2,1)S(1)}, u32[]{:S(2)}) copy-start(bf16[2,128,640]{2,1,0:T(8,128)(2,1)S(1)} %collective-permute-done.4.rest_0_) | copy-start | bytes 983044

commit v2 on v1

v2 whole, which is shorter than its diff:
```python
import functools

import jax
import jax.numpy as jnp
from jax import lax
from jax.experimental import pallas as pl
from jax.experimental.pallas import tpu as pltpu
from jax.sharding import PartitionSpec as P

DH = 128
TILE = 128
EPSILON = 1e-06
SWITCH_STEP = 875
LOG2E = 1.4426950408889634
MIB = 1 << 20

HBM = pl.BlockSpec(memory_space=pltpu.HBM)
VMEM = pl.BlockSpec(memory_space=pltpu.VMEM)
SMEM = pl.BlockSpec(memory_space=pltpu.SMEM)


def tile_rows(index):
    if isinstance(index, int):
        return pl.ds(index * TILE, TILE)
    return pl.ds(pl.multiple_of(index * TILE, TILE), TILE)


def sums_kernel(chunk, edge_ref, q_hbm, k_hbm, v_hbm, sums_ref, q_buf, k_buf, *rest):
    *edges, sems, edge_sems = rest
    rows, width = q_hbm.shape
    copies = []
    for a, (src, dst) in enumerate(((q_hbm, q_buf), (k_hbm, k_buf))):
        for j in range(rows // chunk):
            part = pl.ds(j * chunk, chunk)
            copies.append(pltpu.make_async_copy(src.at[part], dst.at[part], sems.at[a, j]))
            copies[-1].start()
    edge_copies = []
    for e, edge in enumerate(edges):
        part = tile_rows(edge_ref[e])
        for a, src in enumerate((k_hbm, v_hbm)):
            edge_copies.append(pltpu.make_async_copy(src.at[part], edge.at[a], edge_sems.at[e, a]))
            edge_copies[-1].start()
    diagonal = lax.broadcasted_iota(jnp.int32, (TILE, TILE), 0) == lax.broadcasted_iota(
        jnp.int32, (TILE, TILE), 1
    )
    tiles = rows // TILE
    for a, buf in enumerate((q_buf, k_buf)):
        for t in range(tiles):
            if t * TILE % chunk == 0:
                copies[a * (rows // chunk) + t * TILE // chunk].wait()
            total = 0.0
            for j in range(width // DH):
                x = buf[t * TILE : (t + 1) * TILE, j * DH : (j + 1) * DH].astype(jnp.float32)
                total = total + x * x
            total = jnp.sum(total, axis=1, keepdims=True)
            total = jnp.sum(jnp.where(diagonal, total, 0.0), axis=0, keepdims=True)
            sums_ref[a * tiles + t : a * tiles + t + 1, :] = total
    for copy in edge_copies:
        copy.wait()


def scores_kernel(place_ref, step_ref, gq_ref, gk_ref, q_ref, k_ref, v_hbm, *rest):
    del place_ref
    edges = rest[:-3]
    score_ref, v_ref, sems = rest[-3:]
    rows = q_ref.shape[0]
    heads = q_ref.shape[1] // DH
    copies = [pltpu.make_async_copy(v_hbm, v_ref.at[pl.ds(0, rows)], sems.at[0])]
    for e, edge in enumerate(edges):
        part = pl.ds(rows + e * TILE, TILE)
        copies.append(pltpu.make_async_copy(edge.at[1], v_ref.at[part], sems.at[1 + e]))
    for copy in copies:
        copy.start()
    expert = jnp.where(step_ref[0] >= SWITCH_STEP, 0, 1)
    gain = gq_ref[pl.ds(expert, 1), :] * gk_ref[pl.ds(expert, 1), :] * (DH ** -0.5 * LOG2E)
    for h in range(heads):
        cols = slice(h * DH, (h + 1) * DH)
        query = (q_ref[:, cols].astype(jnp.float32) * gain[:, cols]).astype(jnp.bfloat16)
        keys = [k_ref[:, cols]] + [edge[0, :, cols] for edge in edges]
        at = 0
        for key in keys:
            for j in range(0, key.shape[0], 2 * TILE):
                part = key[j : min(j + 2 * TILE, key.shape[0])]
                score_ref[h, :, at : at + part.shape[0]] = lax.dot_general(
                    query, part, (((1,), (1,)), ((), ())), preferred_element_type=jnp.float32
                )
                at += part.shape[0]
    for copy in copies:
        copy.wait()


def attention_kernel(
    full_width, depth, slot_ref, sums_ref, score_ref, v_ref, *rest
):
    *edge_sums, out_hbm, out_buf, k_scale, sems = rest
    tiles, slots = slot_ref.shape[0] - 1, slot_ref.shape[1]
    heads = score_ref.shape[0]

    def scale(sums):
        return lax.rsqrt(sums * (1.0 / full_width) + EPSILON)

    q_scale = scale(sums_ref[0:tiles, :])
    q_scale = jnp.concatenate([q_scale, jnp.zeros((8 - tiles % 8, TILE), jnp.float32)], axis=0).T
    k_scale[0:tiles, :] = scale(sums_ref[tiles : 2 * tiles, :])
    for e, border in enumerate(edge_sums):
        k_scale[tiles + e : tiles + e + 1, :] = scale(border[pl.ds(slot_ref[tiles, e], 1), :])
    ones = jnp.ones((TILE, DH), jnp.bfloat16)

    def weights(i, h):
        rows = pl.ds(i * TILE, TILE)
        score = [
            score_ref[h, rows, tile_rows(slot_ref[i, n])] * k_scale[pl.ds(slot_ref[i, n], 1), :]
            for n in range(slots)
        ]
        top = jnp.max(functools.reduce(jnp.maximum, score), axis=1, keepdims=True)
        return jnp.concatenate(
            [jnp.exp2((x - top) * q_scale[:, i : i + 1]).astype(jnp.bfloat16) for x in score], axis=1
        )

    def mix(i, h, weight):
        cols = slice(h * DH, (h + 1) * DH)
        value = jnp.concatenate(
            [
                jnp.concatenate([v_ref[tile_rows(slot_ref[i, n]), cols], ones], axis=1)
                for n in range(slots)
            ],
            axis=0,
        )
        return jnp.dot(weight, value, preferred_element_type=jnp.float32)

    def finish(i, h, mixed):
        rows = pl.ds(i * TILE, TILE)
        out_buf[rows, h * DH : (h + 1) * DH] = (mixed[:, :DH] / mixed[:, DH:]).astype(jnp.bfloat16)
        if h == heads - 1:
            pltpu.make_async_copy(out_buf.at[rows], out_hbm.at[rows], sems.at[i]).start()

    pairs = [(i, h) for i in range(tiles) for h in range(heads)]
    weight, mixed = {}, {}
    for s in range(len(pairs) + 2 * depth):
        if s < len(pairs):
            weight[s] = weights(*pairs[s])
        if depth <= s < len(pairs) + depth:
            mixed[s - depth] = mix(*pairs[s - depth], weight.pop(s - depth))
        if s >= 2 * depth:
            finish(*pairs[s - 2 * depth], mixed.pop(s - 2 * depth))
    for i in range(tiles):
        rows = pl.ds(i * TILE, TILE)
        pltpu.make_async_copy(out_buf.at[rows], out_hbm.at[rows], sems.at[i]).wait()


def shards(queries, key_input, value_input, timestep, neighbours, q_gain, k_gain):
    q_rows, k_rows, v_rows = queries[0], key_input[0], value_input[0]
    rows, width = q_rows.shape
    tiles = rows // TILE
    slots = neighbours.shape[2]
    groups, devices = lax.axis_size("mp"), lax.axis_size("seq")
    place = lax.axis_index("seq")

    up = [(i, (i + 1) % devices) for i in range(devices)]
    down = [(i, (i - 1) % devices) for i in range(devices)]
    if devices == 2:
        hops = [up]
        edge_tiles = jnp.where(place == 0, tiles - 1, 0).reshape(1)
    else:
        hops = [down, up]
        edge_tiles = jnp.array([0, tiles - 1], jnp.int32)
    count = len(hops)
    edge_tiles = edge_tiles.astype(jnp.int32)

    chunk = 2 * TILE if tiles % 2 == 0 else TILE
    sums, q_all, k_all, *edges = pl.pallas_call(
        functools.partial(sums_kernel, chunk),
        out_shape=[pltpu.VMEM((2 * tiles, TILE), jnp.float32)]
        + [pltpu.VMEM((rows, width), jnp.bfloat16)] * 2
        + [pltpu.VMEM((2, TILE, width), jnp.bfloat16)] * count,
        in_specs=[SMEM, HBM, HBM, HBM],
        out_specs=[VMEM] * (3 + count),
        scratch_shapes=[
            pltpu.SemaphoreType.DMA((2, rows // chunk)),
            pltpu.SemaphoreType.DMA((count, 2)),
        ],
        compiler_params=pltpu.CompilerParams(vmem_limit_bytes=58 * MIB),
        cost_estimate=pl.CostEstimate(flops=4 * rows * width, bytes_accessed=4 * rows * width, transcendentals=0),
        name="sums",
    )(edge_tiles, q_rows, k_rows, v_rows)

    parts = [
        lax.ppermute(sums, "mp", [(i, (i + s) % groups) for i in range(groups)])
        for s in list(range(groups - 1, groups - 2, -1)) + list(range(1, groups - 1))
    ]
    edges = [lax.ppermute(edge, "seq", hop) for edge, hop in zip(edges, hops)]

    local = neighbours[0] - place * tiles
    where_at = jnp.where(local == tiles, tiles, jnp.where(local < 0, tiles + count - 1, local))
    border = jnp.where(jnp.arange(slots) == 0, place, 1) if count == 1 else jnp.minimum(jnp.arange(slots), 1)
    where_at = jnp.concatenate([where_at, border[None]], axis=0).astype(jnp.int32)

    key_rows = rows + count * TILE
    held = width // DH * rows * key_rows * 4 + (key_rows + 2 * rows + 2 * count * TILE) * width * 2
    scores, v_all = pl.pallas_call(
        scores_kernel,
        out_shape=[
            pltpu.VMEM((width // DH, rows, key_rows), jnp.float32),
            pltpu.VMEM((key_rows, width), jnp.bfloat16),
        ],
        in_specs=[SMEM, SMEM, VMEM, VMEM, VMEM, VMEM, HBM] + [VMEM] * count,
        out_specs=[VMEM] * 2,
        scratch_shapes=[pltpu.SemaphoreType.DMA((1 + count,))],
        compiler_params=pltpu.CompilerParams(vmem_limit_bytes=63 * MIB - held),
        cost_estimate=pl.CostEstimate(flops=2 * rows * key_rows * width, bytes_accessed=6 * rows * width, transcendentals=0),
        name="scores",
    )(where_at, timestep, q_gain, k_gain, q_all, k_all, v_rows, *edges)
    *parts, scores, v_all = lax.optimization_barrier((*parts, scores, v_all))

    total = functools.reduce(jnp.add, parts, sums)
    borders = jnp.concatenate([total[tiles : tiles + 1], total[2 * tiles - 1 : 2 * tiles]], axis=0)
    edge_sums = [lax.ppermute(borders, "seq", hop) for hop in hops]

    pairs = tiles * slots * TILE * TILE * (width // DH)
    mixed = pl.pallas_call(
        functools.partial(attention_kernel, width * groups, 1),
        out_shape=jax.ShapeDtypeStruct((rows, width), jnp.bfloat16),
        in_specs=[SMEM] + [VMEM] * (3 + count),
        out_specs=HBM,
        scratch_shapes=[
            pltpu.VMEM((rows, width), jnp.bfloat16),
            pltpu.VMEM((tiles + 2, TILE), jnp.float32),
            pltpu.SemaphoreType.DMA((tiles,)),
        ],
        compiler_params=pltpu.CompilerParams(vmem_limit_bytes=32 * MIB),
        cost_estimate=pl.CostEstimate(flops=2 * pairs * DH, bytes_accessed=2 * rows * width, transcendentals=pairs),
        name="attention",
    )(where_at, total, scores, v_all, *edge_sums)
    return mixed.reshape(1, rows, width)


def solution(mesh):
    return jax.shard_map(
        shards,
        mesh=mesh,
        in_specs=(
            P("expert", "seq", "mp"),
            P("expert", "seq", "mp"),
            P("expert", "seq", "mp"),
            P("expert"),
            P("expert", "seq", None),
            P(None, "mp"),
            P(None, "mp"),
        ),
        out_specs=P("expert", "seq", "mp"),
        check_vma=False,
    )
```

time: 22.9 us -> 24.2 us (1.057)
  the two profiles are of different devices: /device:TPU:0 before, /device:TPU:13 now
where the time goes in v2:
time: 24.2 us; the launch traced here: 24 us
  Pallas kernels  10.2 us (42%)
  starting transfers between devices  7.16 us (30%)
  local copies, waits for them, and re-layouts  4.07 us (17%)
  waiting for transfers between devices  1.14 us (5%)
  between operations  0.74 us (3%)
  other arithmetic  0.63 us (3%)
    ppermute x3, starting transfers between devices, shards(): lax.ppermute(sums, 'mp', [(i, (i + s) % groups) for i in range(groups)])  5.57 us
    pallas_call x1, Pallas kernels, shards(): pl.pallas_call(functools.partial(attention_kernel, width * groups, 1), ou...  4.52 us
    unnamed x9, local copies, waits for them, and re-layouts  4.06 us
    pallas_call x1, Pallas kernels, shards(): pl.pallas_call(scores_kernel, out_shape=[pltpu.VMEM((width // DH, rows, k...  3.8 us
    pallas_call x1, Pallas kernels, shards(): pl.pallas_call(functools.partial(sums_kernel, chunk), out_shape=[pltpu.VM...  1.93 us
    ppermute x1, starting transfers between devices, shards(): edges = [lax.ppermute(edge, 'seq', hop) for edge, hop in zip(edges, hops)]  1.52 us
    ppermute x1, waiting for transfers between devices, shards(): edge_sums = [lax.ppermute(borders, 'seq', hop) for hop in hops]  1.13 us
    concatenate x1, other arithmetic, shards(): jnp.concatenate([where_at, border[None]], axis=0).astype(jnp.int32)  0.6 us
  transfers between devices with their start and end apart: 5, of which 1 were waited for; matrix products, arithmetic and copies ran while one was open for 6% of the time, Pallas kernels for 16%

profile of v2, /device:TPU:13, one launch (start us, length us, event | category | flops | bytes accessed | tf_op | source)
XLA Modules:
  0.0 24.0 jit_solution(5387064767305343652)
XLA Ops:
  0.0 1.9 %sums.1 = (f32[12,128]{1,0:T(8,128)S(1)}, bf16[768,640]{1,0:T(8,128)(2,1)S(1)}, bf16[768,640]{1,0:T(8,128)(2,1)S(1)}, bf16[2,128,640]{2,1,0:T(8,128)(2,1)S(1)}) custom-call(s32[1]{0:T(128)} %bitcast.1.edge_ref, bf16[768,640]{1,0:T(8,128)(2,1)} %bitcast.12, bf16[768,640]{1,0:T(8,128)(2,1)} %bitcast.13, bf16[768,640]{1,0:T(8,128)(2,1)} %bitcast.10), custom_call_target="tpu_custom_call" | custom-call | flops 1966080 | bytes 1966080 | tf_op jit(solution)/shard_map/sums/pallas_call | solution.py:171
  1.9 0.0 copy-start
  1.9 0.9 %copy-done = bf16[768,640]{1,0:T(8,128)(2,1)} copy-done((bf16[768,640]{1,0:T(8,128)(2,1)}, bf16[768,640]{1,0:T(8,128)(2,1)S(1)}, u32[]{:S(2)}) %copy-start) | copy-done | bytes 983064
  2.9 0.0 copy-start.1
  2.9 0.9 %copy-done.1 = bf16[768,640]{1,0:T(8,128)(2,1)} copy-done((bf16[768,640]{1,0:T(8,128)(2,1)}, bf16[768,640]{1,0:T(8,128)(2,1)S(1)}, u32[]{:S(2)}) %copy-start.1) | copy-done | bytes 983064
  3.8 0.2 collective-permute-start
  4.0 1.3 %collective-permute-start.1 = (f32[12,128]{1,0:T(8,128)S(1)}, f32[12,128]{1,0:T(8,128)S(1)}, u32[]{:S(2)}, u32[]{:S(2)}) collective-permute-start(f32[12,128]{1,0:T(8,128)S(1)} %get-tuple-element.16), channel_id=1, source_target_pairs={{0,1},{1,2},{2,3},{3,0},{4,5},{5,6},{6,7},{7,4},{8,9},{9,10},{10,1... | collective-permute-start | bytes 18440 | tf_op jit(solution)/shard_map/ppermute | solution.py:188
  5.3 4.1 %collective-permute-start.2 = (f32[12,128]{1,0:T(8,128)S(1)}, f32[12,128]{1,0:T(8,128)S(1)}, u32[]{:S(2)}, u32[]{:S(2)}) collective-permute-start(f32[12,128]{1,0:T(8,128)S(1)} %get-tuple-element.16), channel_id=1, source_target_pairs={{0,2},{1,3},{2,0},{3,1},{4,6},{5,7},{6,4},{7,5},{8,10},{9,11},{10,... | collective-permute-start | bytes 18440 | tf_op jit(solution)/shard_map/ppermute | solution.py:188
  9.4 1.5 %collective-permute-start.3 = (bf16[2,128,640]{2,1,0:T(8,128)(2,1)S(1)}, bf16[2,128,640]{2,1,0:T(8,128)(2,1)S(1)}, u32[]{:S(2)}, u32[]{:S(2)}) collective-permute-start(bf16[2,128,640]{2,1,0:T(8,128)(2,1)S(1)} %get-tuple-element.19), channel_id=1, source_target_pairs={{0,4},{4,0},{1,5},{5,1},{2,6},{6,2},{3,7},{7,3},{8,12},{12,8},{9,1... | collective-permute-start | bytes 983048 | tf_op jit(solution)/shard_map/ppermute | solution.py:191
  10.9 0.8 %copy.8 = s32[1,6,5]{2,1,0:T(8,128)S(1)} copy(s32[1,6,5]{1,0,2:T(1,128)} %param.11) | data formatting | bytes 240 | tf_op args[4]
  12.4 0.6 %pad_add_fusion.place_ref.slot_ref = s32[7,5]{1,0:T(8,128)} fusion(s32[1,5]{1,0:T(1,128)S(1)} %compare_select_fusion.1, s32[6,5]{1,0:T(8,128)S(1)} %fusion), kind=kLoop, calls=%fused_computation.3 | loop fusion | flops 35 | bytes 280 | tf_op jit(solution)/shard_map/concatenate | solution.py:196
  13.0 0.0 collective-permute-done.3.rest_0_
  13.0 0.0 copy-start.3
  13.0 0.7 %copy-done.3 = bf16[2,128,640]{2,1,0:T(8,128)(2,1)} copy-done((bf16[2,128,640]{2,1,0:T(8,128)(2,1)}, bf16[2,128,640]{2,1,0:T(8,128)(2,1)S(1)}, u32[]{:S(2)}) %copy-start.3) | copy-done | bytes 327704
  13.7 3.8 %scores.1 = (f32[5,768,896]{2,1,0:T(8,128)S(1)}, bf16[896,640]{1,0:T(8,128)(2,1)S(1)}) custom-call(s32[7,5]{1,0:T(8,128)} %pad_add_fusion.place_ref.slot_ref, s32[1]{0:T(128)S(6)} %copy.9.step_ref, f32[2,640]{1,0:T(2,128)} %gq_ref.1, f32[2,640]{1,0:T(2,128)} %gk_ref.1, bf16[768,640]{1,0:T(8,128)(2,1)} %copy-done, bf16[768,640]{1,0:T(8,128)(2,1)} %copy-done.1, ...), custom_call_target="tpu_custom_call" | custom-call | flops 880803840 | bytes 2949120 | tf_op jit(solution)/shard_map/scores/pallas_call | solution.py:200
  17.5 0.0 collective-permute-done
  17.5 0.0 collective-permute-done.1
  17.5 0.0 collective-permute-done.2
  17.6 0.1 collective-permute-start.4
  17.7 1.1 %collective-permute-done.4.rest_0_ = f32[2,128]{1,0:T(2,128)S(1)} collective-permute-done((f32[2,128]{1,0:T(2,128)S(1)}, f32[2,128]{1,0:T(2,128)S(1)}, u32[]{:S(2)}, u32[]{:S(2)}) %collective-permute-start.4) | collective-permute-done | bytes 1056 | tf_op jit(solution)/shard_map/ppermute | solution.py:217
  18.8 0.0 copy-start.2
  18.8 0.7 %copy-done.2 = s32[7,5]{1,0:T(8,128)S(1)} copy-done((s32[7,5]{1,0:T(8,128)S(1)}, s32[7,5]{1,0:T(8,128)}, u32[]{:S(2)}) %copy-start.2) | copy-done | bytes 164
  19.5 4.5 %attention.1 = bf16[768,640]{1,0:T(8,128)(2,1)} custom-call(s32[7,5]{1,0:T(8,128)S(1)} %copy-done.2, f32[12,128]{1,0:T(8,128)S(1)} %add_add_fusion.sums_ref, f32[5,768,896]{2,1,0:T(8,128)S(1)} %get-tuple-element.25.score_ref, bf16[896,640]{1,0:T(8,128)(2,1)S(1)} %get-tuple-element.26.v_ref, f32[2,128]{1,0:T(2,128)S(1)} %collective-permute-done.4.rest_0_), custom_call_target="tpu_custom_call" | custom-call | flops 629145600 | bytes 983040 | tf_op jit(solution)/shard_map/attention/pallas_call | solution.py:220
  (5 shorter events, 0.0 us)
Async XLA Ops:
  1.9 0.9 %copy-start = (bf16[768,640]{1,0:T(8,128)(2,1)}, bf16[768,640]{1,0:T(8,128)(2,1)S(1)}, u32[]{:S(2)}) copy-start(bf16[768,640]{1,0:T(8,128)(2,1)S(1)} %get-tuple-element.17.q_ref) | copy-start | bytes 2949124
  2.9 0.9 %copy-start.1 = (bf16[768,640]{1,0:T(8,128)(2,1)}, bf16[768,640]{1,0:T(8,128)(2,1)S(1)}, u32[]{:S(2)}) copy-start(bf16[768,640]{1,0:T(8,128)(2,1)S(1)} %get-tuple-element.18.k_ref) | copy-start | bytes 2949124
  3.8 13.7 %collective-permute-start = (f32[12,128]{1,0:T(8,128)S(1)}, f32[12,128]{1,0:T(8,128)S(1)}, u32[]{:S(2)}, u32[]{:S(2)}) collective-permute-start(f32[12,128]{1,0:T(8,128)S(1)} %get-tuple-element.16), channel_id=1, source_target_pairs={{0,3},{1,0},{2,1},{3,2},{4,7},{5,4},{6,5},{7,6},{8,11},{9,8},{10,9... | collective-permute-start | bytes 18440 | tf_op jit(solution)/shard_map/ppermute | solution.py:188
  4.0 13.5 %collective-permute-start.1 = (f32[12,128]{1,0:T(8,128)S(1)}, f32[12,128]{1,0:T(8,128)S(1)}, u32[]{:S(2)}, u32[]{:S(2)}) collective-permute-start(f32[12,128]{1,0:T(8,128)S(1)} %get-tuple-element.16), channel_id=1, source_target_pairs={{0,1},{1,2},{2,3},{3,0},{4,5},{5,6},{6,7},{7,4},{8,9},{9,10},{10,1... | collective-permute-start | bytes 18440 | tf_op jit(solution)/shard_map/ppermute | solution.py:188
  5.3 12.2 %collective-permute-start.2 = (f32[12,128]{1,0:T(8,128)S(1)}, f32[12,128]{1,0:T(8,128)S(1)}, u32[]{:S(2)}, u32[]{:S(2)}) collective-permute-start(f32[12,128]{1,0:T(8,128)S(1)} %get-tuple-element.16), channel_id=1, source_target_pairs={{0,2},{1,3},{2,0},{3,1},{4,6},{5,7},{6,4},{7,5},{8,10},{9,11},{10,... | collective-permute-start | bytes 18440 | tf_op jit(solution)/shard_map/ppermute | solution.py:188
  9.4 3.6 %collective-permute-start.3 = (bf16[2,128,640]{2,1,0:T(8,128)(2,1)S(1)}, bf16[2,128,640]{2,1,0:T(8,128)(2,1)S(1)}, u32[]{:S(2)}, u32[]{:S(2)}) collective-permute-start(bf16[2,128,640]{2,1,0:T(8,128)(2,1)S(1)} %get-tuple-element.19), channel_id=1, source_target_pairs={{0,4},{4,0},{1,5},{5,1},{2,6},{6,2},{3,7},{7,3},{8,12},{12,8},{9,1... | collective-permute-start | bytes 983048 | tf_op jit(solution)/shard_map/ppermute | solution.py:191
  13.0 0.7 %copy-start.3 = (bf16[2,128,640]{2,1,0:T(8,128)(2,1)}, bf16[2,128,640]{2,1,0:T(8,128)(2,1)S(1)}, u32[]{:S(2)}) copy-start(bf16[2,128,640]{2,1,0:T(8,128)(2,1)S(1)} %collective-permute-done.3.rest_0_) | copy-start | bytes 983044
  17.6 1.2 %collective-permute-start.4 = (f32[2,128]{1,0:T(2,128)S(1)}, f32[2,128]{1,0:T(2,128)S(1)}, u32[]{:S(2)}, u32[]{:S(2)}) collective-permute-start(f32[2,128]{1,0:T(2,128)S(1)} %pad_maximum_fusion), channel_id=1, source_target_pairs={{0,4},{4,0},{1,5},{5,1},{2,6},{6,2},{3,7},{7,3},{8,12},{12,8},{9,1... | collective-permute-start | bytes 3080 | tf_op jit(solution)/shard_map/ppermute | solution.py:217
  18.8 0.7 %copy-start.2 = (s32[7,5]{1,0:T(8,128)S(1)}, s32[7,5]{1,0:T(8,128)}, u32[]{:S(2)}) copy-start(s32[7,5]{1,0:T(8,128)} %pad_add_fusion.place_ref.slot_ref) | copy-start | bytes 424

commit v3 on v2

v3 whole, which is shorter than its diff:
```python
import functools

import jax
import jax.numpy as jnp
from jax import lax
from jax.experimental import pallas as pl
from jax.experimental.pallas import tpu as pltpu
from jax.sharding import PartitionSpec as P

DH = 128
TILE = 128
EPSILON = 1e-06
SWITCH_STEP = 875
LOG2E = 1.4426950408889634
MIB = 1 << 20

HBM = pl.BlockSpec(memory_space=pltpu.HBM)
VMEM = pl.BlockSpec(memory_space=pltpu.VMEM)
SMEM = pl.BlockSpec(memory_space=pltpu.SMEM)


def tile_rows(index):
    if isinstance(index, int):
        return pl.ds(index * TILE, TILE)
    return pl.ds(pl.multiple_of(index * TILE, TILE), TILE)


def sums_kernel(chunk, near_hbm, gq_hbm, gk_hbm, q_hbm, k_hbm, v_hbm, sums_ref, gain_ref, slot_ref,
                q_ref, k_ref, *rest):
    *edges, near, gq, gk, sems, edge_sems, small_sems = rest
    rows, width = q_hbm.shape
    tiles, slots = rows // TILE, near_hbm.shape[0]
    place = lax.axis_index("seq")
    copies = []
    for a, (src, dst) in enumerate(((q_hbm, q_ref), (k_hbm, k_ref))):
        for j in range(rows // chunk):
            part = pl.ds(j * chunk, chunk)
            copies.append(pltpu.make_async_copy(src.at[part], dst.at[part], sems.at[a, j]))
            copies[-1].start()
    small = [
        pltpu.make_async_copy(src, dst, small_sems.at[a])
        for a, (src, dst) in enumerate(((near_hbm, near), (gq_hbm, gq), (gk_hbm, gk)))
    ]
    for copy in small:
        copy.start()
    edge_copies = []
    for e, edge in enumerate(edges):
        first = jnp.where(place == 0, tiles - 1, 0) if len(edges) == 1 else (0, tiles - 1)[e]
        for a, src in enumerate((k_hbm, v_hbm)):
            edge_copies.append(pltpu.make_async_copy(src.at[tile_rows(first)], edge.at[a], edge_sems.at[e, a]))
            edge_copies[-1].start()
    diagonal = lax.broadcasted_iota(jnp.int32, (TILE, TILE), 0) == lax.broadcasted_iota(
        jnp.int32, (TILE, TILE), 1
    )
    for a, buf in enumerate((q_ref, k_ref)):
        for t in range(tiles):
            if t * TILE % chunk == 0:
                copies[a * (rows // chunk) + t * TILE // chunk].wait()
            total = 0.0
            for j in range(width // DH):
                x = buf[t * TILE : (t + 1) * TILE, j * DH : (j + 1) * DH].astype(jnp.float32)
                total = total + x * x
            total = jnp.sum(total, axis=1, keepdims=True)
            total = jnp.sum(jnp.where(diagonal, total, 0.0), axis=0, keepdims=True)
            sums_ref[a * tiles + t : a * tiles + t + 1, :] = total
        if a == 0:
            for copy in small:
                copy.wait()
            gain_ref[...] = gq[...] * gk[...] * (DH ** -0.5 * LOG2E)
            for i in range(tiles):
                for n in range(slots):
                    local = near[n, 0, i] - place * tiles
                    local = jnp.where(local < 0, tiles + len(edges) - 1, jnp.minimum(local, tiles))
                    slot_ref[i * slots + n : i * slots + n + 1, :] = jnp.full((1, TILE), local, jnp.int32)
    for copy in edge_copies:
        copy.wait()


def add_kernel(a_ref, b_ref, out_ref):
    out_ref[...] = a_ref[...] + b_ref[...]


def total_kernel(a_ref, b_ref, out_ref, border_ref):
    total = a_ref[...] + b_ref[...]
    out_ref[...] = total
    tiles = total.shape[0] // 2
    border_ref[0:1, :] = total[tiles : tiles + 1]
    border_ref[1:2, :] = total[2 * tiles - 1 : 2 * tiles]


def expert_gain(step_ref, gain_ref):
    return jnp.where(step_ref[...] >= SWITCH_STEP, gain_ref[0:1, :], gain_ref[1:2, :])


def own_scores(gain, q_ref, k_ref, score_ref, at, h):
    cols = slice(h * DH, (h + 1) * DH)
    query = (q_ref[:, cols].astype(jnp.float32) * gain[:, cols]).astype(jnp.bfloat16)
    rows = k_ref.shape[0]
    for j in range(0, rows, 2 * TILE):
        end = min(j + 2 * TILE, rows)
        score_ref[at, :, j:end] = lax.dot_general(
            query, k_ref[j:end, cols], (((1,), (1,)), ((), ())), preferred_element_type=jnp.float32
        )


def first_kernel(step_ref, gain_ref, q_ref, k_ref, score_ref):
    gain = expert_gain(step_ref, gain_ref)
    for h in range(score_ref.shape[0]):
        own_scores(gain, q_ref, k_ref, score_ref, h, h)


def second_kernel(half_ref, step_ref, gain_ref, q_ref, k_ref, v_hbm, *rest):
    del half_ref
    *edges, given_ref, first_ref, score_ref, v_ref, sems = rest
    del given_ref
    rows = q_ref.shape[0]
    copies = [pltpu.make_async_copy(v_hbm, v_ref.at[pl.ds(0, rows)], sems.at[0])]
    for e, edge in enumerate(edges):
        part = pl.ds(rows + e * TILE, TILE)
        copies.append(pltpu.make_async_copy(edge.at[1], v_ref.at[part], sems.at[1 + e]))
    for copy in copies:
        copy.start()
    gain = expert_gain(step_ref, gain_ref)
    done = first_ref.shape[0]
    for h in range(done + score_ref.shape[0]):
        cols = slice(h * DH, (h + 1) * DH)
        out_ref, at = (first_ref, h) if h < done else (score_ref, h - done)
        if h >= done:
            own_scores(gain, q_ref, k_ref, score_ref, at, h)
        query = (q_ref[:, cols].astype(jnp.float32) * gain[:, cols]).astype(jnp.bfloat16)
        for e, edge in enumerate(edges):
            out_ref[at, :, rows + e * TILE : rows + (e + 1) * TILE] = lax.dot_general(
                query, edge[0, :, cols], (((1,), (1,)), ((), ())), preferred_element_type=jnp.float32
            )
    for copy in copies:
        copy.wait()


def attention_kernel(full_width, block, sums_ref, slot_ref, first_ref, second_ref, v_ref, *rest):
    *borders, out_hbm, out_buf, weight_buf, scale_buf, sems = rest
    tiles = sums_ref.shape[0] // 2
    slots = slot_ref.shape[0] // tiles
    done = first_ref.shape[0]
    heads = done + second_ref.shape[0]
    place = lax.axis_index("seq")

    def scale(sums):
        return lax.rsqrt(sums * (1.0 / full_width) + EPSILON)

    q_scale = scale(sums_ref[0:tiles, :])
    q_scale = jnp.concatenate([q_scale, jnp.zeros((8 - tiles % 8, TILE), jnp.float32)], axis=0).T
    k_scale = [sums_ref[tiles + t : tiles + t + 1, :] for t in range(tiles)]
    if len(borders) == 1:
        k_scale.append(jnp.where(place == 0, borders[0][0:1, :], borders[0][1:2, :]))
    else:
        k_scale += [borders[0][0:1, :], borders[1][1:2, :]]
    listed = slot_ref[...]
    scales = jnp.zeros(listed.shape, jnp.float32)
    for t, row in enumerate(k_scale):
        scales = jnp.where(listed == t, scale(row), scales)
    scale_buf[...] = scales
    slot = [[jnp.max(slot_ref[i * slots + n : i * slots + n + 1, :]) for n in range(slots)] for i in range(tiles)]
    ones = jnp.ones((TILE, DH), jnp.bfloat16)
    buffers = weight_buf.shape[0]

    def weights(s, i, h):
        score_ref, at = (first_ref, h) if h < done else (second_ref, h - done)
        for b in range(TILE // block):
            rows = pl.ds(i * TILE + b * block, block)
            score = [
                score_ref[at, rows, tile_rows(slot[i][n])] * scale_buf[i * slots + n : i * slots + n + 1, :]
                for n in range(slots)
            ]
            top = jnp.max(functools.reduce(jnp.maximum, score), axis=1, keepdims=True)
            for n, x in enumerate(score):
                weight_buf[s % buffers, b * block : (b + 1) * block, n * TILE : (n + 1) * TILE] = jnp.exp2(
                    (x - top) * q_scale[b * block : (b + 1) * block, i : i + 1]
                ).astype(jnp.bfloat16)

    def mix(s, i, h):
        cols = slice(h * DH, (h + 1) * DH)
        value = jnp.concatenate(
            [jnp.concatenate([v_ref[tile_rows(slot[i][n]), cols], ones], axis=1) for n in range(slots)],
            axis=0,
        )
        return jnp.dot(weight_buf[s % buffers], value, preferred_element_type=jnp.float32)

    def finish(i, h, mixed):
        rows = pl.ds(i * TILE, TILE)
        out_buf[rows, h * DH : (h + 1) * DH] = (mixed[:, :DH] / mixed[:, DH:]).astype(jnp.bfloat16)
        if h == heads - 1:
            pltpu.make_async_copy(out_buf.at[rows], out_hbm.at[rows], sems.at[i]).start()

    pairs = [(i, h) for i in range(tiles) for h in range(heads)]
    mixed = {}
    for s in range(len(pairs) + 2):
        if s < len(pairs):
            weights(s, *pairs[s])
        if 1 <= s <= len(pairs):
            mixed[s - 1] = mix(s - 1, *pairs[s - 1])
        if s >= 2:
            finish(*pairs[s - 2], mixed.pop(s - 2))
    for i in range(tiles):
        rows = pl.ds(i * TILE, TILE)
        pltpu.make_async_copy(out_buf.at[rows], out_hbm.at[rows], sems.at[i]).wait()


def shards(queries, key_input, value_input, timestep, neighbours, q_gain, k_gain):
    q_rows, k_rows, v_rows = queries[0], key_input[0], value_input[0]
    rows, width = q_rows.shape
    tiles, heads = rows // TILE, width // DH
    slots = neighbours.shape[2]
    groups, devices = lax.axis_size("mp"), lax.axis_size("seq")

    up = [(i, (i + 1) % devices) for i in range(devices)]
    down = [(i, (i - 1) % devices) for i in range(devices)]
    hops = [up] if devices == 2 else [down, up]
    count = len(hops)

    chunk = 2 * TILE if tiles % 2 == 0 else TILE
    bf16, f32 = jnp.bfloat16, jnp.float32
    sums, gain, slot, q_all, k_all, *edges = pl.pallas_call(
        functools.partial(sums_kernel, chunk),
        out_shape=[
            pltpu.VMEM((2 * tiles, TILE), f32),
            pltpu.VMEM((2, width), f32),
            pltpu.VMEM((tiles * slots, TILE), jnp.int32),
            pltpu.VMEM((rows, width), bf16),
            pltpu.VMEM((rows, width), bf16),
        ]
        + [pltpu.VMEM((2, TILE, width), bf16)] * count,
        in_specs=[HBM] * 6,
        out_specs=[VMEM] * (5 + count),
        scratch_shapes=[
            pltpu.SMEM((slots, 1, tiles), jnp.int32),
            pltpu.VMEM((2, width), f32),
            pltpu.VMEM((2, width), f32),
            pltpu.SemaphoreType.DMA((2, rows // chunk)),
            pltpu.SemaphoreType.DMA((count, 2)),
            pltpu.SemaphoreType.DMA((3,)),
        ],
        compiler_params=pltpu.CompilerParams(vmem_limit_bytes=61 * MIB),
        cost_estimate=pl.CostEstimate(flops=4 * rows * width, bytes_accessed=4 * rows * width, transcendentals=0),
        name="sums",
    )(jnp.transpose(neighbours, (2, 0, 1)), q_gain, k_gain, q_rows, k_rows, v_rows)

    small = pltpu.CompilerParams(vmem_limit_bytes=1 * MIB)
    add = pl.pallas_call(
        add_kernel, out_shape=pltpu.VMEM((2 * tiles, TILE), f32), in_specs=[VMEM] * 2, out_specs=VMEM,
        compiler_params=small, name="add",
    )
    received = lax.ppermute(sums, "mp", [(i, i ^ 1) for i in range(groups)])
    edges = [lax.ppermute(edge, "seq", hop) for edge, hop in zip(edges, hops)]

    key_rows = rows + count * TILE
    early = (heads + 1) // 2
    step = timestep.reshape(1, 1)
    first = pl.pallas_call(
        first_kernel,
        out_shape=pltpu.VMEM((early, rows, key_rows), f32),
        in_specs=[VMEM] * 4,
        out_specs=VMEM,
        compiler_params=pltpu.CompilerParams(vmem_limit_bytes=8 * MIB),
        cost_estimate=pl.CostEstimate(flops=2 * rows * rows * early * DH, bytes_accessed=0, transcendentals=0),
        name="first",
    )(step, gain, q_all, k_all)
    received, first = lax.optimization_barrier((received, first))
    half = add(sums, received)
    received = lax.ppermute(half, "mp", [(i, i ^ 2) for i in range(groups)])
    first, second, v_all = pl.pallas_call(
        second_kernel,
        out_shape=[
            pltpu.VMEM((early, rows, key_rows), f32),
            pltpu.VMEM((heads - early, rows, key_rows), f32),
            pltpu.VMEM((key_rows, width), bf16),
        ],
        in_specs=[VMEM] * 5 + [HBM] + [VMEM] * (count + 1),
        out_specs=[VMEM] * 3,
        input_output_aliases={6 + count: 0},
        scratch_shapes=[pltpu.SemaphoreType.DMA((1 + count,))],
        compiler_params=pltpu.CompilerParams(vmem_limit_bytes=8 * MIB),
        cost_estimate=pl.CostEstimate(flops=2 * rows * rows * early * DH, bytes_accessed=0, transcendentals=0),
        name="second",
    )(half, step, gain, q_all, k_all, v_rows, *edges, first)
    received, first, second, v_all = lax.optimization_barrier((received, first, second, v_all))
    total, border = pl.pallas_call(
        total_kernel,
        out_shape=[pltpu.VMEM((2 * tiles, TILE), f32), pltpu.VMEM((2, TILE), f32)],
        in_specs=[VMEM] * 2, out_specs=[VMEM] * 2, compiler_params=small, name="total",
    )(half, received)
    borders = [lax.ppermute(border, "seq", hop) for hop in hops]

    pairs = tiles * slots * TILE * TILE * heads
    mixed = pl.pallas_call(
        functools.partial(attention_kernel, width * groups, 32),
        out_shape=jax.ShapeDtypeStruct((rows, width), bf16),
        in_specs=[VMEM] * (5 + count),
        out_specs=HBM,
        scratch_shapes=[
            pltpu.VMEM((rows, width), bf16),
            pltpu.VMEM((3, TILE, slots * TILE), bf16),
            pltpu.VMEM((tiles * slots, TILE), f32),
            pltpu.SemaphoreType.DMA((tiles,)),
        ],
        compiler_params=pltpu.CompilerParams(vmem_limit_bytes=24 * MIB),
        cost_estimate=pl.CostEstimate(flops=2 * pairs * DH, bytes_accessed=2 * rows * width, transcendentals=pairs),
        name="attention",
    )(total, slot, first, second, v_all, *borders)
    return mixed.reshape(1, rows, width)


def solution(mesh):
    return jax.shard_map(
        shards,
        mesh=mesh,
        in_specs=(
            P("expert", "seq", "mp"),
            P("expert", "seq", "mp"),
            P("expert", "seq", "mp"),
            P("expert"),
            P("expert", "seq", None),
            P(None, "mp"),
            P(None, "mp"),
        ),
        out_specs=P("expert", "seq", "mp"),
        check_vma=False,
    )
```

time: 24.2 us -> 17.8 us (0.74)
  the two profiles are of different devices: /device:TPU:13 before, /device:TPU:0 now
where the time goes in v3:
time: 17.8 us; the launch traced here: 17.7 us
  Pallas kernels  9.67 us (54%)
  starting transfers between devices  6.03 us (34%)
  waiting for transfers between devices  1.26 us (7%)
  between operations  0.7 us (4%)
    pallas_call x1, Pallas kernels, shards(): pl.pallas_call(functools.partial(attention_kernel, width * groups, 32), o...  4.89 us
    ppermute x1, starting transfers between devices, shards(): received = lax.ppermute(half, 'mp', [(i, i ^ 2) for i in range(groups)])  2.86 us
    ppermute x1, starting transfers between devices, shards(): received = lax.ppermute(sums, 'mp', [(i, i ^ 1) for i in range(groups)])  2.65 us
    pallas_call x1, Pallas kernels, shards(): pl.pallas_call(functools.partial(sums_kernel, chunk), out_shape=[pltpu.VM...  2.01 us
    pallas_call x1, Pallas kernels, shards(): pl.pallas_call(second_kernel, out_shape=[pltpu.VMEM((early, rows, key_row...  1.62 us
    ppermute x1, waiting for transfers between devices, shards(): borders = [lax.ppermute(border, 'seq', hop) for hop in hops]  1.14 us
    pallas_call x1, Pallas kernels, shards(): pl.pallas_call(first_kernel, out_shape=pltpu.VMEM((early, rows, key_rows)...  1.13 us
    ppermute x1, starting transfers between devices, shards(): edges = [lax.ppermute(edge, 'seq', hop) for edge, hop in zip(edges, hops)]  0.52 us
  transfers between devices with their start and end apart: 4, of which 2 were waited for; matrix products, arithmetic and copies ran while one was open for 0% of the time, Pallas kernels for 16%

profile of v3, /device:TPU:0, one launch (start us, length us, event | category | flops | bytes accessed | tf_op | source)
XLA Modules:
  0.0 17.7 jit_solution(17034820109345146832)
XLA Ops:
  0.0 2.0 %sums.1 = (f32[12,128]{1,0:T(8,128)S(1)}, f32[2,640]{1,0:T(2,128)S(1)}, s32[30,128]{1,0:T(8,128)S(1)}, bf16[768,640]{1,0:T(8,128)(2,1)S(1)}, bf16[768,640]{1,0:T...) custom-call(s32[5,1,6]{2,1,0:T(1,128)} %bitcast.12, f32[2,640]{1,0:T(2,128)} %gq_hbm.1, f32[2,640]{1,0:T(2,128)} %gk_hbm.1, ...), custom_call_target="tpu_custom_call" | custom-call | flops 1966080 | bytes 1966080 | tf_op jit(solution)/shard_map/sums/pallas_call | solution.py:222
  2.0 0.0 copy-start
  2.0 0.5 %collective-permute-start.2 = (bf16[2,128,640]{2,1,0:T(8,128)(2,1)S(1)}, bf16[2,128,640]{2,1,0:T(8,128)(2,1)S(1)}, u32[]{:S(2)}, u32[]{:S(2)}) collective-permute-start(bf16[2,128,640]{2,1,0:T(8,128)(2,1)S(1)} %get-tuple-element.27), channel_id=1, source_target_pairs={{0,4},{4,0},{1,5},{5,1},{2,6},{6,2},{3,7},{7,3},{8,12},{12,8},{9,1... | collective-permute-start | bytes 983048 | tf_op jit(solution)/shard_map/ppermute | solution.py:253
  2.6 2.6 %collective-permute-start = (f32[12,128]{1,0:T(8,128)S(1)}, f32[12,128]{1,0:T(8,128)S(1)}, u32[]{:S(2)}, u32[]{:S(2)}) collective-permute-start(f32[12,128]{1,0:T(8,128)S(1)} %get-tuple-element.22.a_ref), channel_id=1, source_target_pairs={{0,1},{1,0},{2,3},{3,2},{4,5},{5,4},{6,7},{7,6},{8,9},{9,8},{10,11... | collective-permute-start | bytes 18440 | tf_op jit(solution)/shard_map/ppermute | solution.py:252
  5.9 1.1 %first.1.rest_1_ = f32[3,768,896]{2,1,0:T(8,128)S(1)} custom-call(s32[1,1]{1,0:T(1,128)} %bitcast.6.step_ref, f32[2,640]{1,0:T(2,128)S(1)} %get-tuple-element.23.gain_ref, bf16[768,640]{1,0:T(8,128)(2,1)S(1)} %get-tuple-element.24.q_ref, bf16[768,640]{1,0:T(8,128)(2,1)S(1)} %get-tuple-element.25.k_ref), custom_call_target="tpu_custom_call" | custom-call | flops 452984832 | tf_op jit(solution)/shard_map/first/pallas_call | solution.py:258
  7.0 0.0 collective-permute-done.b_ref
  7.0 2.9 %collective-permute-start.1 = (f32[12,128]{1,0:T(8,128)S(1)}, f32[12,128]{1,0:T(8,128)S(1)}, u32[]{:S(2)}, u32[]{:S(2)}) collective-permute-start(f32[12,128]{1,0:T(8,128)S(1)} %add.1.half_ref.a_ref), channel_id=1, source_target_pairs={{0,2},{1,3},{2,0},{3,1},{4,6},{5,7},{6,4},{7,5},{8,10},{9,11},{10,... | collective-permute-start | bytes 18440 | tf_op jit(solution)/shard_map/ppermute | solution.py:269
  9.9 0.0 collective-permute-done.2.rest_0_
  9.9 0.0 copy-done
  9.9 1.6 %second.1 = (f32[3,768,896]{2,1,0:T(8,128)S(1)}, f32[2,768,896]{2,1,0:T(8,128)S(1)}, bf16[896,640]{1,0:T(8,128)(2,1)S(1)}) custom-call(f32[12,128]{1,0:T(8,128)S(1)} %add.1.half_ref.a_ref, s32[1,1]{1,0:T(1,128)} %bitcast.7.step_ref, f32[2,640]{1,0:T(2,128)S(1)} %get-tuple-element.23.gain_ref, ...), custom_call_target="tpu_custom_call", output_to_operand_aliasing={{0}: (7, {})} | custom-call | flops 452984832 | tf_op jit(solution)/shard_map/second/pallas_call | solution.py:270
  11.5 0.1 collective-permute-done.1.b_ref
  11.6 0.0 collective-permute-start.3
  11.6 1.1 %collective-permute-done.3.rest_0_ = f32[2,128]{1,0:T(2,128)S(1)} collective-permute-done((f32[2,128]{1,0:T(2,128)S(1)}, f32[2,128]{1,0:T(2,128)S(1)}, u32[]{:S(2)}, u32[]{:S(2)}) %collective-permute-start.3) | collective-permute-done | bytes 1056 | tf_op jit(solution)/shard_map/ppermute | solution.py:291
  12.8 4.9 %attention.1 = bf16[768,640]{1,0:T(8,128)(2,1)} custom-call(f32[12,128]{1,0:T(8,128)S(1)} %get-tuple-element.33.sums_ref, s32[30,128]{1,0:T(8,128)S(1)} %get-tuple-element.34.slot_ref, f32[3,768,896]{2,1,0:T(8,128)S(1)} %get-tuple-element.35.first_ref, f32[2,768,896]{2,1,0:T(8,128)S(1)} %get-tuple-element.36.second_ref, ...), custom_call_target="tpu_custom_call" | custom-call | flops 629145600 | bytes 983040 | tf_op jit(solution)/shard_map/attention/pallas_call | solution.py:294
  (2 shorter events, 0.0 us)
Async XLA Ops:
  2.0 7.9 %copy-start = (bf16[1,768,640]{2,1,0:T(8,128)(2,1)S(1)}, bf16[1,768,640]{2,1,0:T(8,128)(2,1)}, u32[]{:S(2)}) copy-start(bf16[1,768,640]{2,1,0:T(8,128)(2,1)} %param.9) | copy-start | bytes 2949124
  2.0 7.8 %collective-permute-start.2 = (bf16[2,128,640]{2,1,0:T(8,128)(2,1)S(1)}, bf16[2,128,640]{2,1,0:T(8,128)(2,1)S(1)}, u32[]{:S(2)}, u32[]{:S(2)}) collective-permute-start(bf16[2,128,640]{2,1,0:T(8,128)(2,1)S(1)} %get-tuple-element.27), channel_id=1, source_target_pairs={{0,4},{4,0},{1,5},{5,1},{2,6},{6,2},{3,7},{7,3},{8,12},{12,8},{9,1... | collective-permute-start | bytes 983048 | tf_op jit(solution)/shard_map/ppermute | solution.py:253
  2.6 4.4 %collective-permute-start = (f32[12,128]{1,0:T(8,128)S(1)}, f32[12,128]{1,0:T(8,128)S(1)}, u32[]{:S(2)}, u32[]{:S(2)}) collective-permute-start(f32[12,128]{1,0:T(8,128)S(1)} %get-tuple-element.22.a_ref), channel_id=1, source_target_pairs={{0,1},{1,0},{2,3},{3,2},{4,5},{5,4},{6,7},{7,6},{8,9},{9,8},{10,11... | collective-permute-start | bytes 18440 | tf_op jit(solution)/shard_map/ppermute | solution.py:252
  7.0 4.6 %collective-permute-start.1 = (f32[12,128]{1,0:T(8,128)S(1)}, f32[12,128]{1,0:T(8,128)S(1)}, u32[]{:S(2)}, u32[]{:S(2)}) collective-permute-start(f32[12,128]{1,0:T(8,128)S(1)} %add.1.half_ref.a_ref), channel_id=1, source_target_pairs={{0,2},{1,3},{2,0},{3,1},{4,6},{5,7},{6,4},{7,5},{8,10},{9,11},{10,... | collective-permute-start | bytes 18440 | tf_op jit(solution)/shard_map/ppermute | solution.py:269
  11.6 1.1 %collective-permute-start.3 = (f32[2,128]{1,0:T(2,128)S(1)}, f32[2,128]{1,0:T(2,128)S(1)}, u32[]{:S(2)}, u32[]{:S(2)}) collective-permute-start(f32[2,128]{1,0:T(2,128)S(1)} %get-tuple-element.38), channel_id=1, source_target_pairs={{0,4},{4,0},{1,5},{5,1},{2,6},{6,2},{3,7},{7,3},{8,12},{12,8},{9,1... | collective-permute-start | bytes 3080 | tf_op jit(solution)/shard_map/ppermute | solution.py:291

commit v4 on v3

--- a/solution.py
+++ b/solution.py
@@ -13,6 +13,7 @@
 SWITCH_STEP = 875
 LOG2E = 1.4426950408889634
 MIB = 1 << 20
+DEPTH = 1
 
 HBM = pl.BlockSpec(memory_space=pltpu.HBM)
 VMEM = pl.BlockSpec(memory_space=pltpu.VMEM)
@@ -137,7 +138,7 @@
 
 
 def attention_kernel(full_width, block, sums_ref, slot_ref, first_ref, second_ref, v_ref, *rest):
-    *borders, out_hbm, out_buf, weight_buf, scale_buf, sems = rest
+    *borders, out_hbm, out_buf, scale_buf, key_buf, sems = rest
     tiles = sums_ref.shape[0] // 2
     slots = slot_ref.shape[0] // tiles
     done = first_ref.shape[0]
@@ -158,32 +159,39 @@
     scales = jnp.zeros(listed.shape, jnp.float32)
     for t, row in enumerate(k_scale):
         scales = jnp.where(listed == t, scale(row), scales)
-    scale_buf[...] = scales
+    key_buf[...] = scales
     slot = [[jnp.max(slot_ref[i * slots + n : i * slots + n + 1, :]) for n in range(slots)] for i in range(tiles)]
     ones = jnp.ones((TILE, DH), jnp.bfloat16)
-    buffers = weight_buf.shape[0]
-
-    def weights(s, i, h):
+
+    def prepare(i):
+        for n in range(slots):
+            scale_buf[i % 2, :, n * TILE : (n + 1) * TILE] = (
+                q_scale[:, i : i + 1] * key_buf[i * slots + n : i * slots + n + 1, :]
+            )
+
+    def weights(i, h):
         score_ref, at = (first_ref, h) if h < done else (second_ref, h - done)
-        for b in range(TILE // block):
-            rows = pl.ds(i * TILE + b * block, block)
+        rows = pl.ds(i * TILE, TILE)
+        if h == 0:
+            prepare(i)
+        parts = []
+        for b in range(0, TILE, block):
             score = [
-                score_ref[at, rows, tile_rows(slot[i][n])] * scale_buf[i * slots + n : i * slots + n + 1, :]
+                score_ref[at, pl.ds(i * TILE + b, block), tile_rows(slot[i][n])]
+                * scale_buf[i % 2, b : b + block, n * TILE : (n + 1) * TILE]
                 for n in range(slots)
             ]
             top = jnp.max(functools.reduce(jnp.maximum, score), axis=1, keepdims=True)
-            for n, x in enumerate(score):
-                weight_buf[s % buffers, b * block : (b + 1) * block, n * TILE : (n + 1) * TILE] = jnp.exp2(
-                    (x - top) * q_scale[b * block : (b + 1) * block, i : i + 1]
-                ).astype(jnp.bfloat16)
-
-    def mix(s, i, h):
+            parts.append(jnp.concatenate([jnp.exp2(x - top).astype(jnp.bfloat16) for x in score], axis=1))
+        return jnp.concatenate(parts, axis=0)
+
+    def mix(i, h, weight):
         cols = slice(h * DH, (h + 1) * DH)
         value = jnp.concatenate(
             [jnp.concatenate([v_ref[tile_rows(slot[i][n]), cols], ones], axis=1) for n in range(slots)],
             axis=0,
         )
-        return jnp.dot(weight_buf[s % buffers], value, preferred_element_type=jnp.float32)
+        return jnp.dot(weight, value, preferred_element_type=jnp.float32)
 
     def finish(i, h, mixed):
         rows = pl.ds(i * TILE, TILE)
@@ -192,14 +200,14 @@
             pltpu.make_async_copy(out_buf.at[rows], out_hbm.at[rows], sems.at[i]).start()
 
     pairs = [(i, h) for i in range(tiles) for h in range(heads)]
-    mixed = {}
-    for s in range(len(pairs) + 2):
+    weight, mixed = {}, {}
+    for s in range(len(pairs) + DEPTH + 1):
         if s < len(pairs):
-            weights(s, *pairs[s])
-        if 1 <= s <= len(pairs):
-            mixed[s - 1] = mix(s - 1, *pairs[s - 1])
-        if s >= 2:
-            finish(*pairs[s - 2], mixed.pop(s - 2))
+            weight[s] = weights(*pairs[s])
+        if DEPTH <= s < len(pairs) + DEPTH:
+            mixed[s - DEPTH] = mix(*pairs[s - DEPTH], weight.pop(s - DEPTH))
+        if s > DEPTH:
+            finish(*pairs[s - DEPTH - 1], mixed.pop(s - DEPTH - 1))
     for i in range(tiles):
         rows = pl.ds(i * TILE, TILE)
         pltpu.make_async_copy(out_buf.at[rows], out_hbm.at[rows], sems.at[i]).wait()
@@ -292,13 +300,13 @@
 
     pairs = tiles * slots * TILE * TILE * heads
     mixed = pl.pallas_call(
-        functools.partial(attention_kernel, width * groups, 32),
+        functools.partial(attention_kernel, width * groups, 128),
         out_shape=jax.ShapeDtypeStruct((rows, width), bf16),
         in_specs=[VMEM] * (5 + count),
         out_specs=HBM,
         scratch_shapes=[
             pltpu.VMEM((rows, width), bf16),
-            pltpu.VMEM((3, TILE, slots * TILE), bf16),
+            pltpu.VMEM((2, TILE, slots * TILE), f32),
             pltpu.VMEM((tiles * slots, TILE), f32),
             pltpu.SemaphoreType.DMA((tiles,)),
         ],

time: 17.8 us -> 17.2 us (0.966)
  Pallas kernels: 9.67 us -> 9.04 us
    pallas_call x1, Pallas kernels: 4.89 us -> 4.26 us  [shards(): pl.pallas_call(functools.partial(attention_kernel, width * groups, 128),...]
where the time goes in v4:
time: 17.2 us; the launch traced here: 17 us
  Pallas kernels  9.04 us (53%)
  starting transfers between devices  6.03 us (35%)
  waiting for transfers between devices  1.26 us (7%)
  between operations  0.7 us (4%)
    pallas_call x1, Pallas kernels, shards(): pl.pallas_call(functools.partial(attention_kernel, width * groups, 128),...  4.26 us
    ppermute x1, starting transfers between devices, shards(): received = lax.ppermute(half, 'mp', [(i, i ^ 2) for i in range(groups)])  2.86 us
    ppermute x1, starting transfers between devices, shards(): received = lax.ppermute(sums, 'mp', [(i, i ^ 1) for i in range(groups)])  2.65 us
    pallas_call x1, Pallas kernels, shards(): pl.pallas_call(functools.partial(sums_kernel, chunk), out_shape=[pltpu.VM...  2.01 us
    pallas_call x1, Pallas kernels, shards(): pl.pallas_call(second_kernel, out_shape=[pltpu.VMEM((early, rows, key_row...  1.62 us
    ppermute x1, waiting for transfers between devices, shards(): borders = [lax.ppermute(border, 'seq', hop) for hop in hops]  1.14 us
    pallas_call x1, Pallas kernels, shards(): pl.pallas_call(first_kernel, out_shape=pltpu.VMEM((early, rows, key_rows)...  1.13 us
    ppermute x1, starting transfers between devices, shards(): edges = [lax.ppermute(edge, 'seq', hop) for edge, hop in zip(edges, hops)]  0.52 us
  transfers between devices with their start and end apart: 4, of which 2 were waited for; matrix products, arithmetic and copies ran while one was open for 0% of the time, Pallas kernels for 16%

profile of v4, /device:TPU:0, one launch (start us, length us, event | category | flops | bytes accessed | tf_op | source)
XLA Modules:
  0.0 17.0 jit_solution(11865506732864582118)
XLA Ops:
  0.0 2.0 %sums.1 = (f32[12,128]{1,0:T(8,128)S(1)}, f32[2,640]{1,0:T(2,128)S(1)}, s32[30,128]{1,0:T(8,128)S(1)}, bf16[768,640]{1,0:T(8,128)(2,1)S(1)}, bf16[768,640]{1,0:T...) custom-call(s32[5,1,6]{2,1,0:T(1,128)} %bitcast.12, f32[2,640]{1,0:T(2,128)} %gq_hbm.1, f32[2,640]{1,0:T(2,128)} %gk_hbm.1, ...), custom_call_target="tpu_custom_call" | custom-call | flops 1966080 | bytes 1966080 | tf_op jit(solution)/shard_map/sums/pallas_call | solution.py:230
  2.0 0.0 copy-start
  2.0 0.5 %collective-permute-start.2 = (bf16[2,128,640]{2,1,0:T(8,128)(2,1)S(1)}, bf16[2,128,640]{2,1,0:T(8,128)(2,1)S(1)}, u32[]{:S(2)}, u32[]{:S(2)}) collective-permute-start(bf16[2,128,640]{2,1,0:T(8,128)(2,1)S(1)} %get-tuple-element.27), channel_id=1, source_target_pairs={{0,4},{4,0},{1,5},{5,1},{2,6},{6,2},{3,7},{7,3},{8,12},{12,8},{9,1... | collective-permute-start | bytes 983048 | tf_op jit(solution)/shard_map/ppermute | solution.py:261
  2.6 2.6 %collective-permute-start = (f32[12,128]{1,0:T(8,128)S(1)}, f32[12,128]{1,0:T(8,128)S(1)}, u32[]{:S(2)}, u32[]{:S(2)}) collective-permute-start(f32[12,128]{1,0:T(8,128)S(1)} %get-tuple-element.22.a_ref), channel_id=1, source_target_pairs={{0,1},{1,0},{2,3},{3,2},{4,5},{5,4},{6,7},{7,6},{8,9},{9,8},{10,11... | collective-permute-start | bytes 18440 | tf_op jit(solution)/shard_map/ppermute | solution.py:260
  5.9 1.1 %first.1.rest_1_ = f32[3,768,896]{2,1,0:T(8,128)S(1)} custom-call(s32[1,1]{1,0:T(1,128)} %bitcast.6.step_ref, f32[2,640]{1,0:T(2,128)S(1)} %get-tuple-element.23.gain_ref, bf16[768,640]{1,0:T(8,128)(2,1)S(1)} %get-tuple-element.24.q_ref, bf16[768,640]{1,0:T(8,128)(2,1)S(1)} %get-tuple-element.25.k_ref), custom_call_target="tpu_custom_call" | custom-call | flops 452984832 | tf_op jit(solution)/shard_map/first/pallas_call | solution.py:266
  7.0 0.0 collective-permute-done.b_ref
  7.0 2.9 %collective-permute-start.1 = (f32[12,128]{1,0:T(8,128)S(1)}, f32[12,128]{1,0:T(8,128)S(1)}, u32[]{:S(2)}, u32[]{:S(2)}) collective-permute-start(f32[12,128]{1,0:T(8,128)S(1)} %add.1.half_ref.a_ref), channel_id=1, source_target_pairs={{0,2},{1,3},{2,0},{3,1},{4,6},{5,7},{6,4},{7,5},{8,10},{9,11},{10,... | collective-permute-start | bytes 18440 | tf_op jit(solution)/shard_map/ppermute | solution.py:277
  9.9 0.0 collective-permute-done.2.rest_0_
  9.9 0.0 copy-done
  9.9 1.6 %second.1 = (f32[3,768,896]{2,1,0:T(8,128)S(1)}, f32[2,768,896]{2,1,0:T(8,128)S(1)}, bf16[896,640]{1,0:T(8,128)(2,1)S(1)}) custom-call(f32[12,128]{1,0:T(8,128)S(1)} %add.1.half_ref.a_ref, s32[1,1]{1,0:T(1,128)} %bitcast.7.step_ref, f32[2,640]{1,0:T(2,128)S(1)} %get-tuple-element.23.gain_ref, ...), custom_call_target="tpu_custom_call", output_to_operand_aliasing={{0}: (7, {})} | custom-call | flops 452984832 | tf_op jit(solution)/shard_map/second/pallas_call | solution.py:278
  11.5 0.1 collective-permute-done.1.b_ref
  11.6 0.0 collective-permute-start.3
  11.6 1.1 %collective-permute-done.3.rest_0_ = f32[2,128]{1,0:T(2,128)S(1)} collective-permute-done((f32[2,128]{1,0:T(2,128)S(1)}, f32[2,128]{1,0:T(2,128)S(1)}, u32[]{:S(2)}, u32[]{:S(2)}) %collective-permute-start.3) | collective-permute-done | bytes 1056 | tf_op jit(solution)/shard_map/ppermute | solution.py:299
  12.8 4.3 %attention.1 = bf16[768,640]{1,0:T(8,128)(2,1)} custom-call(f32[12,128]{1,0:T(8,128)S(1)} %get-tuple-element.33.sums_ref, s32[30,128]{1,0:T(8,128)S(1)} %get-tuple-element.34.slot_ref, f32[3,768,896]{2,1,0:T(8,128)S(1)} %get-tuple-element.35.first_ref, f32[2,768,896]{2,1,0:T(8,128)S(1)} %get-tuple-element.36.second_ref, ...), custom_call_target="tpu_custom_call" | custom-call | flops 629145600 | bytes 983040 | tf_op jit(solution)/shard_map/attention/pallas_call | solution.py:302
  (2 shorter events, 0.0 us)
Async XLA Ops:
  2.0 7.9 %copy-start = (bf16[1,768,640]{2,1,0:T(8,128)(2,1)S(1)}, bf16[1,768,640]{2,1,0:T(8,128)(2,1)}, u32[]{:S(2)}) copy-start(bf16[1,768,640]{2,1,0:T(8,128)(2,1)} %param.9) | copy-start | bytes 2949124
  2.0 7.8 %collective-permute-start.2 = (bf16[2,128,640]{2,1,0:T(8,128)(2,1)S(1)}, bf16[2,128,640]{2,1,0:T(8,128)(2,1)S(1)}, u32[]{:S(2)}, u32[]{:S(2)}) collective-permute-start(bf16[2,128,640]{2,1,0:T(8,128)(2,1)S(1)} %get-tuple-element.27), channel_id=1, source_target_pairs={{0,4},{4,0},{1,5},{5,1},{2,6},{6,2},{3,7},{7,3},{8,12},{12,8},{9,1... | collective-permute-start | bytes 983048 | tf_op jit(solution)/shard_map/ppermute | solution.py:261
  2.6 4.4 %collective-permute-start = (f32[12,128]{1,0:T(8,128)S(1)}, f32[12,128]{1,0:T(8,128)S(1)}, u32[]{:S(2)}, u32[]{:S(2)}) collective-permute-start(f32[12,128]{1,0:T(8,128)S(1)} %get-tuple-element.22.a_ref), channel_id=1, source_target_pairs={{0,1},{1,0},{2,3},{3,2},{4,5},{5,4},{6,7},{7,6},{8,9},{9,8},{10,11... | collective-permute-start | bytes 18440 | tf_op jit(solution)/shard_map/ppermute | solution.py:260
  7.0 4.6 %collective-permute-start.1 = (f32[12,128]{1,0:T(8,128)S(1)}, f32[12,128]{1,0:T(8,128)S(1)}, u32[]{:S(2)}, u32[]{:S(2)}) collective-permute-start(f32[12,128]{1,0:T(8,128)S(1)} %add.1.half_ref.a_ref), channel_id=1, source_target_pairs={{0,2},{1,3},{2,0},{3,1},{4,6},{5,7},{6,4},{7,5},{8,10},{9,11},{10,... | collective-permute-start | bytes 18440 | tf_op jit(solution)/shard_map/ppermute | solution.py:277
  11.6 1.1 %collective-permute-start.3 = (f32[2,128]{1,0:T(2,128)S(1)}, f32[2,128]{1,0:T(2,128)S(1)}, u32[]{:S(2)}, u32[]{:S(2)}) collective-permute-start(f32[2,128]{1,0:T(2,128)S(1)} %get-tuple-element.38), channel_id=1, source_target_pairs={{0,4},{4,0},{1,5},{5,1},{2,6},{6,2},{3,7},{7,3},{8,12},{12,8},{9,1... | collective-permute-start | bytes 3080 | tf_op jit(solution)/shard_map/ppermute | solution.py:299

commit v5 on v4

--- a/solution.py
+++ b/solution.py
@@ -77,16 +77,12 @@
         copy.wait()
 
 
-def add_kernel(a_ref, b_ref, out_ref):
-    out_ref[...] = a_ref[...] + b_ref[...]
-
-
-def total_kernel(a_ref, b_ref, out_ref, border_ref):
-    total = a_ref[...] + b_ref[...]
-    out_ref[...] = total
-    tiles = total.shape[0] // 2
-    border_ref[0:1, :] = total[tiles : tiles + 1]
-    border_ref[1:2, :] = total[2 * tiles - 1 : 2 * tiles]
+def half_kernel(a_ref, b_ref, out_ref, border_ref):
+    half = a_ref[...] + b_ref[...]
+    out_ref[...] = half
+    tiles = half.shape[0] // 2
+    border_ref[0:1, :] = half[tiles : tiles + 1]
+    border_ref[1:2, :] = half[2 * tiles - 1 : 2 * tiles]
 
 
 def expert_gain(step_ref, gain_ref):
@@ -137,9 +133,11 @@
         copy.wait()
 
 
-def attention_kernel(full_width, block, sums_ref, slot_ref, first_ref, second_ref, v_ref, *rest):
+def attention_kernel(full_width, block, half_ref, other_ref, slot_ref, first_ref, second_ref, v_ref, *rest):
     *borders, out_hbm, out_buf, scale_buf, key_buf, sems = rest
-    tiles = sums_ref.shape[0] // 2
+    borders = [a[...] + b[...] for a, b in zip(borders[: len(borders) // 2], borders[len(borders) // 2 :])]
+    sums = half_ref[...] + other_ref[...]
+    tiles = sums.shape[0] // 2
     slots = slot_ref.shape[0] // tiles
     done = first_ref.shape[0]
     heads = done + second_ref.shape[0]
@@ -148,9 +146,9 @@
     def scale(sums):
         return lax.rsqrt(sums * (1.0 / full_width) + EPSILON)
 
-    q_scale = scale(sums_ref[0:tiles, :])
+    q_scale = scale(sums[0:tiles, :])
     q_scale = jnp.concatenate([q_scale, jnp.zeros((8 - tiles % 8, TILE), jnp.float32)], axis=0).T
-    k_scale = [sums_ref[tiles + t : tiles + t + 1, :] for t in range(tiles)]
+    k_scale = [sums[tiles + t : tiles + t + 1, :] for t in range(tiles)]
     if len(borders) == 1:
         k_scale.append(jnp.where(place == 0, borders[0][0:1, :], borders[0][1:2, :]))
     else:
@@ -253,10 +251,6 @@
     )(jnp.transpose(neighbours, (2, 0, 1)), q_gain, k_gain, q_rows, k_rows, v_rows)
 
     small = pltpu.CompilerParams(vmem_limit_bytes=1 * MIB)
-    add = pl.pallas_call(
-        add_kernel, out_shape=pltpu.VMEM((2 * tiles, TILE), f32), in_specs=[VMEM] * 2, out_specs=VMEM,
-        compiler_params=small, name="add",
-    )
     received = lax.ppermute(sums, "mp", [(i, i ^ 1) for i in range(groups)])
     edges = [lax.ppermute(edge, "seq", hop) for edge, hop in zip(edges, hops)]
 
@@ -273,8 +267,20 @@
         name="first",
     )(step, gain, q_all, k_all)
     received, first = lax.optimization_barrier((received, first))
-    half = add(sums, received)
+    half, border = pl.pallas_call(
+        half_kernel,
+        out_shape=[pltpu.VMEM((2 * tiles, TILE), f32), pltpu.VMEM((2, TILE), f32)],
+        in_specs=[VMEM] * 2, out_specs=[VMEM] * 2, compiler_params=small, name="half",
+    )(sums, received)
     received = lax.ppermute(half, "mp", [(i, i ^ 2) for i in range(groups)])
+    across = [
+        lax.ppermute(
+            border, ("seq", "mp"),
+            [(a * groups + i, b * groups + (i ^ 2)) for a, b in hop for i in range(groups)],
+        )
+        for hop in hops
+    ]
+    beside = [lax.ppermute(border, "seq", hop) for hop in hops]
     first, second, v_all = pl.pallas_call(
         second_kernel,
         out_shape=[
@@ -290,19 +296,15 @@
         cost_estimate=pl.CostEstimate(flops=2 * rows * rows * early * DH, bytes_accessed=0, transcendentals=0),
         name="second",
     )(half, step, gain, q_all, k_all, v_rows, *edges, first)
-    received, first, second, v_all = lax.optimization_barrier((received, first, second, v_all))
-    total, border = pl.pallas_call(
-        total_kernel,
-        out_shape=[pltpu.VMEM((2 * tiles, TILE), f32), pltpu.VMEM((2, TILE), f32)],
-        in_specs=[VMEM] * 2, out_specs=[VMEM] * 2, compiler_params=small, name="total",
-    )(half, received)
-    borders = [lax.ppermute(border, "seq", hop) for hop in hops]
+    received, across, beside, first, second, v_all = lax.optimization_barrier(
+        (received, across, beside, first, second, v_all)
+    )
 
     pairs = tiles * slots * TILE * TILE * heads
     mixed = pl.pallas_call(
         functools.partial(attention_kernel, width * groups, 128),
         out_shape=jax.ShapeDtypeStruct((rows, width), bf16),
-        in_specs=[VMEM] * (5 + count),
+        in_specs=[VMEM] * (6 + 2 * count),
         out_specs=HBM,
         scratch_shapes=[
             pltpu.VMEM((rows, width), bf16),
@@ -313,7 +315,7 @@
         compiler_params=pltpu.CompilerParams(vmem_limit_bytes=24 * MIB),
         cost_estimate=pl.CostEstimate(flops=2 * pairs * DH, bytes_accessed=2 * rows * width, transcendentals=pairs),
         name="attention",
-    )(total, slot, first, second, v_all, *borders)
+    )(half, received, slot, first, second, v_all, *across, *beside)
     return mixed.reshape(1, rows, width)
 
 

time: 17.2 us -> 18.9 us (1.099)
  waiting for transfers between devices: 1.26 us -> 2.78 us
  starting transfers between devices: 6.03 us -> 6.27 us
    ppermute x1 -> x2, starting transfers between devices: 0.01 us -> 2.97 us  [the longest x1 2.43 us: shards(): lax.ppermute(border, ('seq', 'mp'), [(a * groups + i, b * groups + (i ^ 2...]
    ppermute x1, starting transfers between devices: 2.86 us -> 0.13 us  [shards(): received = lax.ppermute(half, 'mp', [(i, i ^ 2) for i in range(groups)])]
    ppermute x1, waiting for transfers between devices: 0.12 us -> 2.77 us  [shards(): received = lax.ppermute(half, 'mp', [(i, i ^ 2) for i in range(groups)])]
    ppermute x1 -> x2, waiting for transfers between devices: 1.14 us -> 0.01 us  [the longest x1 0.01 us: shards(): lax.ppermute(border, ('seq', 'mp'), [(a * groups + i, b * groups + (i ^ 2...]
  transfers between devices with their start and end apart: 4 -> 5, of which waited for: 2 -> 1; matrix products, arithmetic and copies ran while one was open for 0% -> 0% of each run, Pallas kernels for 16% -> 15%
where the time goes in v5:
time: 18.9 us; the launch traced here: 18.8 us
  Pallas kernels  9.03 us (48%)
  starting transfers between devices  6.27 us (33%)
  waiting for transfers between devices  2.78 us (15%)
  between operations  0.71 us (4%)
    pallas_call x1, Pallas kernels, shards(): pl.pallas_call(functools.partial(attention_kernel, width * groups, 128),...  4.25 us
    ppermute x1, waiting for transfers between devices, shards(): received = lax.ppermute(half, 'mp', [(i, i ^ 2) for i in range(groups)])  2.77 us
    ppermute x1, starting transfers between devices, shards(): received = lax.ppermute(sums, 'mp', [(i, i ^ 1) for i in range(groups)])  2.65 us
    ppermute x1, starting transfers between devices, shards(): lax.ppermute(border, ('seq', 'mp'), [(a * groups + i, b * groups + (i ^ 2...  2.43 us
    pallas_call x1, Pallas kernels, shards(): pl.pallas_call(functools.partial(sums_kernel, chunk), out_shape=[pltpu.VM...  2.01 us
    pallas_call x1, Pallas kernels, shards(): pl.pallas_call(second_kernel, out_shape=[pltpu.VMEM((early, rows, key_row...  1.62 us
    pallas_call x1, Pallas kernels, shards(): pl.pallas_call(first_kernel, out_shape=pltpu.VMEM((early, rows, key_rows)...  1.13 us
    ppermute x1, starting transfers between devices, shards(): beside = [lax.ppermute(border, 'seq', hop) for hop in hops]  0.55 us
  transfers between devices with their start and end apart: 5, of which 1 were waited for; matrix products, arithmetic and copies ran while one was open for 0% of the time, Pallas kernels for 15%

profile of v5, /device:TPU:0, one launch (start us, length us, event | category | flops | bytes accessed | tf_op | source)
XLA Modules:
  0.0 18.8 jit_solution(11525672348040519805)
XLA Ops:
  0.0 2.0 %sums.1 = (f32[12,128]{1,0:T(8,128)S(1)}, f32[2,640]{1,0:T(2,128)S(1)}, s32[30,128]{1,0:T(8,128)S(1)}, bf16[768,640]{1,0:T(8,128)(2,1)S(1)}, bf16[768,640]{1,0:T...) custom-call(s32[5,1,6]{2,1,0:T(1,128)} %bitcast.12, f32[2,640]{1,0:T(2,128)} %gq_hbm.1, f32[2,640]{1,0:T(2,128)} %gk_hbm.1, ...), custom_call_target="tpu_custom_call" | custom-call | flops 1966080 | bytes 1966080 | tf_op jit(solution)/shard_map/sums/pallas_call | solution.py:228
  2.0 0.0 copy-start
  2.0 0.5 %collective-permute-start.4 = (bf16[2,128,640]{2,1,0:T(8,128)(2,1)S(1)}, bf16[2,128,640]{2,1,0:T(8,128)(2,1)S(1)}, u32[]{:S(2)}, u32[]{:S(2)}) collective-permute-start(bf16[2,128,640]{2,1,0:T(8,128)(2,1)S(1)} %get-tuple-element.31), channel_id=1, source_target_pairs={{0,4},{4,0},{1,5},{5,1},{2,6},{6,2},{3,7},{7,3},{8,12},{12,8},{9,1... | collective-permute-start | bytes 983048 | tf_op jit(solution)/shard_map/ppermute | solution.py:255
  2.6 2.6 %collective-permute-start = (f32[12,128]{1,0:T(8,128)S(1)}, f32[12,128]{1,0:T(8,128)S(1)}, u32[]{:S(2)}, u32[]{:S(2)}) collective-permute-start(f32[12,128]{1,0:T(8,128)S(1)} %get-tuple-element.24.a_ref), channel_id=1, source_target_pairs={{0,1},{1,0},{2,3},{3,2},{4,5},{5,4},{6,7},{7,6},{8,9},{9,8},{10,11... | collective-permute-start | bytes 18440 | tf_op jit(solution)/shard_map/ppermute | solution.py:254
  5.9 1.1 %first.1.rest_1_ = f32[3,768,896]{2,1,0:T(8,128)S(1)} custom-call(s32[1,1]{1,0:T(1,128)} %bitcast.6.step_ref, f32[2,640]{1,0:T(2,128)S(1)} %get-tuple-element.25.gain_ref, bf16[768,640]{1,0:T(8,128)(2,1)S(1)} %get-tuple-element.26.q_ref, bf16[768,640]{1,0:T(8,128)(2,1)S(1)} %get-tuple-element.27.k_ref), custom_call_target="tpu_custom_call" | custom-call | flops 452984832 | tf_op jit(solution)/shard_map/first/pallas_call | solution.py:260
  7.0 0.0 collective-permute-done.b_ref
  7.0 2.4 %collective-permute-start.2 = (f32[2,128]{1,0:T(2,128)S(1)}, f32[2,128]{1,0:T(2,128)S(1)}, u32[]{:S(2)}, u32[]{:S(2)}) collective-permute-start(f32[2,128]{1,0:T(2,128)S(1)} %get-tuple-element.30), channel_id=1, source_target_pairs={{0,6},{1,7},{2,4},{3,5},{4,2},{5,3},{6,0},{7,1},{8,14},{9,15},{10,... | collective-permute-start | bytes 3080 | tf_op jit(solution)/shard_map/ppermute | solution.py:277
  9.4 0.5 %collective-permute-start.3 = (f32[2,128]{1,0:T(2,128)S(1)}, f32[2,128]{1,0:T(2,128)S(1)}, u32[]{:S(2)}, u32[]{:S(2)}) collective-permute-start(f32[2,128]{1,0:T(2,128)S(1)} %get-tuple-element.30), channel_id=1, source_target_pairs={{0,4},{4,0},{1,5},{5,1},{2,6},{6,2},{3,7},{7,3},{8,12},{12,8},{9,1... | collective-permute-start | bytes 3080 | tf_op jit(solution)/shard_map/ppermute | solution.py:283
  10.0 0.1 collective-permute-start.1
  10.1 0.0 collective-permute-done.4.rest_0_
  10.1 0.0 copy-done
  10.1 1.6 %second.1 = (f32[3,768,896]{2,1,0:T(8,128)S(1)}, f32[2,768,896]{2,1,0:T(8,128)S(1)}, bf16[896,640]{1,0:T(8,128)(2,1)S(1)}) custom-call(f32[12,128]{1,0:T(8,128)S(1)} %get-tuple-element.29.half_ref, s32[1,1]{1,0:T(1,128)} %bitcast.7.step_ref, f32[2,640]{1,0:T(2,128)S(1)} %get-tuple-element.25.gain_ref, ...), custom_call_target="tpu_custom_call", output_to_operand_aliasing={{0}: (7, {})} | custom-call | flops 452984832 | tf_op jit(solution)/shard_map/second/pallas_call | solution.py:284
  11.8 0.0 collective-permute-done.2.rest_0_
  11.8 0.0 collective-permute-done.3.rest_1_
  11.8 2.8 %collective-permute-done.1.other_ref = f32[12,128]{1,0:T(8,128)S(1)} collective-permute-done((f32[12,128]{1,0:T(8,128)S(1)}, f32[12,128]{1,0:T(8,128)S(1)}, u32[]{:S(2)}, u32[]{:S(2)}) %collective-permute-start.1) | collective-permute-done | bytes 6176 | tf_op jit(solution)/shard_map/ppermute | solution.py:275
  14.5 4.3 %attention.1 = bf16[768,640]{1,0:T(8,128)(2,1)} custom-call(f32[12,128]{1,0:T(8,128)S(1)} %get-tuple-element.29.half_ref, f32[12,128]{1,0:T(8,128)S(1)} %collective-permute-done.1.other_ref, s32[30,128]{1,0:T(8,128)S(1)} %get-tuple-element.37.slot_ref, f32[3,768,896]{2,1,0:T(8,128)S(1)} %get-tuple-element.38.first_ref, ...), custom_call_target="tpu_custom_call" | custom-call | flops 629145600 | bytes 983040 | tf_op jit(solution)/shard_map/attention/pallas_call | solution.py:304
  (1 shorter events, 0.0 us)
Async XLA Ops:
  2.0 8.1 %copy-start = (bf16[1,768,640]{2,1,0:T(8,128)(2,1)S(1)}, bf16[1,768,640]{2,1,0:T(8,128)(2,1)}, u32[]{:S(2)}) copy-start(bf16[1,768,640]{2,1,0:T(8,128)(2,1)} %param.9) | copy-start | bytes 2949124
  2.0 8.1 %collective-permute-start.4 = (bf16[2,128,640]{2,1,0:T(8,128)(2,1)S(1)}, bf16[2,128,640]{2,1,0:T(8,128)(2,1)S(1)}, u32[]{:S(2)}, u32[]{:S(2)}) collective-permute-start(bf16[2,128,640]{2,1,0:T(8,128)(2,1)S(1)} %get-tuple-element.31), channel_id=1, source_target_pairs={{0,4},{4,0},{1,5},{5,1},{2,6},{6,2},{3,7},{7,3},{8,12},{12,8},{9,1... | collective-permute-start | bytes 983048 | tf_op jit(solution)/shard_map/ppermute | solution.py:255
  2.6 4.4 %collective-permute-start = (f32[12,128]{1,0:T(8,128)S(1)}, f32[12,128]{1,0:T(8,128)S(1)}, u32[]{:S(2)}, u32[]{:S(2)}) collective-permute-start(f32[12,128]{1,0:T(8,128)S(1)} %get-tuple-element.24.a_ref), channel_id=1, source_target_pairs={{0,1},{1,0},{2,3},{3,2},{4,5},{5,4},{6,7},{7,6},{8,9},{9,8},{10,11... | collective-permute-start | bytes 18440 | tf_op jit(solution)/shard_map/ppermute | solution.py:254
  7.0 4.7 %collective-permute-start.2 = (f32[2,128]{1,0:T(2,128)S(1)}, f32[2,128]{1,0:T(2,128)S(1)}, u32[]{:S(2)}, u32[]{:S(2)}) collective-permute-start(f32[2,128]{1,0:T(2,128)S(1)} %get-tuple-element.30), channel_id=1, source_target_pairs={{0,6},{1,7},{2,4},{3,5},{4,2},{5,3},{6,0},{7,1},{8,14},{9,15},{10,... | collective-permute-start | bytes 3080 | tf_op jit(solution)/shard_map/ppermute | solution.py:277
  9.4 2.3 %collective-permute-start.3 = (f32[2,128]{1,0:T(2,128)S(1)}, f32[2,128]{1,0:T(2,128)S(1)}, u32[]{:S(2)}, u32[]{:S(2)}) collective-permute-start(f32[2,128]{1,0:T(2,128)S(1)} %get-tuple-element.30), channel_id=1, source_target_pairs={{0,4},{4,0},{1,5},{5,1},{2,6},{6,2},{3,7},{7,3},{8,12},{12,8},{9,1... | collective-permute-start | bytes 3080 | tf_op jit(solution)/shard_map/ppermute | solution.py:283
  10.0 4.6 %collective-permute-start.1 = (f32[12,128]{1,0:T(8,128)S(1)}, f32[12,128]{1,0:T(8,128)S(1)}, u32[]{:S(2)}, u32[]{:S(2)}) collective-permute-start(f32[12,128]{1,0:T(8,128)S(1)} %get-tuple-element.29.half_ref), channel_id=1, source_target_pairs={{0,2},{1,3},{2,0},{3,1},{4,6},{5,7},{6,4},{7,5},{8,10},{9,11},{10,... | collective-permute-start | bytes 18440 | tf_op jit(solution)/shard_map/ppermute | solution.py:275

commit v6 on v4

--- a/solution.py
+++ b/solution.py
@@ -137,53 +137,46 @@
         copy.wait()
 
 
-def attention_kernel(full_width, block, sums_ref, slot_ref, first_ref, second_ref, v_ref, *rest):
-    *borders, out_hbm, out_buf, scale_buf, key_buf, sems = rest
+def scale_kernel(full_width, first_tile, sums_ref, *rest):
+    *borders, _, _, first_ref, second_ref = rest
     tiles = sums_ref.shape[0] // 2
+
+    def scale(sums):
+        return lax.rsqrt(sums * (1.0 / full_width) + EPSILON)
+
+    if not borders:
+        k_scale = [scale(sums_ref[tiles + t : tiles + t + 1, :]) for t in range(tiles)]
+    elif len(borders) == 1:
+        place = lax.axis_index("seq")
+        k_scale = [scale(jnp.where(place == 0, borders[0][0:1, :], borders[0][1:2, :]))]
+    else:
+        k_scale = [scale(borders[0][0:1, :]), scale(borders[1][1:2, :])]
+    q_scale = scale(sums_ref[0:tiles, :])
+    q_scale = jnp.concatenate([q_scale, jnp.zeros((8 - tiles % 8, TILE), jnp.float32)], axis=0).T
+    for i in range(tiles):
+        column = jnp.broadcast_to(q_scale[:, i : i + 1], (TILE, TILE))
+        rows = slice(i * TILE, (i + 1) * TILE)
+        for t, row in enumerate(k_scale):
+            both = column * row
+            cols = slice((first_tile + t) * TILE, (first_tile + t + 1) * TILE)
+            for ref in (first_ref, second_ref):
+                for h in range(ref.shape[0]):
+                    ref[h, rows, cols] = ref[h, rows, cols] * both
+
+
+def attention_kernel(tiles, slot_ref, first_ref, second_ref, v_ref, out_hbm, out_buf, sems):
     slots = slot_ref.shape[0] // tiles
     done = first_ref.shape[0]
     heads = done + second_ref.shape[0]
-    place = lax.axis_index("seq")
-
-    def scale(sums):
-        return lax.rsqrt(sums * (1.0 / full_width) + EPSILON)
-
-    q_scale = scale(sums_ref[0:tiles, :])
-    q_scale = jnp.concatenate([q_scale, jnp.zeros((8 - tiles % 8, TILE), jnp.float32)], axis=0).T
-    k_scale = [sums_ref[tiles + t : tiles + t + 1, :] for t in range(tiles)]
-    if len(borders) == 1:
-        k_scale.append(jnp.where(place == 0, borders[0][0:1, :], borders[0][1:2, :]))
-    else:
-        k_scale += [borders[0][0:1, :], borders[1][1:2, :]]
-    listed = slot_ref[...]
-    scales = jnp.zeros(listed.shape, jnp.float32)
-    for t, row in enumerate(k_scale):
-        scales = jnp.where(listed == t, scale(row), scales)
-    key_buf[...] = scales
     slot = [[jnp.max(slot_ref[i * slots + n : i * slots + n + 1, :]) for n in range(slots)] for i in range(tiles)]
     ones = jnp.ones((TILE, DH), jnp.bfloat16)
-
-    def prepare(i):
-        for n in range(slots):
-            scale_buf[i % 2, :, n * TILE : (n + 1) * TILE] = (
-                q_scale[:, i : i + 1] * key_buf[i * slots + n : i * slots + n + 1, :]
-            )
 
     def weights(i, h):
         score_ref, at = (first_ref, h) if h < done else (second_ref, h - done)
         rows = pl.ds(i * TILE, TILE)
-        if h == 0:
-            prepare(i)
-        parts = []
-        for b in range(0, TILE, block):
-            score = [
-                score_ref[at, pl.ds(i * TILE + b, block), tile_rows(slot[i][n])]
-                * scale_buf[i % 2, b : b + block, n * TILE : (n + 1) * TILE]
-                for n in range(slots)
-            ]
-            top = jnp.max(functools.reduce(jnp.maximum, score), axis=1, keepdims=True)
-            parts.append(jnp.concatenate([jnp.exp2(x - top).astype(jnp.bfloat16) for x in score], axis=1))
-        return jnp.concatenate(parts, axis=0)
+        score = [score_ref[at, rows, tile_rows(slot[i][n])] for n in range(slots)]
+        top = jnp.max(functools.reduce(jnp.maximum, score), axis=1, keepdims=True)
+        return jnp.concatenate([jnp.exp2(x - top).astype(jnp.bfloat16) for x in score], axis=1)
 
     def mix(i, h, weight):
         cols = slice(h * DH, (h + 1) * DH)
@@ -298,22 +291,34 @@
     )(half, received)
     borders = [lax.ppermute(border, "seq", hop) for hop in hops]
 
+    def scaled(first_tile, borders, first, second):
+        at = 1 + len(borders)
+        return pl.pallas_call(
+            functools.partial(scale_kernel, width * groups, first_tile),
+            out_shape=[pltpu.VMEM(first.shape, f32), pltpu.VMEM(second.shape, f32)],
+            in_specs=[VMEM] * (at + 2),
+            out_specs=[VMEM] * 2,
+            input_output_aliases={at: 0, at + 1: 1},
+            compiler_params=small,
+            cost_estimate=pl.CostEstimate(flops=rows * rows * heads, bytes_accessed=0, transcendentals=0),
+            name="scale",
+        )(total, *borders, first, second)
+
+    first, second = scaled(0, [], first, second)
+    borders, first, second = lax.optimization_barrier((borders, first, second))
+    first, second = scaled(tiles, borders, first, second)
+
     pairs = tiles * slots * TILE * TILE * heads
     mixed = pl.pallas_call(
-        functools.partial(attention_kernel, width * groups, 128),
+        functools.partial(attention_kernel, tiles),
         out_shape=jax.ShapeDtypeStruct((rows, width), bf16),
-        in_specs=[VMEM] * (5 + count),
+        in_specs=[VMEM] * 4,
         out_specs=HBM,
-        scratch_shapes=[
-            pltpu.VMEM((rows, width), bf16),
-            pltpu.VMEM((2, TILE, slots * TILE), f32),
-            pltpu.VMEM((tiles * slots, TILE), f32),
-            pltpu.SemaphoreType.DMA((tiles,)),
-        ],
+        scratch_shapes=[pltpu.VMEM((rows, width), bf16), pltpu.SemaphoreType.DMA((tiles,))],
         compiler_params=pltpu.CompilerParams(vmem_limit_bytes=24 * MIB),
         cost_estimate=pl.CostEstimate(flops=2 * pairs * DH, bytes_accessed=2 * rows * width, transcendentals=pairs),
         name="attention",
-    )(total, slot, first, second, v_all, *borders)
+    )(slot, first, second, v_all)
     return mixed.reshape(1, rows, width)
 
 

time: 17.2 us -> 17.1 us (level)
  waiting for transfers between devices: 1.26 us -> 0.24 us
  Pallas kernels: 9.04 us -> 9.97 us
    ppermute x1, waiting for transfers between devices: 1.14 us -> 0.11 us  [shards(): borders = [lax.ppermute(border, 'seq', hop) for hop in hops]]
    pallas_call x1 -> x3, Pallas kernels: 4.26 us -> 5.19 us  [the longest x1 3.83 us: shards(): pl.pallas_call(functools.partial(attention_kernel, tiles), out_shape=jax....]
  transfers between devices with their start and end apart: 4 -> 4, of which waited for: 2 -> 2; matrix products, arithmetic and copies ran while one was open for 0% -> 0% of each run, Pallas kernels for 16% -> 22%
where the time goes in v6:
time: 17.1 us; the launch traced here: 17 us
  Pallas kernels  9.97 us (58%)
  starting transfers between devices  6.03 us (35%)
  between operations  0.71 us (4%)
  waiting for transfers between devices  0.24 us (1%)
    pallas_call x1, Pallas kernels, shards(): pl.pallas_call(functools.partial(attention_kernel, tiles), out_shape=jax....  3.83 us
    ppermute x1, starting transfers between devices, shards(): received = lax.ppermute(half, 'mp', [(i, i ^ 2) for i in range(groups)])  2.86 us
    ppermute x1, starting transfers between devices, shards(): received = lax.ppermute(sums, 'mp', [(i, i ^ 1) for i in range(groups)])  2.65 us
    pallas_call x1, Pallas kernels, shards(): pl.pallas_call(functools.partial(sums_kernel, chunk), out_shape=[pltpu.VM...  2.01 us
    pallas_call x1, Pallas kernels, shards(): pl.pallas_call(second_kernel, out_shape=[pltpu.VMEM((early, rows, key_row...  1.62 us
    pallas_call x2, Pallas kernels, scaled(): pl.pallas_call(functools.partial(scale_kernel, width * groups, first_tile...  1.36 us
    pallas_call x1, Pallas kernels, shards(): pl.pallas_call(first_kernel, out_shape=pltpu.VMEM((early, rows, key_rows)...  1.13 us
    ppermute x1, starting transfers between devices, shards(): edges = [lax.ppermute(edge, 'seq', hop) for edge, hop in zip(edges, hops)]  0.52 us
  transfers between devices with their start and end apart: 4, of which 2 were waited for; matrix products, arithmetic and copies ran while one was open for 0% of the time, Pallas kernels for 22%

profile of v6, /device:TPU:0, one launch (start us, length us, event | category | flops | bytes accessed | tf_op | source)
XLA Modules:
  0.0 17.0 jit_solution(14751452062600138245)
XLA Ops:
  0.0 2.0 %sums.1 = (f32[12,128]{1,0:T(8,128)S(1)}, f32[2,640]{1,0:T(2,128)S(1)}, s32[30,128]{1,0:T(8,128)S(1)}, bf16[768,640]{1,0:T(8,128)(2,1)S(1)}, bf16[768,640]{1,0:T...) custom-call(s32[5,1,6]{2,1,0:T(1,128)} %bitcast.12, f32[2,640]{1,0:T(2,128)} %gq_hbm.1, f32[2,640]{1,0:T(2,128)} %gk_hbm.1, ...), custom_call_target="tpu_custom_call" | custom-call | flops 1966080 | bytes 1966080 | tf_op jit(solution)/shard_map/sums/pallas_call | solution.py:223
  2.0 0.0 copy-start
  2.0 0.5 %collective-permute-start.2 = (bf16[2,128,640]{2,1,0:T(8,128)(2,1)S(1)}, bf16[2,128,640]{2,1,0:T(8,128)(2,1)S(1)}, u32[]{:S(2)}, u32[]{:S(2)}) collective-permute-start(bf16[2,128,640]{2,1,0:T(8,128)(2,1)S(1)} %get-tuple-element.35), channel_id=1, source_target_pairs={{0,4},{4,0},{1,5},{5,1},{2,6},{6,2},{3,7},{7,3},{8,12},{12,8},{9,1... | collective-permute-start | bytes 983048 | tf_op jit(solution)/shard_map/ppermute | solution.py:254
  2.6 2.6 %collective-permute-start = (f32[12,128]{1,0:T(8,128)S(1)}, f32[12,128]{1,0:T(8,128)S(1)}, u32[]{:S(2)}, u32[]{:S(2)}) collective-permute-start(f32[12,128]{1,0:T(8,128)S(1)} %get-tuple-element.30.a_ref), channel_id=1, source_target_pairs={{0,1},{1,0},{2,3},{3,2},{4,5},{5,4},{6,7},{7,6},{8,9},{9,8},{10,11... | collective-permute-start | bytes 18440 | tf_op jit(solution)/shard_map/ppermute | solution.py:253
  5.9 1.1 %first.1.rest_1_ = f32[3,768,896]{2,1,0:T(8,128)S(1)} custom-call(s32[1,1]{1,0:T(1,128)} %bitcast.6.step_ref, f32[2,640]{1,0:T(2,128)S(1)} %get-tuple-element.31.gain_ref, bf16[768,640]{1,0:T(8,128)(2,1)S(1)} %get-tuple-element.32.q_ref, bf16[768,640]{1,0:T(8,128)(2,1)S(1)} %get-tuple-element.33.k_ref), custom_call_target="tpu_custom_call" | custom-call | flops 452984832 | tf_op jit(solution)/shard_map/first/pallas_call | solution.py:259
  7.0 0.0 collective-permute-done.b_ref
  7.0 2.9 %collective-permute-start.1 = (f32[12,128]{1,0:T(8,128)S(1)}, f32[12,128]{1,0:T(8,128)S(1)}, u32[]{:S(2)}, u32[]{:S(2)}) collective-permute-start(f32[12,128]{1,0:T(8,128)S(1)} %add.1.half_ref.a_ref), channel_id=1, source_target_pairs={{0,2},{1,3},{2,0},{3,1},{4,6},{5,7},{6,4},{7,5},{8,10},{9,11},{10,... | collective-permute-start | bytes 18440 | tf_op jit(solution)/shard_map/ppermute | solution.py:270
  9.9 0.0 collective-permute-done.2.rest_0_
  9.9 0.0 copy-done
  9.9 1.6 %second.1 = (f32[3,768,896]{2,1,0:T(8,128)S(1)}, f32[2,768,896]{2,1,0:T(8,128)S(1)}, bf16[896,640]{1,0:T(8,128)(2,1)S(1)}) custom-call(f32[12,128]{1,0:T(8,128)S(1)} %add.1.half_ref.a_ref, s32[1,1]{1,0:T(1,128)} %bitcast.7.step_ref, f32[2,640]{1,0:T(2,128)S(1)} %get-tuple-element.31.gain_ref, ...), custom_call_target="tpu_custom_call", output_to_operand_aliasing={{0}: (7, {})} | custom-call | flops 452984832 | tf_op jit(solution)/shard_map/second/pallas_call | solution.py:271
  11.5 0.1 collective-permute-done.1.b_ref
  11.6 0.0 collective-permute-start.3
  11.6 1.0 %scale.2 = (f32[3,768,896]{2,1,0:T(8,128)S(1)}, f32[2,768,896]{2,1,0:T(8,128)S(1)}) custom-call(f32[12,128]{1,0:T(8,128)S(1)} %get-tuple-element.41.sums_ref, f32[3,768,896]{2,1,0:T(8,128)S(1)} %get-tuple-element.43.rest_0_, f32[2,768,896]{2,1,0:T(8,128)S(1)} %get-tuple-element.44.rest_1_), custom_call_target="tpu_custom_call", output_to_operand_aliasing={{0}: (1, {}), {1}: (2, {})} | custom-call | flops 2949120 | tf_op jit(solution)/shard_map/scale/pallas_call | solution.py:296
  12.7 0.1 collective-permute-done.3.rest_0_
  12.8 0.3 %scale.3 = (f32[3,768,896]{2,1,0:T(8,128)S(1)}, f32[2,768,896]{2,1,0:T(8,128)S(1)}) custom-call(f32[12,128]{1,0:T(8,128)S(1)} %get-tuple-element.41.sums_ref, f32[2,128]{1,0:T(2,128)S(1)} %collective-permute-done.3.rest_0_, f32[3,768,896]{2,1,0:T(8,128)S(1)} %get-tuple-element.48.rest_1_, ...), custom_call_target="tpu_custom_call", output_to_operand_aliasing={{0}: (2, {}), {1}: (3, {})} | custom-call | flops 2949120 | tf_op jit(solution)/shard_map/scale/pallas_call | solution.py:296
  13.1 3.8 %attention.1 = bf16[768,640]{1,0:T(8,128)(2,1)} custom-call(s32[30,128]{1,0:T(8,128)S(1)} %get-tuple-element.29.slot_ref, f32[3,768,896]{2,1,0:T(8,128)S(1)} %get-tuple-element.50.first_ref, f32[2,768,896]{2,1,0:T(8,128)S(1)} %get-tuple-element.51.second_ref, bf16[896,640]{1,0:T(8,128)(2,1)S(1)} %get-tuple-element.52.v_ref), custom_call_target="tpu_custom_call" | custom-call | flops 629145600 | bytes 983040 | tf_op jit(solution)/shard_map/attention/pallas_call | solution.py:312
  (2 shorter events, 0.0 us)
Async XLA Ops:
  2.0 7.9 %copy-start = (bf16[1,768,640]{2,1,0:T(8,128)(2,1)S(1)}, bf16[1,768,640]{2,1,0:T(8,128)(2,1)}, u32[]{:S(2)}) copy-start(bf16[1,768,640]{2,1,0:T(8,128)(2,1)} %param.9) | copy-start | bytes 2949124
  2.0 7.8 %collective-permute-start.2 = (bf16[2,128,640]{2,1,0:T(8,128)(2,1)S(1)}, bf16[2,128,640]{2,1,0:T(8,128)(2,1)S(1)}, u32[]{:S(2)}, u32[]{:S(2)}) collective-permute-start(bf16[2,128,640]{2,1,0:T(8,128)(2,1)S(1)} %get-tuple-element.35), channel_id=1, source_target_pairs={{0,4},{4,0},{1,5},{5,1},{2,6},{6,2},{3,7},{7,3},{8,12},{12,8},{9,1... | collective-permute-start | bytes 983048 | tf_op jit(solution)/shard_map/ppermute | solution.py:254
  2.6 4.4 %collective-permute-start = (f32[12,128]{1,0:T(8,128)S(1)}, f32[12,128]{1,0:T(8,128)S(1)}, u32[]{:S(2)}, u32[]{:S(2)}) collective-permute-start(f32[12,128]{1,0:T(8,128)S(1)} %get-tuple-element.30.a_ref), channel_id=1, source_target_pairs={{0,1},{1,0},{2,3},{3,2},{4,5},{5,4},{6,7},{7,6},{8,9},{9,8},{10,11... | collective-permute-start | bytes 18440 | tf_op jit(solution)/shard_map/ppermute | solution.py:253
  7.0 4.6 %collective-permute-start.1 = (f32[12,128]{1,0:T(8,128)S(1)}, f32[12,128]{1,0:T(8,128)S(1)}, u32[]{:S(2)}, u32[]{:S(2)}) collective-permute-start(f32[12,128]{1,0:T(8,128)S(1)} %add.1.half_ref.a_ref), channel_id=1, source_target_pairs={{0,2},{1,3},{2,0},{3,1},{4,6},{5,7},{6,4},{7,5},{8,10},{9,11},{10,... | collective-permute-start | bytes 18440 | tf_op jit(solution)/shard_map/ppermute | solution.py:270
  11.6 1.1 %collective-permute-start.3 = (f32[2,128]{1,0:T(2,128)S(1)}, f32[2,128]{1,0:T(2,128)S(1)}, u32[]{:S(2)}, u32[]{:S(2)}) collective-permute-start(f32[2,128]{1,0:T(2,128)S(1)} %get-tuple-element.42), channel_id=1, source_target_pairs={{0,4},{4,0},{1,5},{5,1},{2,6},{6,2},{3,7},{7,3},{8,12},{12,8},{9,1... | collective-permute-start | bytes 3080 | tf_op jit(solution)/shard_map/ppermute | solution.py:292

commit v7 on v6

--- a/solution.py
+++ b/solution.py
@@ -72,7 +72,7 @@
                 for n in range(slots):
                     local = near[n, 0, i] - place * tiles
                     local = jnp.where(local < 0, tiles + len(edges) - 1, jnp.minimum(local, tiles))
-                    slot_ref[i * slots + n : i * slots + n + 1, :] = jnp.full((1, TILE), local, jnp.int32)
+                    slot_ref[i * slots + n] = local
     for copy in edge_copies:
         copy.wait()
 
@@ -168,7 +168,7 @@
     slots = slot_ref.shape[0] // tiles
     done = first_ref.shape[0]
     heads = done + second_ref.shape[0]
-    slot = [[jnp.max(slot_ref[i * slots + n : i * slots + n + 1, :]) for n in range(slots)] for i in range(tiles)]
+    slot = [[slot_ref[i * slots + n] for n in range(slots)] for i in range(tiles)]
     ones = jnp.ones((TILE, DH), jnp.bfloat16)
 
     def weights(i, h):
@@ -225,13 +225,13 @@
         out_shape=[
             pltpu.VMEM((2 * tiles, TILE), f32),
             pltpu.VMEM((2, width), f32),
-            pltpu.VMEM((tiles * slots, TILE), jnp.int32),
+            pltpu.SMEM((tiles * slots,), jnp.int32),
             pltpu.VMEM((rows, width), bf16),
             pltpu.VMEM((rows, width), bf16),
         ]
         + [pltpu.VMEM((2, TILE, width), bf16)] * count,
         in_specs=[HBM] * 6,
-        out_specs=[VMEM] * (5 + count),
+        out_specs=[VMEM, VMEM, SMEM] + [VMEM] * (2 + count),
         scratch_shapes=[
             pltpu.SMEM((slots, 1, tiles), jnp.int32),
             pltpu.VMEM((2, width), f32),
@@ -312,7 +312,7 @@
     mixed = pl.pallas_call(
         functools.partial(attention_kernel, tiles),
         out_shape=jax.ShapeDtypeStruct((rows, width), bf16),
-        in_specs=[VMEM] * 4,
+        in_specs=[SMEM] + [VMEM] * 3,
         out_specs=HBM,
         scratch_shapes=[pltpu.VMEM((rows, width), bf16), pltpu.SemaphoreType.DMA((tiles,))],
         compiler_params=pltpu.CompilerParams(vmem_limit_bytes=24 * MIB),

time: 17.1 us -> 16.5 us (0.965)
  Pallas kernels: 9.97 us -> 9.27 us
    pallas_call x1, Pallas kernels: 3.83 us -> 3.17 us  [shards(): pl.pallas_call(functools.partial(attention_kernel, tiles), out_shape=jax....]
  transfers between devices with their start and end apart: 4 -> 4, of which waited for: 2 -> 2; matrix products, arithmetic and copies ran while one was open for 0% -> 0% of each run, Pallas kernels for 22% -> 23%
where the time goes in v7:
time: 16.5 us; the launch traced here: 16.3 us
  Pallas kernels  9.27 us (56%)
  starting transfers between devices  6.03 us (37%)
  between operations  0.71 us (4%)
  waiting for transfers between devices  0.28 us (2%)
    pallas_call x1, Pallas kernels, shards(): pl.pallas_call(functools.partial(attention_kernel, tiles), out_shape=jax....  3.17 us
    ppermute x1, starting transfers between devices, shards(): received = lax.ppermute(half, 'mp', [(i, i ^ 2) for i in range(groups)])  2.86 us
    ppermute x1, starting transfers between devices, shards(): received = lax.ppermute(sums, 'mp', [(i, i ^ 1) for i in range(groups)])  2.65 us
    pallas_call x1, Pallas kernels, shards(): pl.pallas_call(functools.partial(sums_kernel, chunk), out_shape=[pltpu.VM...  2.03 us
    pallas_call x1, Pallas kernels, shards(): pl.pallas_call(second_kernel, out_shape=[pltpu.VMEM((early, rows, key_row...  1.62 us
    pallas_call x2, Pallas kernels, scaled(): pl.pallas_call(functools.partial(scale_kernel, width * groups, first_tile...  1.31 us
    pallas_call x1, Pallas kernels, shards(): pl.pallas_call(first_kernel, out_shape=pltpu.VMEM((early, rows, key_rows)...  1.13 us
    ppermute x1, starting transfers between devices, shards(): edges = [lax.ppermute(edge, 'seq', hop) for edge, hop in zip(edges, hops)]  0.52 us
  transfers between devices with their start and end apart: 4, of which 2 were waited for; matrix products, arithmetic and copies ran while one was open for 0% of the time, Pallas kernels for 23%

profile of v7, /device:TPU:0, one launch (start us, length us, event | category | flops | bytes accessed | tf_op | source)
XLA Modules:
  0.0 16.3 jit_solution(17323063168905487970)
XLA Ops:
  0.0 2.0 %sums.1 = (f32[12,128]{1,0:T(8,128)S(1)}, f32[2,640]{1,0:T(2,128)S(1)}, s32[30]{0:T(128)S(4)}, bf16[768,640]{1,0:T(8,128)(2,1)S(1)}, bf16[768,640]{1,0:T(8,128)(2,1)S(1)}, /*index=5*/bf16[2,128,640]{2,1,0:T(8,128)(2,1)S(1)}) custom-call(s32[5,1,6]{2,1,0:T(1,128)} %bitcast.12, f32[2,640]{1,0:T(2,128)} %gq_hbm.1, f32[2,640]{1,0:T(2,128)} %gk_hbm.1, ...), custom_call_target="tpu_custom_call" | custom-call | flops 1966080 | bytes 1966080 | tf_op jit(solution)/shard_map/sums/pallas_call | solution.py:223
  2.0 0.0 copy-start
  2.0 0.5 %collective-permute-start.2 = (bf16[2,128,640]{2,1,0:T(8,128)(2,1)S(1)}, bf16[2,128,640]{2,1,0:T(8,128)(2,1)S(1)}, u32[]{:S(2)}, u32[]{:S(2)}) collective-permute-start(bf16[2,128,640]{2,1,0:T(8,128)(2,1)S(1)} %get-tuple-element.35), channel_id=1, source_target_pairs={{0,4},{4,0},{1,5},{5,1},{2,6},{6,2},{3,7},{7,3},{8,12},{12,8},{9,1... | collective-permute-start | bytes 983048 | tf_op jit(solution)/shard_map/ppermute | solution.py:254
  2.6 2.6 %collective-permute-start = (f32[12,128]{1,0:T(8,128)S(1)}, f32[12,128]{1,0:T(8,128)S(1)}, u32[]{:S(2)}, u32[]{:S(2)}) collective-permute-start(f32[12,128]{1,0:T(8,128)S(1)} %get-tuple-element.30.a_ref), channel_id=1, source_target_pairs={{0,1},{1,0},{2,3},{3,2},{4,5},{5,4},{6,7},{7,6},{8,9},{9,8},{10,11... | collective-permute-start | bytes 18440 | tf_op jit(solution)/shard_map/ppermute | solution.py:253
  5.9 1.1 %first.1.rest_1_ = f32[3,768,896]{2,1,0:T(8,128)S(1)} custom-call(s32[1,1]{1,0:T(1,128)} %bitcast.6.step_ref, f32[2,640]{1,0:T(2,128)S(1)} %get-tuple-element.31.gain_ref, bf16[768,640]{1,0:T(8,128)(2,1)S(1)} %get-tuple-element.32.q_ref, bf16[768,640]{1,0:T(8,128)(2,1)S(1)} %get-tuple-element.33.k_ref), custom_call_target="tpu_custom_call" | custom-call | flops 452984832 | tf_op jit(solution)/shard_map/first/pallas_call | solution.py:259
  7.0 0.0 collective-permute-done.b_ref
  7.0 2.9 %collective-permute-start.1 = (f32[12,128]{1,0:T(8,128)S(1)}, f32[12,128]{1,0:T(8,128)S(1)}, u32[]{:S(2)}, u32[]{:S(2)}) collective-permute-start(f32[12,128]{1,0:T(8,128)S(1)} %add.1.half_ref.a_ref), channel_id=1, source_target_pairs={{0,2},{1,3},{2,0},{3,1},{4,6},{5,7},{6,4},{7,5},{8,10},{9,11},{10,... | collective-permute-start | bytes 18440 | tf_op jit(solution)/shard_map/ppermute | solution.py:270
  9.9 0.0 collective-permute-done.2.rest_0_
  9.9 0.0 copy-done
  9.9 1.6 %second.1 = (f32[3,768,896]{2,1,0:T(8,128)S(1)}, f32[2,768,896]{2,1,0:T(8,128)S(1)}, bf16[896,640]{1,0:T(8,128)(2,1)S(1)}) custom-call(f32[12,128]{1,0:T(8,128)S(1)} %add.1.half_ref.a_ref, s32[1,1]{1,0:T(1,128)} %bitcast.7.step_ref, f32[2,640]{1,0:T(2,128)S(1)} %get-tuple-element.31.gain_ref, ...), custom_call_target="tpu_custom_call", output_to_operand_aliasing={{0}: (7, {})} | custom-call | flops 452984832 | tf_op jit(solution)/shard_map/second/pallas_call | solution.py:271
  11.5 0.1 collective-permute-done.1.b_ref
  11.6 0.0 collective-permute-start.3
  11.6 1.0 %scale.2 = (f32[3,768,896]{2,1,0:T(8,128)S(1)}, f32[2,768,896]{2,1,0:T(8,128)S(1)}) custom-call(f32[12,128]{1,0:T(8,128)S(1)} %get-tuple-element.41.sums_ref, f32[3,768,896]{2,1,0:T(8,128)S(1)} %get-tuple-element.43.rest_0_, f32[2,768,896]{2,1,0:T(8,128)S(1)} %get-tuple-element.44.rest_1_), custom_call_target="tpu_custom_call", output_to_operand_aliasing={{0}: (1, {}), {1}: (2, {})} | custom-call | flops 2949120 | tf_op jit(solution)/shard_map/scale/pallas_call | solution.py:296
  12.6 0.2 collective-permute-done.3.rest_0_
  12.8 0.3 %scale.3 = (f32[3,768,896]{2,1,0:T(8,128)S(1)}, f32[2,768,896]{2,1,0:T(8,128)S(1)}) custom-call(f32[12,128]{1,0:T(8,128)S(1)} %get-tuple-element.41.sums_ref, f32[2,128]{1,0:T(2,128)S(1)} %collective-permute-done.3.rest_0_, f32[3,768,896]{2,1,0:T(8,128)S(1)} %get-tuple-element.48.rest_1_, ...), custom_call_target="tpu_custom_call", output_to_operand_aliasing={{0}: (2, {}), {1}: (3, {})} | custom-call | flops 2949120 | tf_op jit(solution)/shard_map/scale/pallas_call | solution.py:296
  13.1 3.2 %attention.1 = bf16[768,640]{1,0:T(8,128)(2,1)} custom-call(s32[30]{0:T(128)S(4)} %get-tuple-element.29.slot_ref, f32[3,768,896]{2,1,0:T(8,128)S(1)} %get-tuple-element.50.first_ref, f32[2,768,896]{2,1,0:T(8,128)S(1)} %get-tuple-element.51.second_ref, bf16[896,640]{1,0:T(8,128)(2,1)S(1)} %get-tuple-element.52.v_ref), custom_call_target="tpu_custom_call" | custom-call | flops 629145600 | bytes 983040 | tf_op jit(solution)/shard_map/attention/pallas_call | solution.py:312
  (2 shorter events, 0.0 us)
Async XLA Ops:
  2.0 7.9 %copy-start = (bf16[1,768,640]{2,1,0:T(8,128)(2,1)S(1)}, bf16[1,768,640]{2,1,0:T(8,128)(2,1)}, u32[]{:S(2)}) copy-start(bf16[1,768,640]{2,1,0:T(8,128)(2,1)} %param.9) | copy-start | bytes 2949124
  2.0 7.8 %collective-permute-start.2 = (bf16[2,128,640]{2,1,0:T(8,128)(2,1)S(1)}, bf16[2,128,640]{2,1,0:T(8,128)(2,1)S(1)}, u32[]{:S(2)}, u32[]{:S(2)}) collective-permute-start(bf16[2,128,640]{2,1,0:T(8,128)(2,1)S(1)} %get-tuple-element.35), channel_id=1, source_target_pairs={{0,4},{4,0},{1,5},{5,1},{2,6},{6,2},{3,7},{7,3},{8,12},{12,8},{9,1... | collective-permute-start | bytes 983048 | tf_op jit(solution)/shard_map/ppermute | solution.py:254
  2.6 4.4 %collective-permute-start = (f32[12,128]{1,0:T(8,128)S(1)}, f32[12,128]{1,0:T(8,128)S(1)}, u32[]{:S(2)}, u32[]{:S(2)}) collective-permute-start(f32[12,128]{1,0:T(8,128)S(1)} %get-tuple-element.30.a_ref), channel_id=1, source_target_pairs={{0,1},{1,0},{2,3},{3,2},{4,5},{5,4},{6,7},{7,6},{8,9},{9,8},{10,11... | collective-permute-start | bytes 18440 | tf_op jit(solution)/shard_map/ppermute | solution.py:253
  7.0 4.6 %collective-permute-start.1 = (f32[12,128]{1,0:T(8,128)S(1)}, f32[12,128]{1,0:T(8,128)S(1)}, u32[]{:S(2)}, u32[]{:S(2)}) collective-permute-start(f32[12,128]{1,0:T(8,128)S(1)} %add.1.half_ref.a_ref), channel_id=1, source_target_pairs={{0,2},{1,3},{2,0},{3,1},{4,6},{5,7},{6,4},{7,5},{8,10},{9,11},{10,... | collective-permute-start | bytes 18440 | tf_op jit(solution)/shard_map/ppermute | solution.py:270
  11.6 1.1 %collective-permute-start.3 = (f32[2,128]{1,0:T(2,128)S(1)}, f32[2,128]{1,0:T(2,128)S(1)}, u32[]{:S(2)}, u32[]{:S(2)}) collective-permute-start(f32[2,128]{1,0:T(2,128)S(1)} %get-tuple-element.42), channel_id=1, source_target_pairs={{0,4},{4,0},{1,5},{5,1},{2,6},{6,2},{3,7},{7,3},{8,12},{12,8},{9,1... | collective-permute-start | bytes 3080 | tf_op jit(solution)/shard_map/ppermute | solution.py:292

commit v8 on v7

--- a/solution.py
+++ b/solution.py
@@ -99,9 +99,11 @@
     rows = k_ref.shape[0]
     for j in range(0, rows, 2 * TILE):
         end = min(j + 2 * TILE, rows)
-        score_ref[at, :, j:end] = lax.dot_general(
+        score = lax.dot_general(
             query, k_ref[j:end, cols], (((1,), (1,)), ((), ())), preferred_element_type=jnp.float32
         )
+        for c in range(0, end - j, TILE):
+            score_ref[at, (j + c) // TILE] = score[:, c : c + TILE]
 
 
 def first_kernel(step_ref, gain_ref, q_ref, k_ref, score_ref):
@@ -130,38 +132,43 @@
             own_scores(gain, q_ref, k_ref, score_ref, at, h)
         query = (q_ref[:, cols].astype(jnp.float32) * gain[:, cols]).astype(jnp.bfloat16)
         for e, edge in enumerate(edges):
-            out_ref[at, :, rows + e * TILE : rows + (e + 1) * TILE] = lax.dot_general(
+            out_ref[at, rows // TILE + e] = lax.dot_general(
                 query, edge[0, :, cols], (((1,), (1,)), ((), ())), preferred_element_type=jnp.float32
             )
     for copy in copies:
         copy.wait()
 
 
-def scale_kernel(full_width, first_tile, sums_ref, *rest):
+def scale_kernel(full_width, sums_ref, *rest):
     *borders, _, _, first_ref, second_ref = rest
     tiles = sums_ref.shape[0] // 2
 
     def scale(sums):
         return lax.rsqrt(sums * (1.0 / full_width) + EPSILON)
 
-    if not borders:
+    refs = (first_ref, second_ref)
+    if borders:
+        if len(borders) == 1:
+            place = lax.axis_index("seq")
+            k_scale = [scale(jnp.where(place == 0, borders[0][0:1, :], borders[0][1:2, :]))]
+        else:
+            k_scale = [scale(borders[0][0:1, :]), scale(borders[1][1:2, :])]
+        for t, row in enumerate(k_scale):
+            for ref in refs:
+                for h in range(ref.shape[0]):
+                    ref[h, tiles + t] = ref[h, tiles + t] * row
+    else:
         k_scale = [scale(sums_ref[tiles + t : tiles + t + 1, :]) for t in range(tiles)]
-    elif len(borders) == 1:
-        place = lax.axis_index("seq")
-        k_scale = [scale(jnp.where(place == 0, borders[0][0:1, :], borders[0][1:2, :]))]
-    else:
-        k_scale = [scale(borders[0][0:1, :]), scale(borders[1][1:2, :])]
-    q_scale = scale(sums_ref[0:tiles, :])
-    q_scale = jnp.concatenate([q_scale, jnp.zeros((8 - tiles % 8, TILE), jnp.float32)], axis=0).T
-    for i in range(tiles):
-        column = jnp.broadcast_to(q_scale[:, i : i + 1], (TILE, TILE))
-        rows = slice(i * TILE, (i + 1) * TILE)
-        for t, row in enumerate(k_scale):
-            both = column * row
-            cols = slice((first_tile + t) * TILE, (first_tile + t + 1) * TILE)
-            for ref in (first_ref, second_ref):
-                for h in range(ref.shape[0]):
-                    ref[h, rows, cols] = ref[h, rows, cols] * both
+        q_scale = scale(sums_ref[0:tiles, :])
+        q_scale = jnp.concatenate([q_scale, jnp.zeros((8 - tiles % 8, TILE), jnp.float32)], axis=0).T
+        for i in range(tiles):
+            column = jnp.broadcast_to(q_scale[:, i : i + 1], (TILE, TILE))
+            rows = slice(i * TILE, (i + 1) * TILE)
+            for t in range(first_ref.shape[1]):
+                both = column * k_scale[t] if t < tiles else column
+                for ref in refs:
+                    for h in range(ref.shape[0]):
+                        ref[h, t, rows, :] = ref[h, t, rows, :] * both
 
 
 def attention_kernel(tiles, slot_ref, first_ref, second_ref, v_ref, out_hbm, out_buf, sems):
@@ -174,7 +181,7 @@
     def weights(i, h):
         score_ref, at = (first_ref, h) if h < done else (second_ref, h - done)
         rows = pl.ds(i * TILE, TILE)
-        score = [score_ref[at, rows, tile_rows(slot[i][n])] for n in range(slots)]
+        score = [score_ref[at, slot[i][n], rows, :] for n in range(slots)]
         top = jnp.max(functools.reduce(jnp.maximum, score), axis=1, keepdims=True)
         return jnp.concatenate([jnp.exp2(x - top).astype(jnp.bfloat16) for x in score], axis=1)
 
@@ -218,7 +225,7 @@
     hops = [up] if devices == 2 else [down, up]
     count = len(hops)
 
-    chunk = 2 * TILE if tiles % 2 == 0 else TILE
+    chunk = rows // 2 if tiles % 2 == 0 else TILE
     bf16, f32 = jnp.bfloat16, jnp.float32
     sums, gain, slot, q_all, k_all, *edges = pl.pallas_call(
         functools.partial(sums_kernel, chunk),
@@ -258,7 +265,7 @@
     step = timestep.reshape(1, 1)
     first = pl.pallas_call(
         first_kernel,
-        out_shape=pltpu.VMEM((early, rows, key_rows), f32),
+        out_shape=pltpu.VMEM((early, key_rows // TILE, rows, TILE), f32),
         in_specs=[VMEM] * 4,
         out_specs=VMEM,
         compiler_params=pltpu.CompilerParams(vmem_limit_bytes=8 * MIB),
@@ -271,8 +278,8 @@
     first, second, v_all = pl.pallas_call(
         second_kernel,
         out_shape=[
-            pltpu.VMEM((early, rows, key_rows), f32),
-            pltpu.VMEM((heads - early, rows, key_rows), f32),
+            pltpu.VMEM((early, key_rows // TILE, rows, TILE), f32),
+            pltpu.VMEM((heads - early, key_rows // TILE, rows, TILE), f32),
             pltpu.VMEM((key_rows, width), bf16),
         ],
         in_specs=[VMEM] * 5 + [HBM] + [VMEM] * (count + 1),
@@ -291,10 +298,10 @@
     )(half, received)
     borders = [lax.ppermute(border, "seq", hop) for hop in hops]
 
-    def scaled(first_tile, borders, first, second):
+    def scaled(borders, first, second):
         at = 1 + len(borders)
         return pl.pallas_call(
-            functools.partial(scale_kernel, width * groups, first_tile),
+            functools.partial(scale_kernel, width * groups),
             out_shape=[pltpu.VMEM(first.shape, f32), pltpu.VMEM(second.shape, f32)],
             in_specs=[VMEM] * (at + 2),
             out_specs=[VMEM] * 2,
@@ -304,9 +311,9 @@
             name="scale",
         )(total, *borders, first, second)
 
-    first, second = scaled(0, [], first, second)
+    first, second = scaled([], first, second)
     borders, first, second = lax.optimization_barrier((borders, first, second))
-    first, second = scaled(tiles, borders, first, second)
+    first, second = scaled(borders, first, second)
 
     pairs = tiles * slots * TILE * TILE * heads
     mixed = pl.pallas_call(

time: 16.5 us -> 16.5 us (level)
    pallas_call x4, Pallas kernels: 4.06 us -> 4.9 us  [the longest x2 2.15 us: scaled(): pl.pallas_call(functools.partial(scale_kernel, width * groups), out_shape...]
    pallas_call x1, Pallas kernels: 3.17 us -> 2.63 us  [shards(): pl.pallas_call(functools.partial(attention_kernel, tiles), out_shape=jax....]
  transfers between devices with their start and end apart: 4 -> 4, of which waited for: 2 -> 1; matrix products, arithmetic and copies ran while one was open for 0% -> 0% of each run, Pallas kernels for 23% -> 29%
where the time goes in v8:
time: 16.5 us; the launch traced here: 16.3 us
  Pallas kernels  9.43 us (57%)
  starting transfers between devices  6.03 us (37%)
  between operations  0.72 us (4%)
    ppermute x1, starting transfers between devices, shards(): received = lax.ppermute(half, 'mp', [(i, i ^ 2) for i in range(groups)])  2.86 us
    ppermute x1, starting transfers between devices, shards(): received = lax.ppermute(sums, 'mp', [(i, i ^ 1) for i in range(groups)])  2.65 us
    pallas_call x1, Pallas kernels, shards(): pl.pallas_call(functools.partial(attention_kernel, tiles), out_shape=jax....  2.63 us
    pallas_call x2, Pallas kernels, scaled(): pl.pallas_call(functools.partial(scale_kernel, width * groups), out_shape...  2.15 us
    pallas_call x1, Pallas kernels, shards(): pl.pallas_call(functools.partial(sums_kernel, chunk), out_shape=[pltpu.VM...  1.89 us
    pallas_call x1, Pallas kernels, shards(): pl.pallas_call(second_kernel, out_shape=[pltpu.VMEM((early, key_rows // T...  1.62 us
    pallas_call x1, Pallas kernels, shards(): pl.pallas_call(first_kernel, out_shape=pltpu.VMEM((early, key_rows // TIL...  1.13 us
    ppermute x1, starting transfers between devices, shards(): edges = [lax.ppermute(edge, 'seq', hop) for edge, hop in zip(edges, hops)]  0.52 us
  transfers between devices with their start and end apart: 4, of which 1 were waited for; matrix products, arithmetic and copies ran while one was open for 0% of the time, Pallas kernels for 29%

profile of v8, /device:TPU:0, one launch (start us, length us, event | category | flops | bytes accessed | tf_op | source)
XLA Modules:
  0.0 16.3 jit_solution(62422626380058334)
XLA Ops:
  0.0 1.9 %sums.1 = (f32[12,128]{1,0:T(8,128)S(1)}, f32[2,640]{1,0:T(2,128)S(1)}, s32[30]{0:T(128)S(4)}, bf16[768,640]{1,0:T(8,128)(2,1)S(1)}, bf16[768,640]{1,0:T(8,128)(2,1)S(1)}, /*index=5*/bf16[2,128,640]{2,1,0:T(8,128)(2,1)S(1)}) custom-call(s32[5,1,6]{2,1,0:T(1,128)} %bitcast.12, f32[2,640]{1,0:T(2,128)} %gq_hbm.1, f32[2,640]{1,0:T(2,128)} %gk_hbm.1, ...), custom_call_target="tpu_custom_call" | custom-call | flops 1966080 | bytes 1966080 | tf_op jit(solution)/shard_map/sums/pallas_call | solution.py:230
  1.9 0.0 copy-start
  1.9 0.5 %collective-permute-start.2 = (bf16[2,128,640]{2,1,0:T(8,128)(2,1)S(1)}, bf16[2,128,640]{2,1,0:T(8,128)(2,1)S(1)}, u32[]{:S(2)}, u32[]{:S(2)}) collective-permute-start(bf16[2,128,640]{2,1,0:T(8,128)(2,1)S(1)} %get-tuple-element.35), channel_id=1, source_target_pairs={{0,4},{4,0},{1,5},{5,1},{2,6},{6,2},{3,7},{7,3},{8,12},{12,8},{9,1... | collective-permute-start | bytes 983048 | tf_op jit(solution)/shard_map/ppermute | solution.py:261
  2.4 2.6 %collective-permute-start = (f32[12,128]{1,0:T(8,128)S(1)}, f32[12,128]{1,0:T(8,128)S(1)}, u32[]{:S(2)}, u32[]{:S(2)}) collective-permute-start(f32[12,128]{1,0:T(8,128)S(1)} %get-tuple-element.30.a_ref), channel_id=1, source_target_pairs={{0,1},{1,0},{2,3},{3,2},{4,5},{5,4},{6,7},{7,6},{8,9},{9,8},{10,11... | collective-permute-start | bytes 18440 | tf_op jit(solution)/shard_map/ppermute | solution.py:260
  5.7 1.1 %first.1.rest_1_ = f32[3,7,768,128]{3,2,1,0:T(8,128)S(1)} custom-call(s32[1,1]{1,0:T(1,128)} %bitcast.6.step_ref, f32[2,640]{1,0:T(2,128)S(1)} %get-tuple-element.31.gain_ref, bf16[768,640]{1,0:T(8,128)(2,1)S(1)} %get-tuple-element.32.q_ref, bf16[768,640]{1,0:T(8,128)(2,1)S(1)} %get-tuple-element.33.k_ref), custom_call_target="tpu_custom_call" | custom-call | flops 452984832 | tf_op jit(solution)/shard_map/first/pallas_call | solution.py:266
  6.9 0.0 collective-permute-done.b_ref
  6.9 2.9 %collective-permute-start.1 = (f32[12,128]{1,0:T(8,128)S(1)}, f32[12,128]{1,0:T(8,128)S(1)}, u32[]{:S(2)}, u32[]{:S(2)}) collective-permute-start(f32[12,128]{1,0:T(8,128)S(1)} %add.1.half_ref.a_ref), channel_id=1, source_target_pairs={{0,2},{1,3},{2,0},{3,1},{4,6},{5,7},{6,4},{7,5},{8,10},{9,11},{10,... | collective-permute-start | bytes 18440 | tf_op jit(solution)/shard_map/ppermute | solution.py:277
  9.7 0.0 collective-permute-done.2.rest_0_
  9.8 0.0 copy-done
  9.8 1.6 %second.1 = (f32[3,7,768,128]{3,2,1,0:T(8,128)S(1)}, f32[2,7,768,128]{3,2,1,0:T(8,128)S(1)}, bf16[896,640]{1,0:T(8,128)(2,1)S(1)}) custom-call(f32[12,128]{1,0:T(8,128)S(1)} %add.1.half_ref.a_ref, s32[1,1]{1,0:T(1,128)} %bitcast.7.step_ref, f32[2,640]{1,0:T(2,128)S(1)} %get-tuple-element.31.gain_ref, ...), custom_call_target="tpu_custom_call", output_to_operand_aliasing={{0}: (7, {})} | custom-call | flops 452984832 | tf_op jit(solution)/shard_map/second/pallas_call | solution.py:278
  11.4 0.1 collective-permute-done.1.b_ref
  11.5 0.0 collective-permute-start.3
  11.5 2.0 %scale.2 = (f32[3,7,768,128]{3,2,1,0:T(8,128)S(1)}, f32[2,7,768,128]{3,2,1,0:T(8,128)S(1)}) custom-call(f32[12,128]{1,0:T(8,128)S(1)} %get-tuple-element.41.sums_ref, f32[3,7,768,128]{3,2,1,0:T(8,128)S(1)} %get-tuple-element.43.rest_0_, f32[2,7,768,128]{3,2,1,0:T(8,128)S(1)} %get-tuple-element.44.rest_1_), custom_call_target="tpu_custom_call", output_to_operand_aliasing={{0}: (1, {}), {1}: (2, {})} | custom-call | flops 2949120 | tf_op jit(solution)/shard_map/scale/pallas_call | solution.py:303
  13.5 0.0 collective-permute-done.3.rest_0_
  13.5 0.1 scale.3
  13.7 2.6 %attention.1 = bf16[768,640]{1,0:T(8,128)(2,1)} custom-call(s32[30]{0:T(128)S(4)} %get-tuple-element.29.slot_ref, f32[3,7,768,128]{3,2,1,0:T(8,128)S(1)} %get-tuple-element.50.first_ref, f32[2,7,768,128]{3,2,1,0:T(8,128)S(1)} %get-tuple-element.51.second_ref, bf16[896,640]{1,0:T(8,128)(2,1)S(1)} %get-tuple-element.52.v_ref), custom_call_target="tpu_custom_call" | custom-call | flops 629145600 | bytes 983040 | tf_op jit(solution)/shard_map/attention/pallas_call | solution.py:319
  (2 shorter events, 0.0 us)
Async XLA Ops:
  1.9 7.9 %copy-start = (bf16[1,768,640]{2,1,0:T(8,128)(2,1)S(1)}, bf16[1,768,640]{2,1,0:T(8,128)(2,1)}, u32[]{:S(2)}) copy-start(bf16[1,768,640]{2,1,0:T(8,128)(2,1)} %param.9) | copy-start | bytes 2949124
  1.9 7.8 %collective-permute-start.2 = (bf16[2,128,640]{2,1,0:T(8,128)(2,1)S(1)}, bf16[2,128,640]{2,1,0:T(8,128)(2,1)S(1)}, u32[]{:S(2)}, u32[]{:S(2)}) collective-permute-start(bf16[2,128,640]{2,1,0:T(8,128)(2,1)S(1)} %get-tuple-element.35), channel_id=1, source_target_pairs={{0,4},{4,0},{1,5},{5,1},{2,6},{6,2},{3,7},{7,3},{8,12},{12,8},{9,1... | collective-permute-start | bytes 983048 | tf_op jit(solution)/shard_map/ppermute | solution.py:261
  2.4 4.4 %collective-permute-start = (f32[12,128]{1,0:T(8,128)S(1)}, f32[12,128]{1,0:T(8,128)S(1)}, u32[]{:S(2)}, u32[]{:S(2)}) collective-permute-start(f32[12,128]{1,0:T(8,128)S(1)} %get-tuple-element.30.a_ref), channel_id=1, source_target_pairs={{0,1},{1,0},{2,3},{3,2},{4,5},{5,4},{6,7},{7,6},{8,9},{9,8},{10,11... | collective-permute-start | bytes 18440 | tf_op jit(solution)/shard_map/ppermute | solution.py:260
  6.9 4.6 %collective-permute-start.1 = (f32[12,128]{1,0:T(8,128)S(1)}, f32[12,128]{1,0:T(8,128)S(1)}, u32[]{:S(2)}, u32[]{:S(2)}) collective-permute-start(f32[12,128]{1,0:T(8,128)S(1)} %add.1.half_ref.a_ref), channel_id=1, source_target_pairs={{0,2},{1,3},{2,0},{3,1},{4,6},{5,7},{6,4},{7,5},{8,10},{9,11},{10,... | collective-permute-start | bytes 18440 | tf_op jit(solution)/shard_map/ppermute | solution.py:277
  11.5 2.0 %collective-permute-start.3 = (f32[2,128]{1,0:T(2,128)S(1)}, f32[2,128]{1,0:T(2,128)S(1)}, u32[]{:S(2)}, u32[]{:S(2)}) collective-permute-start(f32[2,128]{1,0:T(2,128)S(1)} %get-tuple-element.42), channel_id=1, source_target_pairs={{0,4},{4,0},{1,5},{5,1},{2,6},{6,2},{3,7},{7,3},{8,12},{12,8},{9,1... | collective-permute-start | bytes 3080 | tf_op jit(solution)/shard_map/ppermute | solution.py:299

commit v9 on v8

--- a/solution.py
+++ b/solution.py
@@ -140,7 +140,7 @@
 
 
 def scale_kernel(full_width, sums_ref, *rest):
-    *borders, _, _, first_ref, second_ref = rest
+    *borders, _, _, first_ref, second_ref, column_buf = rest
     tiles = sums_ref.shape[0] // 2
 
     def scale(sums):
@@ -161,14 +161,18 @@
         k_scale = [scale(sums_ref[tiles + t : tiles + t + 1, :]) for t in range(tiles)]
         q_scale = scale(sums_ref[0:tiles, :])
         q_scale = jnp.concatenate([q_scale, jnp.zeros((8 - tiles % 8, TILE), jnp.float32)], axis=0).T
+        k_scale += [jnp.ones((1, TILE), jnp.float32)] * (first_ref.shape[1] - tiles)
         for i in range(tiles):
-            column = jnp.broadcast_to(q_scale[:, i : i + 1], (TILE, TILE))
-            rows = slice(i * TILE, (i + 1) * TILE)
-            for t in range(first_ref.shape[1]):
-                both = column * k_scale[t] if t < tiles else column
-                for ref in refs:
-                    for h in range(ref.shape[0]):
-                        ref[h, t, rows, :] = ref[h, t, rows, :] * both
+            column_buf[i * TILE : (i + 1) * TILE, :] = jnp.broadcast_to(q_scale[:, i : i + 1], (TILE, TILE))
+        for ref in refs:
+
+            @pl.loop(0, ref.shape[0])
+            def _(h):
+                for i in range(tiles):
+                    rows = slice(i * TILE, (i + 1) * TILE)
+                    column = column_buf[rows, :]
+                    for t, row in enumerate(k_scale):
+                        ref[h, t, rows, :] = ref[h, t, rows, :] * (column * row)
 
 
 def attention_kernel(tiles, slot_ref, first_ref, second_ref, v_ref, out_hbm, out_buf, sems):
@@ -306,6 +310,7 @@
             in_specs=[VMEM] * (at + 2),
             out_specs=[VMEM] * 2,
             input_output_aliases={at: 0, at + 1: 1},
+            scratch_shapes=[pltpu.VMEM((rows, TILE), f32)],
             compiler_params=small,
             cost_estimate=pl.CostEstimate(flops=rows * rows * heads, bytes_accessed=0, transcendentals=0),
             name="scale",

time: 16.5 us -> 15.9 us (0.964)
  Pallas kernels: 9.43 us -> 8.78 us
    pallas_call x2, Pallas kernels: 2.15 us -> 1.5 us  [scaled(): pl.pallas_call(functools.partial(scale_kernel, width * groups), out_shape...]
  transfers between devices with their start and end apart: 4 -> 4, of which waited for: 1 -> 1; matrix products, arithmetic and copies ran while one was open for 0% -> 0% of each run, Pallas kernels for 29% -> 26%
where the time goes in v9:
time: 15.9 us; the launch traced here: 15.7 us
  Pallas kernels  8.78 us (55%)
  starting transfers between devices  6.03 us (38%)
  between operations  0.72 us (5%)
    ppermute x1, starting transfers between devices, shards(): received = lax.ppermute(half, 'mp', [(i, i ^ 2) for i in range(groups)])  2.86 us
    ppermute x1, starting transfers between devices, shards(): received = lax.ppermute(sums, 'mp', [(i, i ^ 1) for i in range(groups)])  2.65 us
    pallas_call x1, Pallas kernels, shards(): pl.pallas_call(functools.partial(attention_kernel, tiles), out_shape=jax....  2.63 us
    pallas_call x1, Pallas kernels, shards(): pl.pallas_call(functools.partial(sums_kernel, chunk), out_shape=[pltpu.VM...  1.89 us
    pallas_call x1, Pallas kernels, shards(): pl.pallas_call(second_kernel, out_shape=[pltpu.VMEM((early, key_rows // T...  1.62 us
    pallas_call x2, Pallas kernels, scaled(): pl.pallas_call(functools.partial(scale_kernel, width * groups), out_shape...  1.5 us
    pallas_call x1, Pallas kernels, shards(): pl.pallas_call(first_kernel, out_shape=pltpu.VMEM((early, key_rows // TIL...  1.13 us
    ppermute x1, starting transfers between devices, shards(): edges = [lax.ppermute(edge, 'seq', hop) for edge, hop in zip(edges, hops)]  0.52 us
  transfers between devices with their start and end apart: 4, of which 1 were waited for; matrix products, arithmetic and copies ran while one was open for 0% of the time, Pallas kernels for 26%

profile of v9, /device:TPU:0, one launch (start us, length us, event | category | flops | bytes accessed | tf_op | source)
XLA Modules:
  0.0 15.7 jit_solution(6607678815980978388)
XLA Ops:
  0.0 1.9 %sums.1 = (f32[12,128]{1,0:T(8,128)S(1)}, f32[2,640]{1,0:T(2,128)S(1)}, s32[30]{0:T(128)S(4)}, bf16[768,640]{1,0:T(8,128)(2,1)S(1)}, bf16[768,640]{1,0:T(8,128)(2,1)S(1)}, /*index=5*/bf16[2,128,640]{2,1,0:T(8,128)(2,1)S(1)}) custom-call(s32[5,1,6]{2,1,0:T(1,128)} %bitcast.12, f32[2,640]{1,0:T(2,128)} %gq_hbm.1, f32[2,640]{1,0:T(2,128)} %gk_hbm.1, ...), custom_call_target="tpu_custom_call" | custom-call | flops 1966080 | bytes 1966080 | tf_op jit(solution)/shard_map/sums/pallas_call | solution.py:234
  1.9 0.0 copy-start
  1.9 0.5 %collective-permute-start.2 = (bf16[2,128,640]{2,1,0:T(8,128)(2,1)S(1)}, bf16[2,128,640]{2,1,0:T(8,128)(2,1)S(1)}, u32[]{:S(2)}, u32[]{:S(2)}) collective-permute-start(bf16[2,128,640]{2,1,0:T(8,128)(2,1)S(1)} %get-tuple-element.35), channel_id=1, source_target_pairs={{0,4},{4,0},{1,5},{5,1},{2,6},{6,2},{3,7},{7,3},{8,12},{12,8},{9,1... | collective-permute-start | bytes 983048 | tf_op jit(solution)/shard_map/ppermute | solution.py:265
  2.4 2.6 %collective-permute-start = (f32[12,128]{1,0:T(8,128)S(1)}, f32[12,128]{1,0:T(8,128)S(1)}, u32[]{:S(2)}, u32[]{:S(2)}) collective-permute-start(f32[12,128]{1,0:T(8,128)S(1)} %get-tuple-element.30.a_ref), channel_id=1, source_target_pairs={{0,1},{1,0},{2,3},{3,2},{4,5},{5,4},{6,7},{7,6},{8,9},{9,8},{10,11... | collective-permute-start | bytes 18440 | tf_op jit(solution)/shard_map/ppermute | solution.py:264
  5.7 1.1 %first.1.rest_1_ = f32[3,7,768,128]{3,2,1,0:T(8,128)S(1)} custom-call(s32[1,1]{1,0:T(1,128)} %bitcast.6.step_ref, f32[2,640]{1,0:T(2,128)S(1)} %get-tuple-element.31.gain_ref, bf16[768,640]{1,0:T(8,128)(2,1)S(1)} %get-tuple-element.32.q_ref, bf16[768,640]{1,0:T(8,128)(2,1)S(1)} %get-tuple-element.33.k_ref), custom_call_target="tpu_custom_call" | custom-call | flops 452984832 | tf_op jit(solution)/shard_map/first/pallas_call | solution.py:270
  6.9 0.0 collective-permute-done.b_ref
  6.9 2.9 %collective-permute-start.1 = (f32[12,128]{1,0:T(8,128)S(1)}, f32[12,128]{1,0:T(8,128)S(1)}, u32[]{:S(2)}, u32[]{:S(2)}) collective-permute-start(f32[12,128]{1,0:T(8,128)S(1)} %add.1.half_ref.a_ref), channel_id=1, source_target_pairs={{0,2},{1,3},{2,0},{3,1},{4,6},{5,7},{6,4},{7,5},{8,10},{9,11},{10,... | collective-permute-start | bytes 18440 | tf_op jit(solution)/shard_map/ppermute | solution.py:281
  9.7 0.0 collective-permute-done.2.rest_0_
  9.8 0.0 copy-done
  9.8 1.6 %second.1 = (f32[3,7,768,128]{3,2,1,0:T(8,128)S(1)}, f32[2,7,768,128]{3,2,1,0:T(8,128)S(1)}, bf16[896,640]{1,0:T(8,128)(2,1)S(1)}) custom-call(f32[12,128]{1,0:T(8,128)S(1)} %add.1.half_ref.a_ref, s32[1,1]{1,0:T(1,128)} %bitcast.7.step_ref, f32[2,640]{1,0:T(2,128)S(1)} %get-tuple-element.31.gain_ref, ...), custom_call_target="tpu_custom_call", output_to_operand_aliasing={{0}: (7, {})} | custom-call | flops 452984832 | tf_op jit(solution)/shard_map/second/pallas_call | solution.py:282
  11.4 0.1 collective-permute-done.1.b_ref
  11.5 0.0 collective-permute-start.3
  11.5 1.3 %scale.2 = (f32[3,7,768,128]{3,2,1,0:T(8,128)S(1)}, f32[2,7,768,128]{3,2,1,0:T(8,128)S(1)}) custom-call(f32[12,128]{1,0:T(8,128)S(1)} %get-tuple-element.41.sums_ref, f32[3,7,768,128]{3,2,1,0:T(8,128)S(1)} %get-tuple-element.43.rest_0_, f32[2,7,768,128]{3,2,1,0:T(8,128)S(1)} %get-tuple-element.44.rest_1_), custom_call_target="tpu_custom_call", output_to_operand_aliasing={{0}: (1, {}), {1}: (2, {})} | custom-call | flops 2949120 | tf_op jit(solution)/shard_map/scale/pallas_call | solution.py:307
  12.9 0.0 collective-permute-done.3.rest_0_
  12.9 0.1 scale.3
  13.0 2.6 %attention.1 = bf16[768,640]{1,0:T(8,128)(2,1)} custom-call(s32[30]{0:T(128)S(4)} %get-tuple-element.29.slot_ref, f32[3,7,768,128]{3,2,1,0:T(8,128)S(1)} %get-tuple-element.50.first_ref, f32[2,7,768,128]{3,2,1,0:T(8,128)S(1)} %get-tuple-element.51.second_ref, bf16[896,640]{1,0:T(8,128)(2,1)S(1)} %get-tuple-element.52.v_ref), custom_call_target="tpu_custom_call" | custom-call | flops 629145600 | bytes 983040 | tf_op jit(solution)/shard_map/attention/pallas_call | solution.py:324
  (2 shorter events, 0.0 us)
Async XLA Ops:
  1.9 7.9 %copy-start = (bf16[1,768,640]{2,1,0:T(8,128)(2,1)S(1)}, bf16[1,768,640]{2,1,0:T(8,128)(2,1)}, u32[]{:S(2)}) copy-start(bf16[1,768,640]{2,1,0:T(8,128)(2,1)} %param.9) | copy-start | bytes 2949124
  1.9 7.8 %collective-permute-start.2 = (bf16[2,128,640]{2,1,0:T(8,128)(2,1)S(1)}, bf16[2,128,640]{2,1,0:T(8,128)(2,1)S(1)}, u32[]{:S(2)}, u32[]{:S(2)}) collective-permute-start(bf16[2,128,640]{2,1,0:T(8,128)(2,1)S(1)} %get-tuple-element.35), channel_id=1, source_target_pairs={{0,4},{4,0},{1,5},{5,1},{2,6},{6,2},{3,7},{7,3},{8,12},{12,8},{9,1... | collective-permute-start | bytes 983048 | tf_op jit(solution)/shard_map/ppermute | solution.py:265
  2.4 4.4 %collective-permute-start = (f32[12,128]{1,0:T(8,128)S(1)}, f32[12,128]{1,0:T(8,128)S(1)}, u32[]{:S(2)}, u32[]{:S(2)}) collective-permute-start(f32[12,128]{1,0:T(8,128)S(1)} %get-tuple-element.30.a_ref), channel_id=1, source_target_pairs={{0,1},{1,0},{2,3},{3,2},{4,5},{5,4},{6,7},{7,6},{8,9},{9,8},{10,11... | collective-permute-start | bytes 18440 | tf_op jit(solution)/shard_map/ppermute | solution.py:264
  6.9 4.6 %collective-permute-start.1 = (f32[12,128]{1,0:T(8,128)S(1)}, f32[12,128]{1,0:T(8,128)S(1)}, u32[]{:S(2)}, u32[]{:S(2)}) collective-permute-start(f32[12,128]{1,0:T(8,128)S(1)} %add.1.half_ref.a_ref), channel_id=1, source_target_pairs={{0,2},{1,3},{2,0},{3,1},{4,6},{5,7},{6,4},{7,5},{8,10},{9,11},{10,... | collective-permute-start | bytes 18440 | tf_op jit(solution)/shard_map/ppermute | solution.py:281
  11.5 1.4 %collective-permute-start.3 = (f32[2,128]{1,0:T(2,128)S(1)}, f32[2,128]{1,0:T(2,128)S(1)}, u32[]{:S(2)}, u32[]{:S(2)}) collective-permute-start(f32[2,128]{1,0:T(2,128)S(1)} %get-tuple-element.42), channel_id=1, source_target_pairs={{0,4},{4,0},{1,5},{5,1},{2,6},{6,2},{3,7},{7,3},{8,12},{12,8},{9,1... | collective-permute-start | bytes 3080 | tf_op jit(solution)/shard_map/ppermute | solution.py:303

commit v10 on v9

--- a/solution.py
+++ b/solution.py
@@ -26,11 +26,11 @@
     return pl.ds(pl.multiple_of(index * TILE, TILE), TILE)
 
 
-def sums_kernel(chunk, near_hbm, gq_hbm, gk_hbm, q_hbm, k_hbm, v_hbm, sums_ref, gain_ref, slot_ref,
+def sums_kernel(chunk, near_hbm, gq_hbm, gk_hbm, q_hbm, k_hbm, v_hbm, sums_ref, gain_ref, near_ref,
                 q_ref, k_ref, *rest):
-    *edges, near, gq, gk, sems, edge_sems, small_sems = rest
+    *edges, gq, gk, sems, edge_sems, small_sems = rest
     rows, width = q_hbm.shape
-    tiles, slots = rows // TILE, near_hbm.shape[0]
+    tiles = rows // TILE
     place = lax.axis_index("seq")
     copies = []
     for a, (src, dst) in enumerate(((q_hbm, q_ref), (k_hbm, k_ref))):
@@ -40,7 +40,7 @@
             copies[-1].start()
     small = [
         pltpu.make_async_copy(src, dst, small_sems.at[a])
-        for a, (src, dst) in enumerate(((near_hbm, near), (gq_hbm, gq), (gk_hbm, gk)))
+        for a, (src, dst) in enumerate(((near_hbm, near_ref), (gq_hbm, gq), (gk_hbm, gk)))
     ]
     for copy in small:
         copy.start()
@@ -68,11 +68,6 @@
             for copy in small:
                 copy.wait()
             gain_ref[...] = gq[...] * gk[...] * (DH ** -0.5 * LOG2E)
-            for i in range(tiles):
-                for n in range(slots):
-                    local = near[n, 0, i] - place * tiles
-                    local = jnp.where(local < 0, tiles + len(edges) - 1, jnp.minimum(local, tiles))
-                    slot_ref[i * slots + n] = local
     for copy in edge_copies:
         copy.wait()
 
@@ -175,11 +170,17 @@
                         ref[h, t, rows, :] = ref[h, t, rows, :] * (column * row)
 
 
-def attention_kernel(tiles, slot_ref, first_ref, second_ref, v_ref, out_hbm, out_buf, sems):
-    slots = slot_ref.shape[0] // tiles
+def attention_kernel(count, near_ref, first_ref, second_ref, v_ref, out_hbm, out_buf, sems):
+    slots, _, tiles = near_ref.shape
+    place = lax.axis_index("seq")
     done = first_ref.shape[0]
     heads = done + second_ref.shape[0]
-    slot = [[slot_ref[i * slots + n] for n in range(slots)] for i in range(tiles)]
+
+    def where_at(i, n):
+        local = near_ref[n, 0, i] - place * tiles
+        return jnp.where(local < 0, tiles + count - 1, jnp.minimum(local, tiles))
+
+    slot = [[where_at(i, n) for n in range(slots)] for i in range(tiles)]
     ones = jnp.ones((TILE, DH), jnp.bfloat16)
 
     def weights(i, h):
@@ -236,7 +237,7 @@
         out_shape=[
             pltpu.VMEM((2 * tiles, TILE), f32),
             pltpu.VMEM((2, width), f32),
-            pltpu.SMEM((tiles * slots,), jnp.int32),
+            pltpu.SMEM((slots, 1, tiles), jnp.int32),
             pltpu.VMEM((rows, width), bf16),
             pltpu.VMEM((rows, width), bf16),
         ]
@@ -244,7 +245,6 @@
         in_specs=[HBM] * 6,
         out_specs=[VMEM, VMEM, SMEM] + [VMEM] * (2 + count),
         scratch_shapes=[
-            pltpu.SMEM((slots, 1, tiles), jnp.int32),
             pltpu.VMEM((2, width), f32),
             pltpu.VMEM((2, width), f32),
             pltpu.SemaphoreType.DMA((2, rows // chunk)),
@@ -322,7 +322,7 @@
 
     pairs = tiles * slots * TILE * TILE * heads
     mixed = pl.pallas_call(
-        functools.partial(attention_kernel, tiles),
+        functools.partial(attention_kernel, count),
         out_shape=jax.ShapeDtypeStruct((rows, width), bf16),
         in_specs=[SMEM] + [VMEM] * 3,
         out_specs=HBM,

time: 15.9 us -> 15.8 us (level)
  no operation moved by 1% of the time
where the time goes in v10:
time: 15.8 us; the launch traced here: 15.6 us
  Pallas kernels  8.75 us (55%)
  starting transfers between devices  6.03 us (38%)
  between operations  0.72 us (5%)
    ppermute x1, starting transfers between devices, shards(): received = lax.ppermute(half, 'mp', [(i, i ^ 2) for i in range(groups)])  2.86 us
    pallas_call x1, Pallas kernels, shards(): pl.pallas_call(functools.partial(attention_kernel, count), out_shape=jax....  2.66 us
    ppermute x1, starting transfers between devices, shards(): received = lax.ppermute(sums, 'mp', [(i, i ^ 1) for i in range(groups)])  2.65 us
    pallas_call x1, Pallas kernels, shards(): pl.pallas_call(functools.partial(sums_kernel, chunk), out_shape=[pltpu.VM...  1.83 us
    pallas_call x1, Pallas kernels, shards(): pl.pallas_call(second_kernel, out_shape=[pltpu.VMEM((early, key_rows // T...  1.62 us
    pallas_call x2, Pallas kernels, scaled(): pl.pallas_call(functools.partial(scale_kernel, width * groups), out_shape...  1.5 us
    pallas_call x1, Pallas kernels, shards(): pl.pallas_call(first_kernel, out_shape=pltpu.VMEM((early, key_rows // TIL...  1.13 us
    ppermute x1, starting transfers between devices, shards(): edges = [lax.ppermute(edge, 'seq', hop) for edge, hop in zip(edges, hops)]  0.52 us
  transfers between devices with their start and end apart: 4, of which 1 were waited for; matrix products, arithmetic and copies ran while one was open for 0% of the time, Pallas kernels for 26%

profile of v10, /device:TPU:0, one launch (start us, length us, event | category | flops | bytes accessed | tf_op | source)
XLA Modules:
  0.0 15.6 jit_solution(10761559996598391754)
XLA Ops:
  0.0 1.8 %sums.1 = (f32[12,128]{1,0:T(8,128)S(1)}, f32[2,640]{1,0:T(2,128)S(1)}, s32[5,1,6]{2,1,0:T(1,128)S(4)}, bf16[768,640]{1,0:T(8,128)(2,1)S(1)}, bf16[768,640]{1,0:...) custom-call(s32[5,1,6]{2,1,0:T(1,128)} %bitcast.12, f32[2,640]{1,0:T(2,128)} %gq_hbm.1, f32[2,640]{1,0:T(2,128)} %gk_hbm.1, ...), custom_call_target="tpu_custom_call" | custom-call | flops 1966080 | bytes 1966080 | tf_op jit(solution)/shard_map/sums/pallas_call | solution.py:235
  1.8 0.0 copy-start
  1.9 0.5 %collective-permute-start.2 = (bf16[2,128,640]{2,1,0:T(8,128)(2,1)S(1)}, bf16[2,128,640]{2,1,0:T(8,128)(2,1)S(1)}, u32[]{:S(2)}, u32[]{:S(2)}) collective-permute-start(bf16[2,128,640]{2,1,0:T(8,128)(2,1)S(1)} %get-tuple-element.35), channel_id=1, source_target_pairs={{0,4},{4,0},{1,5},{5,1},{2,6},{6,2},{3,7},{7,3},{8,12},{12,8},{9,1... | collective-permute-start | bytes 983048 | tf_op jit(solution)/shard_map/ppermute | solution.py:265
  2.4 2.6 %collective-permute-start = (f32[12,128]{1,0:T(8,128)S(1)}, f32[12,128]{1,0:T(8,128)S(1)}, u32[]{:S(2)}, u32[]{:S(2)}) collective-permute-start(f32[12,128]{1,0:T(8,128)S(1)} %get-tuple-element.30.a_ref), channel_id=1, source_target_pairs={{0,1},{1,0},{2,3},{3,2},{4,5},{5,4},{6,7},{7,6},{8,9},{9,8},{10,11... | collective-permute-start | bytes 18440 | tf_op jit(solution)/shard_map/ppermute | solution.py:264
  5.7 1.1 %first.1.rest_1_ = f32[3,7,768,128]{3,2,1,0:T(8,128)S(1)} custom-call(s32[1,1]{1,0:T(1,128)} %bitcast.6.step_ref, f32[2,640]{1,0:T(2,128)S(1)} %get-tuple-element.31.gain_ref, bf16[768,640]{1,0:T(8,128)(2,1)S(1)} %get-tuple-element.32.q_ref, bf16[768,640]{1,0:T(8,128)(2,1)S(1)} %get-tuple-element.33.k_ref), custom_call_target="tpu_custom_call" | custom-call | flops 452984832 | tf_op jit(solution)/shard_map/first/pallas_call | solution.py:270
  6.8 0.0 collective-permute-done.b_ref
  6.8 2.9 %collective-permute-start.1 = (f32[12,128]{1,0:T(8,128)S(1)}, f32[12,128]{1,0:T(8,128)S(1)}, u32[]{:S(2)}, u32[]{:S(2)}) collective-permute-start(f32[12,128]{1,0:T(8,128)S(1)} %add.1.half_ref.a_ref), channel_id=1, source_target_pairs={{0,2},{1,3},{2,0},{3,1},{4,6},{5,7},{6,4},{7,5},{8,10},{9,11},{10,... | collective-permute-start | bytes 18440 | tf_op jit(solution)/shard_map/ppermute | solution.py:281
  9.7 0.0 collective-permute-done.2.rest_0_
  9.7 0.0 copy-done
  9.7 1.6 %second.1 = (f32[3,7,768,128]{3,2,1,0:T(8,128)S(1)}, f32[2,7,768,128]{3,2,1,0:T(8,128)S(1)}, bf16[896,640]{1,0:T(8,128)(2,1)S(1)}) custom-call(f32[12,128]{1,0:T(8,128)S(1)} %add.1.half_ref.a_ref, s32[1,1]{1,0:T(1,128)} %bitcast.7.step_ref, f32[2,640]{1,0:T(2,128)S(1)} %get-tuple-element.31.gain_ref, ...), custom_call_target="tpu_custom_call", output_to_operand_aliasing={{0}: (7, {})} | custom-call | flops 452984832 | tf_op jit(solution)/shard_map/second/pallas_call | solution.py:282
  11.3 0.1 collective-permute-done.1.b_ref
  11.4 0.0 collective-permute-start.3
  11.5 1.3 %scale.2 = (f32[3,7,768,128]{3,2,1,0:T(8,128)S(1)}, f32[2,7,768,128]{3,2,1,0:T(8,128)S(1)}) custom-call(f32[12,128]{1,0:T(8,128)S(1)} %get-tuple-element.41.sums_ref, f32[3,7,768,128]{3,2,1,0:T(8,128)S(1)} %get-tuple-element.43.rest_0_, f32[2,7,768,128]{3,2,1,0:T(8,128)S(1)} %get-tuple-element.44.rest_1_), custom_call_target="tpu_custom_call", output_to_operand_aliasing={{0}: (1, {}), {1}: (2, {})} | custom-call | flops 2949120 | tf_op jit(solution)/shard_map/scale/pallas_call | solution.py:307
  12.8 0.0 collective-permute-done.3.rest_0_
  12.8 0.1 scale.3
  13.0 2.7 %attention.1 = bf16[768,640]{1,0:T(8,128)(2,1)} custom-call(s32[5,1,6]{2,1,0:T(1,128)S(4)} %get-tuple-element.29.near_ref, f32[3,7,768,128]{3,2,1,0:T(8,128)S(1)} %get-tuple-element.50.first_ref, f32[2,7,768,128]{3,2,1,0:T(8,128)S(1)} %get-tuple-element.51.second_ref, bf16[896,640]{1,0:T(8,128)(2,1)S(1)} %get-tuple-element.52.v_ref), custom_call_target="tpu_custom_call" | custom-call | flops 629145600 | bytes 983040 | tf_op jit(solution)/shard_map/attention/pallas_call | solution.py:324
  (2 shorter events, 0.0 us)
Async XLA Ops:
  1.8 7.9 %copy-start = (bf16[1,768,640]{2,1,0:T(8,128)(2,1)S(1)}, bf16[1,768,640]{2,1,0:T(8,128)(2,1)}, u32[]{:S(2)}) copy-start(bf16[1,768,640]{2,1,0:T(8,128)(2,1)} %param.9) | copy-start | bytes 2949124
  1.9 7.8 %collective-permute-start.2 = (bf16[2,128,640]{2,1,0:T(8,128)(2,1)S(1)}, bf16[2,128,640]{2,1,0:T(8,128)(2,1)S(1)}, u32[]{:S(2)}, u32[]{:S(2)}) collective-permute-start(bf16[2,128,640]{2,1,0:T(8,128)(2,1)S(1)} %get-tuple-element.35), channel_id=1, source_target_pairs={{0,4},{4,0},{1,5},{5,1},{2,6},{6,2},{3,7},{7,3},{8,12},{12,8},{9,1... | collective-permute-start | bytes 983048 | tf_op jit(solution)/shard_map/ppermute | solution.py:265
  2.4 4.4 %collective-permute-start = (f32[12,128]{1,0:T(8,128)S(1)}, f32[12,128]{1,0:T(8,128)S(1)}, u32[]{:S(2)}, u32[]{:S(2)}) collective-permute-start(f32[12,128]{1,0:T(8,128)S(1)} %get-tuple-element.30.a_ref), channel_id=1, source_target_pairs={{0,1},{1,0},{2,3},{3,2},{4,5},{5,4},{6,7},{7,6},{8,9},{9,8},{10,11... | collective-permute-start | bytes 18440 | tf_op jit(solution)/shard_map/ppermute | solution.py:264
  6.8 4.6 %collective-permute-start.1 = (f32[12,128]{1,0:T(8,128)S(1)}, f32[12,128]{1,0:T(8,128)S(1)}, u32[]{:S(2)}, u32[]{:S(2)}) collective-permute-start(f32[12,128]{1,0:T(8,128)S(1)} %add.1.half_ref.a_ref), channel_id=1, source_target_pairs={{0,2},{1,3},{2,0},{3,1},{4,6},{5,7},{6,4},{7,5},{8,10},{9,11},{10,... | collective-permute-start | bytes 18440 | tf_op jit(solution)/shard_map/ppermute | solution.py:281
  11.4 1.4 %collective-permute-start.3 = (f32[2,128]{1,0:T(2,128)S(1)}, f32[2,128]{1,0:T(2,128)S(1)}, u32[]{:S(2)}, u32[]{:S(2)}) collective-permute-start(f32[2,128]{1,0:T(2,128)S(1)} %get-tuple-element.42), channel_id=1, source_target_pairs={{0,4},{4,0},{1,5},{5,1},{2,6},{6,2},{3,7},{7,3},{8,12},{12,8},{9,1... | collective-permute-start | bytes 3080 | tf_op jit(solution)/shard_map/ppermute | solution.py:303

commit v11 on v9

--- a/solution.py
+++ b/solution.py
@@ -54,16 +54,22 @@
         jnp.int32, (TILE, TILE), 1
     )
     for a, buf in enumerate((q_ref, k_ref)):
-        for t in range(tiles):
-            if t * TILE % chunk == 0:
-                copies[a * (rows // chunk) + t * TILE // chunk].wait()
-            total = 0.0
-            for j in range(width // DH):
-                x = buf[t * TILE : (t + 1) * TILE, j * DH : (j + 1) * DH].astype(jnp.float32)
-                total = total + x * x
-            total = jnp.sum(total, axis=1, keepdims=True)
-            total = jnp.sum(jnp.where(diagonal, total, 0.0), axis=0, keepdims=True)
-            sums_ref[a * tiles + t : a * tiles + t + 1, :] = total
+        for j in range(rows // chunk):
+            copies[a * (rows // chunk) + j].wait()
+            per = chunk // TILE
+
+            @pl.loop(0, per // 3)
+            def _(b):
+                for c in range(3):
+                    t = j * per + b * 3 + c
+                    total = 0.0
+                    for p in range(width // DH):
+                        x = buf[tile_rows(t), p * DH : (p + 1) * DH].astype(jnp.float32)
+                        total = total + x * x
+                    total = jnp.sum(total, axis=1, keepdims=True)
+                    total = jnp.sum(jnp.where(diagonal, total, 0.0), axis=0, keepdims=True)
+                    sums_ref[pl.ds(a * tiles + t, 1), :] = total
+
         if a == 0:
             for copy in small:
                 copy.wait()

time: 15.9 us -> 15.9 us (level)
  no operation moved by 1% of the time
where the time goes in v11:
time: 15.9 us; the launch traced here: 15.7 us
  Pallas kernels  8.78 us (55%)
  starting transfers between devices  6.03 us (38%)
  between operations  0.72 us (5%)
    ppermute x1, starting transfers between devices, shards(): received = lax.ppermute(half, 'mp', [(i, i ^ 2) for i in range(groups)])  2.86 us
    ppermute x1, starting transfers between devices, shards(): received = lax.ppermute(sums, 'mp', [(i, i ^ 1) for i in range(groups)])  2.65 us
    pallas_call x1, Pallas kernels, shards(): pl.pallas_call(functools.partial(attention_kernel, tiles), out_shape=jax....  2.63 us
    pallas_call x1, Pallas kernels, shards(): pl.pallas_call(functools.partial(sums_kernel, chunk), out_shape=[pltpu.VM...  1.89 us
    pallas_call x1, Pallas kernels, shards(): pl.pallas_call(second_kernel, out_shape=[pltpu.VMEM((early, key_rows // T...  1.62 us
    pallas_call x2, Pallas kernels, scaled(): pl.pallas_call(functools.partial(scale_kernel, width * groups), out_shape...  1.5 us
    pallas_call x1, Pallas kernels, shards(): pl.pallas_call(first_kernel, out_shape=pltpu.VMEM((early, key_rows // TIL...  1.13 us
    ppermute x1, starting transfers between devices, shards(): edges = [lax.ppermute(edge, 'seq', hop) for edge, hop in zip(edges, hops)]  0.52 us
  transfers between devices with their start and end apart: 4, of which 1 were waited for; matrix products, arithmetic and copies ran while one was open for 0% of the time, Pallas kernels for 26%

profile of v11, /device:TPU:0, one launch (start us, length us, event | category | flops | bytes accessed | tf_op | source)
XLA Modules:
  0.0 15.7 jit_solution(6607678815980978388)
XLA Ops:
  0.0 1.9 %sums.1 = (f32[12,128]{1,0:T(8,128)S(1)}, f32[2,640]{1,0:T(2,128)S(1)}, s32[30]{0:T(128)S(4)}, bf16[768,640]{1,0:T(8,128)(2,1)S(1)}, bf16[768,640]{1,0:T(8,128)(2,1)S(1)}, /*index=5*/bf16[2,128,640]{2,1,0:T(8,128)(2,1)S(1)}) custom-call(s32[5,1,6]{2,1,0:T(1,128)} %bitcast.12, f32[2,640]{1,0:T(2,128)} %gq_hbm.1, f32[2,640]{1,0:T(2,128)} %gk_hbm.1, ...), custom_call_target="tpu_custom_call" | custom-call | flops 1966080 | bytes 1966080 | tf_op jit(solution)/shard_map/sums/pallas_call | solution.py:240
  1.9 0.0 copy-start
  1.9 0.5 %collective-permute-start.2 = (bf16[2,128,640]{2,1,0:T(8,128)(2,1)S(1)}, bf16[2,128,640]{2,1,0:T(8,128)(2,1)S(1)}, u32[]{:S(2)}, u32[]{:S(2)}) collective-permute-start(bf16[2,128,640]{2,1,0:T(8,128)(2,1)S(1)} %get-tuple-element.35), channel_id=1, source_target_pairs={{0,4},{4,0},{1,5},{5,1},{2,6},{6,2},{3,7},{7,3},{8,12},{12,8},{9,1... | collective-permute-start | bytes 983048 | tf_op jit(solution)/shard_map/ppermute | solution.py:271
  2.4 2.6 %collective-permute-start = (f32[12,128]{1,0:T(8,128)S(1)}, f32[12,128]{1,0:T(8,128)S(1)}, u32[]{:S(2)}, u32[]{:S(2)}) collective-permute-start(f32[12,128]{1,0:T(8,128)S(1)} %get-tuple-element.30.a_ref), channel_id=1, source_target_pairs={{0,1},{1,0},{2,3},{3,2},{4,5},{5,4},{6,7},{7,6},{8,9},{9,8},{10,11... | collective-permute-start | bytes 18440 | tf_op jit(solution)/shard_map/ppermute | solution.py:270
  5.7 1.1 %first.1.rest_1_ = f32[3,7,768,128]{3,2,1,0:T(8,128)S(1)} custom-call(s32[1,1]{1,0:T(1,128)} %bitcast.6.step_ref, f32[2,640]{1,0:T(2,128)S(1)} %get-tuple-element.31.gain_ref, bf16[768,640]{1,0:T(8,128)(2,1)S(1)} %get-tuple-element.32.q_ref, bf16[768,640]{1,0:T(8,128)(2,1)S(1)} %get-tuple-element.33.k_ref), custom_call_target="tpu_custom_call" | custom-call | flops 452984832 | tf_op jit(solution)/shard_map/first/pallas_call | solution.py:276
  6.9 0.0 collective-permute-done.b_ref
  6.9 2.9 %collective-permute-start.1 = (f32[12,128]{1,0:T(8,128)S(1)}, f32[12,128]{1,0:T(8,128)S(1)}, u32[]{:S(2)}, u32[]{:S(2)}) collective-permute-start(f32[12,128]{1,0:T(8,128)S(1)} %add.1.half_ref.a_ref), channel_id=1, source_target_pairs={{0,2},{1,3},{2,0},{3,1},{4,6},{5,7},{6,4},{7,5},{8,10},{9,11},{10,... | collective-permute-start | bytes 18440 | tf_op jit(solution)/shard_map/ppermute | solution.py:287
  9.7 0.0 collective-permute-done.2.rest_0_
  9.8 0.0 copy-done
  9.8 1.6 %second.1 = (f32[3,7,768,128]{3,2,1,0:T(8,128)S(1)}, f32[2,7,768,128]{3,2,1,0:T(8,128)S(1)}, bf16[896,640]{1,0:T(8,128)(2,1)S(1)}) custom-call(f32[12,128]{1,0:T(8,128)S(1)} %add.1.half_ref.a_ref, s32[1,1]{1,0:T(1,128)} %bitcast.7.step_ref, f32[2,640]{1,0:T(2,128)S(1)} %get-tuple-element.31.gain_ref, ...), custom_call_target="tpu_custom_call", output_to_operand_aliasing={{0}: (7, {})} | custom-call | flops 452984832 | tf_op jit(solution)/shard_map/second/pallas_call | solution.py:288
  11.4 0.1 collective-permute-done.1.b_ref
  11.5 0.0 collective-permute-start.3
  11.5 1.3 %scale.2 = (f32[3,7,768,128]{3,2,1,0:T(8,128)S(1)}, f32[2,7,768,128]{3,2,1,0:T(8,128)S(1)}) custom-call(f32[12,128]{1,0:T(8,128)S(1)} %get-tuple-element.41.sums_ref, f32[3,7,768,128]{3,2,1,0:T(8,128)S(1)} %get-tuple-element.43.rest_0_, f32[2,7,768,128]{3,2,1,0:T(8,128)S(1)} %get-tuple-element.44.rest_1_), custom_call_target="tpu_custom_call", output_to_operand_aliasing={{0}: (1, {}), {1}: (2, {})} | custom-call | flops 2949120 | tf_op jit(solution)/shard_map/scale/pallas_call | solution.py:313
  12.9 0.0 collective-permute-done.3.rest_0_
  12.9 0.1 scale.3
  13.0 2.6 %attention.1 = bf16[768,640]{1,0:T(8,128)(2,1)} custom-call(s32[30]{0:T(128)S(4)} %get-tuple-element.29.slot_ref, f32[3,7,768,128]{3,2,1,0:T(8,128)S(1)} %get-tuple-element.50.first_ref, f32[2,7,768,128]{3,2,1,0:T(8,128)S(1)} %get-tuple-element.51.second_ref, bf16[896,640]{1,0:T(8,128)(2,1)S(1)} %get-tuple-element.52.v_ref), custom_call_target="tpu_custom_call" | custom-call | flops 629145600 | bytes 983040 | tf_op jit(solution)/shard_map/attention/pallas_call | solution.py:330
  (2 shorter events, 0.0 us)
Async XLA Ops:
  1.9 7.9 %copy-start = (bf16[1,768,640]{2,1,0:T(8,128)(2,1)S(1)}, bf16[1,768,640]{2,1,0:T(8,128)(2,1)}, u32[]{:S(2)}) copy-start(bf16[1,768,640]{2,1,0:T(8,128)(2,1)} %param.9) | copy-start | bytes 2949124
  1.9 7.8 %collective-permute-start.2 = (bf16[2,128,640]{2,1,0:T(8,128)(2,1)S(1)}, bf16[2,128,640]{2,1,0:T(8,128)(2,1)S(1)}, u32[]{:S(2)}, u32[]{:S(2)}) collective-permute-start(bf16[2,128,640]{2,1,0:T(8,128)(2,1)S(1)} %get-tuple-element.35), channel_id=1, source_target_pairs={{0,4},{4,0},{1,5},{5,1},{2,6},{6,2},{3,7},{7,3},{8,12},{12,8},{9,1... | collective-permute-start | bytes 983048 | tf_op jit(solution)/shard_map/ppermute | solution.py:271
  2.4 4.4 %collective-permute-start = (f32[12,128]{1,0:T(8,128)S(1)}, f32[12,128]{1,0:T(8,128)S(1)}, u32[]{:S(2)}, u32[]{:S(2)}) collective-permute-start(f32[12,128]{1,0:T(8,128)S(1)} %get-tuple-element.30.a_ref), channel_id=1, source_target_pairs={{0,1},{1,0},{2,3},{3,2},{4,5},{5,4},{6,7},{7,6},{8,9},{9,8},{10,11... | collective-permute-start | bytes 18440 | tf_op jit(solution)/shard_map/ppermute | solution.py:270
  6.9 4.6 %collective-permute-start.1 = (f32[12,128]{1,0:T(8,128)S(1)}, f32[12,128]{1,0:T(8,128)S(1)}, u32[]{:S(2)}, u32[]{:S(2)}) collective-permute-start(f32[12,128]{1,0:T(8,128)S(1)} %add.1.half_ref.a_ref), channel_id=1, source_target_pairs={{0,2},{1,3},{2,0},{3,1},{4,6},{5,7},{6,4},{7,5},{8,10},{9,11},{10,... | collective-permute-start | bytes 18440 | tf_op jit(solution)/shard_map/ppermute | solution.py:287
  11.5 1.4 %collective-permute-start.3 = (f32[2,128]{1,0:T(2,128)S(1)}, f32[2,128]{1,0:T(2,128)S(1)}, u32[]{:S(2)}, u32[]{:S(2)}) collective-permute-start(f32[2,128]{1,0:T(2,128)S(1)} %get-tuple-element.42), channel_id=1, source_target_pairs={{0,4},{4,0},{1,5},{5,1},{2,6},{6,2},{3,7},{7,3},{8,12},{12,8},{9,1... | collective-permute-start | bytes 3080 | tf_op jit(solution)/shard_map/ppermute | solution.py:309
